TPU v7x, 512 devices: a whole 4x4x16 slice. The times are simulated.
512 devices in a mesh: dp: 16 (over x, y), blk: 32 (over z, core).
Axes of the slice: x: 4, y: 4, z: 16, core: 2. Of those that a mesh axis runs over, the one named last changes fastest.
Arguments:
- tokens: bfloat16 [4096, 8192], P('dp', 'blk'), may hold values from -6 to 6
- up_blocks: bfloat16 [32, 80, 128, 128], P('blk'), may hold values from -0.125 to 0.125
- block_list: int32 [32, 80, 2], P('blk'), may hold values from -1 to 63, as said below
- row_cut: int32 [32, 2], replicated, may hold values from 0 to 63, as said below
- out_grad: bfloat16 [4096, 16384], P('dp', 'blk'), may hold values from -6 to 6
Outputs:
- activated: bfloat16 [4096, 16384], P('dp', 'blk')
- in_grad: bfloat16 [4096, 8192], P('dp', 'blk')
- block_grad: float32 [32, 80, 128, 128], P('blk', 'dp')
Inputs may be any that keep to these rules, and one draw needn't show every extreme that they name: In each block_list[j] the used slots name distinct blocks with a block row below 64 and a column slot below 4; an unused slot holds -1 in both entries, anywhere in the list; every index j uses at least 48 slots and some j uses all 80. Every block row appears exactly once in row_cut.
All inputs are finite; a program needn't handle non-finite values.
Results may differ from a plain program's by a relative error of at most 0.015.
Values may be sent and summed in bfloat16 or wider, within the bound.
No kernel may reach another device: no remote copies, remote signals or barrier semaphores. Data moves between devices by JAX's collectives and lax.ppermute only.
A program may use at most 128 MiB of HBM per device.

v0:
```python
import jax
import jax.numpy as jnp
from jax import lax
from jax.sharding import PartitionSpec as P


def on_device(tokens, up_blocks, block_list, row_cut, out_grad):
    dev_count = lax.axis_size("blk")
    dp_count = lax.axis_size("dp")
    tok_rows = tokens.shape[0]
    blk_size = up_blocks.shape[-1]
    width = tokens.shape[1] * dev_count
    row_count = width // blk_size
    col_count = out_grad.shape[1] // blk_size
    weights = up_blocks[0]
    listed = block_list[0]
    block_rows = listed[:, 0]
    block_cols = listed[:, 1]
    is_used = block_rows >= 0
    used_mask = is_used.astype(jnp.float32)
    safe_rows = jnp.maximum(block_rows, 0)
    safe_cols = jnp.maximum(block_cols, 0)
    col_pick = (
        (safe_cols[:, None] == jnp.arange(col_count, dtype=jnp.int32)[None, :]) & is_used[:, None]
    ).astype(jnp.float32)
    gathered = lax.all_gather(tokens, "blk", axis=1, tiled=True)
    picked = jnp.take(gathered.reshape(tok_rows, row_count, blk_size), safe_rows, axis=1)
    per_slot = jnp.einsum("tsi,sio->sto", picked, weights, preferred_element_type=jnp.float32)
    hidden = jnp.einsum("sto,sc->tco", per_slot, col_pick, precision=lax.Precision.HIGHEST)
    gate_sig = jax.nn.sigmoid(hidden)
    activated = (hidden * gate_sig).astype(jnp.bfloat16).reshape(tok_rows, col_count * blk_size)
    upstream = out_grad.reshape(tok_rows, col_count, blk_size).astype(jnp.float32)
    pre_grad = (upstream * gate_sig * (1.0 + hidden * (1.0 - gate_sig))).astype(jnp.bfloat16)
    col_grads = jnp.take(pre_grad, safe_cols, axis=1)
    dest_rows = row_cut.reshape(-1)
    row_place = (
        jnp.zeros((row_count,), jnp.int32).at[dest_rows].set(jnp.arange(row_count, dtype=jnp.int32))
    )
    target = jnp.where(is_used, row_place[safe_rows], row_count)
    slot_terms = jnp.einsum("tso,sio->sti", col_grads, weights, preferred_element_type=jnp.float32)
    partial_value = jax.ops.segment_sum(slot_terms, target, num_segments=row_count).astype(
        jnp.bfloat16
    )
    received = lax.all_to_all(
        partial_value.reshape(dev_count, row_count // dev_count, tok_rows, blk_size),
        "blk",
        split_axis=0,
        concat_axis=0,
        tiled=True,
    )
    summed = jnp.sum(received.astype(jnp.float32), axis=0)
    in_grad = jnp.transpose(summed, (1, 0, 2)).reshape(tok_rows, -1).astype(jnp.bfloat16)
    grad_scale = 1.0 / jnp.sqrt(jnp.float32(tok_rows * dp_count))
    term = jnp.einsum("tsi,tso->sio", picked, col_grads, preferred_element_type=jnp.float32)
    own_grads = (
        lax.psum_scatter(
            (term * used_mask[:, None, None]).astype(jnp.bfloat16),
            "dp",
            scatter_dimension=0,
            tiled=True,
        ).astype(jnp.float32)
        * grad_scale
    )
    return (activated, in_grad, own_grads[None])


def solution(mesh):
    return jax.shard_map(
        on_device,
        mesh=mesh,
        in_specs=(
            P("dp", "blk"),
            P("blk", None, None, None),
            P("blk", None, None),
            P(),
            P("dp", "blk"),
        ),
        out_specs=(P("dp", "blk"), P("dp", "blk"), P("blk", "dp", None, None)),
        check_vma=False,
    )
```

profile of v0, /device:TPU:1, one launch (start us, length us, event | category | flops | bytes accessed | tf_op | source)
XLA Modules:
  0.0 368.2 jit_solution(13364037818333791644)
XLA Ops:
  7.2 0.0 copy-start
  7.2 0.0 all-gather.2.cloned.1.call-start
  7.2 1.8 copy.33
  9.0 0.0 all-gather.2.cloned.1.call-update
  9.1 0.8 copy.36
  9.8 0.1 reshape.72
  9.9 1.1 reshape.74
  11.1 0.8 scatter_custom_fusion
  11.9 0.7 maximum_bitcast_fusion
  12.6 1.2 gather_fusion.1
  13.8 0.8 fusion.23
  14.6 0.8 fusion.31
  15.3 74.9 %all-gather.2.cloned.1.call-done = bf16[256,8192]{0,1:T(8,128)(2,1)} async-done(((bf16[256,256]{0,1:T(8,128)(2,1)}), bf16[256,8192]{0,1:T(8,128)(2,1)}) %all-gather.2.cloned.1.call-update) | async-done | bytes 4194320 | tf_op jit(solution)/shard_map/all_gather | solution.py:26
  90.2 6.4 %copy.34 = bf16[256,64,128]{2,0,1:T(8,128)(2,1)} copy(bf16[256,64,128]{0,2,1:T(8,128)(2,1)} %bitcast.58) | data formatting | bytes 8388608 | tf_op jit(solution)/shard_map/reshape | solution.py:27
  96.6 7.9 %gather_fusion = bf16[80,256,128]{2,1,0:T(8,128)(2,1)} fusion(bf16[256,64,128]{2,0,1:T(8,128)(2,1)} %copy.34, s32[1024]{0:T(1024)S(1)} %pad_clamp_fusion.1), kind=kCustom, calls=%fused_computation | custom fusion | bytes 10486080 | tf_op jit(solution)/shard_map/jit(_take)/gather | solution.py:27
  104.5 0.0 copy-done
  104.5 3.7 %fusion.7 = f32[80,256,128]{2,1,0:T(8,128)S(1)} fusion(bf16[1,80,128,128]{3,2,1,0:T(8,128)(2,1)S(1)} %copy-done, bf16[80,256,128]{2,1,0:T(8,128)(2,1)} %gather_fusion, pred[80]{0:T(512)(128)(4,1)S(1)} %get-tuple-element.9), kind=kOutput, calls=%fused_computation.12 | convolution fusion | flops 673710080 | bytes 18350160 | tf_op jit(solution)/shard_map/tsi,sio->sto/dot_general | solution.py:28
  108.2 9.6 %multiply_convert_fusion.1 = (bf16[256,4,128]{2,1,0:T(4,128)(2,1)S(1)}, bf16[256,4,128]{2,1,0:T(4,128)(2,1)S(1)}) fusion(f32[256,4,128]{2,1,0:T(4,128)S(1)} %reshape.74, f32[80,256,128]{2,1,0:T(8,128)S(1)} %fusion.7, s32[80]{0:T(128)S(1)} %get-tuple-element.13, pred[80]{0:T(512)(128)(4,1)S(1)} %get-tuple-element.11), kind=kOutput, calls=%fused_computation.20 | convolution fusion | flops 127271552 | bytes 11534736 | tf_op jit(solution)/shard_map/sto,sc->tco/dot_general | solution.py:29
  117.9 5.5 %gather_fusion.2 = bf16[80,256,128]{2,1,0:T(8,128)(2,1)} fusion(bf16[256,4,128]{2,0,1:T(8,128)(2,1)S(1)} %copy.37, s32[1024]{0:T(1024)S(1)} %pad_clamp_fusion), kind=kCustom, calls=%fused_computation.2 | custom fusion | bytes 10486080 | tf_op jit(solution)/shard_map/jit(_take)/gather | solution.py:34
  123.4 8.0 %fusion.4 = f32[80,256,128]{2,1,0:T(8,128)} fusion(bf16[1,80,128,128]{3,2,1,0:T(8,128)(2,1)S(1)} %copy-done, bf16[80,256,128]{2,1,0:T(8,128)(2,1)} %gather_fusion.2, pred[80]{0:T(512)(128)(4,1)S(1)} %get-tuple-element.10), kind=kOutput, calls=%fused_computation.9 | convolution fusion | flops 673710080 | bytes 18350160 | tf_op jit(solution)/shard_map/tso,sio->sti/dot_general | solution.py:40
  131.4 4.4 %broadcast_in_dim.35 = f32[64,256,128]{2,1,0:T(8,128)} broadcast(f32[]{:T(128)} %constant.42.clone.1), dimensions={} | broadcast | bytes 8388612 | tf_op jit(solution)/shard_map/broadcast_in_dim | solution.py:41
  135.8 24.2 %scatter_fusion = f32[64,256,128]{2,1,0:T(8,128)} fusion(f32[64,256,128]{2,1,0:T(8,128)} %broadcast_in_dim.35, s32[80]{0:T(128)S(1)} %get-tuple-element.12, f32[80,256,128]{2,1,0:T(8,128)} %fusion.4), kind=kCustom, calls=%fused_computation.4 | custom fusion | flops 2621440 | bytes 31457600 | tf_op jit(solution)/shard_map/scatter-add | solution.py:41
  160.0 6.1 %convert_element_type.42 = bf16[64,256,128]{2,1,0:T(8,128)(2,1)} convert(f32[64,256,128]{2,1,0:T(8,128)} %scatter_fusion) | non-fusion elementwise | flops 2097152 | bytes 12582912 | tf_op jit(solution)/shard_map/convert_element_type | solution.py:41
  166.0 8.3 %all-to-all-start = ((bf16[32,2,256,128]{3,2,1,0:T(8,128)(2,1)}), bf16[32,2,256,128]{3,2,1,0:T(8,128)(2,1)}, u32[]{:S(2)}, u32[]{:S(2)}) async-start(bf16[32,2,256,128]{3,2,1,0:T(8,128)(2,1)} %bitcast.57), calls=%async_computation | async-start | bytes 8388608 | tf_op jit(solution)/shard_map/all_to_all | solution.py:44
  174.4 0.0 reduce-scatter.4.cloned.1.call-start
  174.4 7.9 %multiply_convert_fusion = bf16[80,128,128]{2,1,0:T(8,128)(2,1)} fusion(f32[80]{0:T(128)S(1)} %get-tuple-element.8, bf16[80,256,128]{2,1,0:T(8,128)(2,1)} %gather_fusion.2, pred[80]{0:T(512)(128)(4,1)S(1)} %get-tuple-element.10, bf16[80,256,128]{2,1,0:T(8,128)(2,1)} %gather_fusion, pred[80]{0:T(512)(128)(4,1)S(1)} %get-tuple-element.9), kind=kOutput, calls=%fused_computation.14 | convolution fusion | flops 678952960 | bytes 13107680 | tf_op jit(solution)/shard_map/tsi,tso->sio/dot_general | solution.py:54
  182.3 0.0 reduce-scatter.4.cloned.1.call-update
  182.4 0.7 copy.50
  183.1 89.1 %reduce-scatter.4.cloned.1.call-done = bf16[5,128,128]{2,1,0:T(8,128)(2,1)} async-done(((bf16[80,128,128]{2,1,0:T(8,128)(2,1)}), bf16[5,128,128]{2,1,0:T(8,128)(2,1)}) %reduce-scatter.4.cloned.1.call-update) | async-done | bytes 163856
  272.2 1.7 multiply_bitcast_fusion
  273.9 83.8 %all-to-all-done = bf16[32,2,256,128]{3,2,1,0:T(8,128)(2,1)} async-done(((bf16[32,2,256,128]{3,2,1,0:T(8,128)(2,1)}), bf16[32,2,256,128]{3,2,1,0:T(8,128)(2,1)}, u32[]{:S(2)}, u32[]{:S(2)}) %all-to-all-start) | async-done | bytes 4194336 | tf_op jit(solution)/shard_map/all_to_all | solution.py:44
  357.6 2.8 reduce_sum.12
  360.5 0.1 copy.38
  360.6 0.8 copy.40
  (5 shorter events, 0.1 us)
Async XLA Ops:
  7.2 97.3 %copy-start = (bf16[1,80,128,128]{3,2,1,0:T(8,128)(2,1)S(1)}, bf16[1,80,128,128]{3,2,1,0:T(8,128)(2,1)}, u32[]{:S(2)}) copy-start(bf16[1,80,128,128]{3,2,1,0:T(8,128)(2,1)} %param.6) | copy-start | bytes 7864324
  7.2 83.0 %all-gather.2.cloned.1.call-start = ((), (), s32[]{:S(2)}) async-start(), calls=%async_computation.2 | async-start | bytes 4325376 | tf_op jit(solution)/shard_map/all_gather | solution.py:26
  166.0 191.6 %all-to-all-start = ((bf16[32,2,256,128]{3,2,1,0:T(8,128)(2,1)}), bf16[32,2,256,128]{3,2,1,0:T(8,128)(2,1)}, u32[]{:S(2)}, u32[]{:S(2)}) async-start(bf16[32,2,256,128]{3,2,1,0:T(8,128)(2,1)} %bitcast.57), calls=%async_computation | async-start | bytes 8388608 | tf_op jit(solution)/shard_map/all_to_all | solution.py:44
  174.4 97.8 %reduce-scatter.4.cloned.1.call-start = ((), (), s32[]{:S(2)}) async-start(), calls=%async_computation.3 | async-start | bytes 2785280
Sparse Core Ops, SparseCore 0:
  10.7 79.4 all-gather.1
  182.5 89.6 reduce-scatter.3
where the time goes:
time: 374 us; the launch traced here: 368 us
  waiting for transfers between devices  248 us (66%)
  other arithmetic  37 us (10%)
  local copies, waits for them, and re-layouts  31.6 us (8%)
  matrix products  29.3 us (8%)
  between operations  14.1 us (4%)
  starting transfers between devices  8.41 us (2%)
    unnamed x3, waiting for transfers between devices  89.1 us
    all_to_all x1, waiting for transfers between devices, on_device(): lax.all_to_all(partial_value.reshape(dev_count, row_count // dev_count, t...  83.8 us
    all_gather x1, waiting for transfers between devices, on_device(): gathered = lax.all_gather(tokens, 'blk', axis=1, tiled=True)  74.9 us
    scatter-add x1, other arithmetic, on_device(): jax.ops.segment_sum(slot_terms, target, num_segments=row_count)  24.2 us
    dot_general x1, matrix products, on_device(): jnp.einsum('sto,sc->tco', per_slot, col_pick, precision=lax.Precision.HIG...  9.64 us
    all_to_all x1, starting transfers between devices, on_device(): lax.all_to_all(partial_value.reshape(dev_count, row_count // dev_count, t...  8.33 us
    dot_general x1, matrix products, on_device(): jnp.einsum('tso,sio->sti', col_grads, weights, preferred_element_type=jnp...  8.04 us
    dot_general x1, matrix products, on_device(): jnp.einsum('tsi,tso->sio', picked, col_grads, preferred_element_type=jnp....  7.91 us
  transfers between devices with their start and end apart: 3, of which 3 were waited for; matrix products, arithmetic and copies ran while one was open for 4% of the time, Pallas kernels for 0%

commit v1 on v0

v1 whole, which is shorter than its diff:
```python
import functools

import jax
import jax.numpy as jnp
from jax import lax
from jax.experimental import pallas as pl
from jax.experimental.pallas import tpu as pltpu
from jax.sharding import PartitionSpec as P

SMEM = pl.BlockSpec(memory_space=pltpu.SMEM)
VMEM = pl.BlockSpec(memory_space=pltpu.VMEM)
MIB = 1 << 20


def lay_weights(rows_per_dev, listed, cut, core, w_ref, up_ref, down_ref, place):
    half = cut.shape[0] // 2
    slots, blk = w_ref.shape[0], w_ref.shape[1]

    def note(p, carry):
        owner, a = p // rows_per_dev, p % rows_per_dev
        side = (owner % 2 != core[0]).astype(jnp.int32)
        place[cut[p]] = side * half + (owner // 2) * rows_per_dev + a
        return carry

    lax.fori_loop(0, cut.shape[0], note, 0)
    up_ref[...] = jnp.zeros_like(up_ref)
    down_ref[...] = jnp.zeros_like(down_ref)

    def put(s, carry):
        row, col = listed[2 * s], listed[2 * s + 1]

        @pl.when(row >= 0)
        def _():
            block = w_ref[s]
            dev, a = row // rows_per_dev, row % rows_per_dev
            up_ref[dev, pl.ds(pl.multiple_of(a * blk, blk), blk), pl.ds(pl.multiple_of(col * blk, blk), blk)] = block
            to = place[row]
            down_ref[to // rows_per_dev, pl.ds(pl.multiple_of(col * blk, blk), blk),
                     pl.ds(pl.multiple_of((to % rows_per_dev) * blk, blk), blk)] = block.T

        return carry

    lax.fori_loop(0, slots, put, 0)


def hidden_pass(x_ref, up_ref, down_ref, og_ref, act_ref, pg_ref, own_ref, other_ref, acc):
    devs = x_ref.shape[0]
    acc[...] = jnp.dot(x_ref[0], up_ref[0], preferred_element_type=jnp.float32)

    def add(b, carry):
        acc[...] += jnp.dot(x_ref[b], up_ref[b], preferred_element_type=jnp.float32)
        return carry

    lax.fori_loop(1, devs, add, 0)
    hidden = acc[...]
    sig = jax.nn.sigmoid(hidden)
    act_ref[...] = (hidden * sig).astype(jnp.bfloat16)
    pg_ref[...] = (og_ref[...].astype(jnp.float32) * sig * (1.0 + hidden * (1.0 - sig))).astype(jnp.bfloat16)
    half = devs // 2

    def back(k, carry):
        pg = pg_ref[...]
        own_ref[k] = jnp.dot(pg, down_ref[k], preferred_element_type=jnp.float32).astype(jnp.bfloat16)
        other_ref[k] = jnp.dot(pg, down_ref[half + k], preferred_element_type=jnp.float32).astype(jnp.bfloat16)
        return carry

    lax.fori_loop(0, half, back, 0)


def weight_terms(side, rows_per_dev, listed, at, x_ref, pg_ref, *out_refs):
    y_refs, x_refs = out_refs[:side], out_refs[side:]
    per, half, blk = y_refs[0].shape[1:]
    for dx in range(side):
        for dy in range(side):
            owner = lax.rem(at[0] + dx, side) * side + lax.rem(at[1] + dy, side)

            def one(q, carry, dx=dx, dy=dy, owner=owner):
                s = owner * per + q
                row, col = listed[2 * s], listed[2 * s + 1]

                @pl.when(row >= 0)
                def _():
                    dev, a = row // rows_per_dev, row % rows_per_dev
                    x = x_ref[dev, :, pl.ds(pl.multiple_of(a * blk, blk), blk)]
                    g = pg_ref[:, pl.ds(pl.multiple_of(col * blk, blk), blk)]
                    term = lax.dot_general(x, g, (((0,), (0,)), ((), ())), preferred_element_type=jnp.float32)
                    term = term.astype(jnp.bfloat16)
                    y_refs[dy][dx, q] = term[:half]
                    x_refs[dx][dy, q] = term[half:]

                @pl.when(row < 0)
                def _():
                    y_refs[dy][dx, q] = jnp.zeros((half, blk), jnp.bfloat16)
                    x_refs[dx][dy, q] = jnp.zeros((half, blk), jnp.bfloat16)

                return carry

            lax.fori_loop(0, per, one, 0)


def on_device(n_dp, n_blk, tokens, up_blocks, block_list, row_cut, out_grad):
    tok_rows, feats = tokens.shape
    slots, blk = up_blocks.shape[1], up_blocks.shape[2]
    width = out_grad.shape[1]
    rows_per_dev = row_cut.shape[1]
    side = 4
    bf16 = jnp.bfloat16
    z_groups = [list(range(c, n_blk, 2)) for c in range(2)]
    swap = [(i, i ^ 1) for i in range(n_blk)]
    listed = block_list.reshape(-1)
    cut = row_cut.reshape(-1)
    core = (lax.axis_index("blk") % 2).reshape(1).astype(jnp.int32)
    dp_at = lax.axis_index("dp")
    at = jnp.stack([dp_at // side, dp_at % side]).astype(jnp.int32)

    gathered = lax.all_gather(tokens, "blk", axis=0, tiled=False)

    up_w, down_w = pl.pallas_call(
        functools.partial(lay_weights, rows_per_dev),
        out_shape=(
            jax.ShapeDtypeStruct((n_blk, feats, width), bf16),
            jax.ShapeDtypeStruct((n_blk, width, feats), bf16),
        ),
        in_specs=[SMEM, SMEM, SMEM, VMEM],
        out_specs=(VMEM, VMEM),
        scratch_shapes=[pltpu.SMEM((cut.shape[0],), jnp.int32)],
        compiler_params=pltpu.CompilerParams(vmem_limit_bytes=24 * MIB),
        cost_estimate=pl.CostEstimate(flops=0, bytes_accessed=20 * MIB, transcendentals=0),
    )(listed, cut, core, up_blocks[0])

    act, pg, own, other = pl.pallas_call(
        hidden_pass,
        out_shape=(
            jax.ShapeDtypeStruct((tok_rows, width), bf16),
            jax.ShapeDtypeStruct((tok_rows, width), bf16),
            jax.ShapeDtypeStruct((n_blk // 2, tok_rows, feats), bf16),
            jax.ShapeDtypeStruct((n_blk // 2, tok_rows, feats), bf16),
        ),
        in_specs=[VMEM] * 4,
        out_specs=(VMEM,) * 4,
        scratch_shapes=[pltpu.VMEM((tok_rows, width), jnp.float32)],
        compiler_params=pltpu.CompilerParams(vmem_limit_bytes=32 * MIB),
        cost_estimate=pl.CostEstimate(
            flops=4 * tok_rows * width * n_blk * feats, bytes_accessed=24 * MIB, transcendentals=tok_rows * width
        ),
    )(gathered, up_w, down_w, out_grad)

    met = own.astype(jnp.float32) + lax.ppermute(other, "blk", swap).astype(jnp.float32)
    in_grad = lax.psum_scatter(
        met.astype(bf16), "blk", scatter_dimension=0, axis_index_groups=z_groups, tiled=True
    )[0]

    per = slots // n_dp
    piece = jax.ShapeDtypeStruct((side, per, blk // 2, blk), bf16)
    terms = pl.pallas_call(
        functools.partial(weight_terms, side, rows_per_dev),
        out_shape=(piece,) * (2 * side),
        in_specs=[SMEM, SMEM, VMEM, VMEM],
        out_specs=(VMEM,) * (2 * side),
        compiler_params=pltpu.CompilerParams(vmem_limit_bytes=16 * MIB),
        cost_estimate=pl.CostEstimate(
            flops=2 * slots * tok_rows * blk * blk, bytes_accessed=8 * MIB, transcendentals=0
        ),
    )(listed, at, gathered, pg)

    def y_perm(d):
        return [(side * a + b, side * a + (b + d) % side) for a in range(side) for b in range(side)]

    def x_perm(d):
        return [(side * a + b, side * ((a + d) % side) + b) for a in range(side) for b in range(side)]

    def two_hops(parts, first, then):
        got = [parts[0]] + [lax.ppermute(parts[d], "dp", first(d)) for d in range(1, side)]
        half = []
        for d in range(side):
            total = got[0][d].astype(jnp.float32)
            for g in got[1:]:
                total = total + g[d].astype(jnp.float32)
            half.append(total)
        total = half[0]
        for d in range(1, side):
            total = total + lax.ppermute(half[d].astype(bf16), "dp", then(d)).astype(jnp.float32)
        return total

    scale = 1.0 / jnp.sqrt(jnp.float32(tok_rows * n_dp))
    top = two_hops(terms[:side], y_perm, x_perm)
    bottom = two_hops(terms[side:], x_perm, y_perm)
    own_grads = jnp.concatenate([top, bottom], axis=1) * scale
    return act, in_grad, own_grads[None]


def solution(mesh):
    return jax.shard_map(
        functools.partial(on_device, mesh.shape["dp"], mesh.shape["blk"]),
        mesh=mesh,
        in_specs=(
            P("dp", "blk"),
            P("blk", None, None, None),
            P("blk", None, None),
            P(),
            P("dp", "blk"),
        ),
        out_specs=(P("dp", "blk"), P("dp", "blk"), P("blk", "dp", None, None)),
        check_vma=False,
    )
```

time: 374 us -> 196 us (0.52)
  waiting for transfers between devices: 248 us -> 75.4 us
  Pallas kernels: 0 us -> 41.2 us
  other arithmetic: 37 us -> 3.31 us
  starting transfers between devices: 8.41 us -> 41.6 us
  matrix products: 29.3 us -> 0 us
  local copies, waits for them, and re-layouts: 31.6 us -> 17.8 us
    unnamed x3 -> x2, waiting for transfers between devices: 89.1 us -> 0.7 us
    all_to_all x1 -> x0, waiting for transfers between devices: 83.8 us -> none  [on_device(): lax.all_to_all(partial_value.reshape(dev_count, row_count // dev_count, t...]
    ppermute x0 -> x13, starting transfers between devices: none -> 41.5 us  [the longest x6 21.3 us: two_hops(): lax.ppermute(parts[d], 'dp', first(d))]
    pallas_call x0 -> x3, Pallas kernels: none -> 41.2 us  [the longest x1 16.7 us: on_device(): pl.pallas_call(functools.partial(weight_terms, side, rows_per_dev), out_s...]
    dot_general x4 -> x0, matrix products: 29.3 us -> none  [the longest x1 9.64 us: on_device(): jnp.einsum('sto,sc->tco', per_slot, col_pick, precision=lax.Precision.HIG...]
    scatter-add x1 -> x0, other arithmetic: 24.2 us -> none  [on_device(): jax.ops.segment_sum(slot_terms, target, num_segments=row_count)]
    gather x3 -> x0, local copies, waits for them, and re-layouts: 14.6 us -> none  [the longest x1 7.87 us: on_device(): jnp.take(gathered.reshape(tok_rows, row_count, blk_size), safe_rows, axis=1)]
    unnamed x6 -> x16, local copies, waits for them, and re-layouts: 4.09 us -> 17.5 us
  transfers between devices with their start and end apart: 3 -> 15, of which waited for: 3 -> 4; matrix products, arithmetic and copies ran while one was open for 4% -> 2% of each run, Pallas kernels for 0% -> 13%
where the time goes in v1:
time: 196 us; the launch traced here: 194 us
  waiting for transfers between devices  75.4 us (38%)
  starting transfers between devices  41.6 us (21%)
  Pallas kernels  41.2 us (21%)
  local copies, waits for them, and re-layouts  17.8 us (9%)
  between operations  14.3 us (7%)
  other arithmetic  3.31 us (2%)
    all_gather x1, waiting for transfers between devices, on_device(): gathered = lax.all_gather(tokens, 'blk', axis=0, tiled=False)  63.3 us
    ppermute x6, starting transfers between devices, two_hops(): lax.ppermute(parts[d], 'dp', first(d))  21.3 us
    ppermute x6, starting transfers between devices, two_hops(): lax.ppermute(half[d].astype(bf16), 'dp', then(d)).astype(jnp.float32)  18 us
    unnamed x16, local copies, waits for them, and re-layouts  17.5 us
    pallas_call x1, Pallas kernels, on_device(): pl.pallas_call(functools.partial(weight_terms, side, rows_per_dev), out_s...  16.7 us
    pallas_call x1, Pallas kernels, on_device(): pl.pallas_call(hidden_pass, out_shape=(jax.ShapeDtypeStruct((tok_rows, wi...  16.2 us
    pallas_call x1, Pallas kernels, on_device(): pl.pallas_call(functools.partial(lay_weights, rows_per_dev), out_shape=(j...  8.32 us
    ppermute x6, waiting for transfers between devices, two_hops(): lax.ppermute(half[d].astype(bf16), 'dp', then(d)).astype(jnp.float32)  5.49 us
  transfers between devices with their start and end apart: 15, of which 4 were waited for; matrix products, arithmetic and copies ran while one was open for 2% of the time, Pallas kernels for 13%

profile of v1, /device:TPU:1, one launch (start us, length us, event | category | flops | bytes accessed | tf_op | source)
XLA Modules:
  0.0 193.6 jit_solution(7200379817109470796)
XLA Ops:
  7.2 0.0 all-gather.3.cloned.1.call-start
  7.2 0.7 all-gather.3.cloned.1.call-update
  7.9 0.0 reduce-scatter.2.cloned.1.call-start
  8.0 0.8 copy.10
  8.7 0.1 reshape.107.cut
  8.8 0.8 copy.9
  9.6 0.1 reshape.106.listed
  9.7 0.0 copy-start.5
  9.8 1.7 copy-done.5
  11.5 8.3 %shard_map.76 = (bf16[32,256,512]{2,1,0:T(8,128)(2,1)S(1)}, bf16[32,512,256]{2,1,0:T(8,128)(2,1)S(1)}) custom-call(s32[160]{0:T(256)S(1)} %reshape.106.listed, s32[64]{0:T(128)S(1)} %reshape.107.cut, s32[1]{0:T(128)} %bitcast.1.core, bf16[80,128,128]{2,1,0:T(8,128)(2,1)S(1)} %bitcast.40), custom_call_target="tpu_custom_call" | custom-call | bytes 20971520 | tf_op jit(solution)/shard_map/pallas_call | solution.py:118
  19.8 3.3 %copy-done.2 = bf16[32,256,512]{2,1,0:T(8,128)(2,1)} copy-done((bf16[32,256,512]{2,1,0:T(8,128)(2,1)}, bf16[32,256,512]{2,1,0:T(8,128)(2,1)S(1)}, u32[]{:S(2)}) %copy-start.2) | copy-done | bytes 8388632
  23.1 3.2 %copy-done.4 = bf16[32,512,256]{2,1,0:T(8,128)(2,1)} copy-done((bf16[32,512,256]{2,1,0:T(8,128)(2,1)}, bf16[32,512,256]{2,1,0:T(8,128)(2,1)S(1)}, u32[]{:S(2)}) %copy-start.4) | copy-done | bytes 8388632
  26.3 63.3 %all-gather.3.cloned.1.call-done = bf16[8192,256]{1,0:T(8,128)(2,1)} async-done(((bf16[256,256]{1,0:T(8,128)(2,1)}), bf16[8192,256]{1,0:T(8,128)(2,1)}) %all-gather.3.cloned.1.call-update) | async-done | bytes 4194320 | tf_op jit(solution)/shard_map/all_gather | solution.py:116
  89.6 2.2 %copy-done = bf16[8192,256]{1,0:T(8,128)(2,1)S(1)} copy-done((bf16[8192,256]{1,0:T(8,128)(2,1)S(1)}, bf16[8192,256]{1,0:T(8,128)(2,1)}, u32[]{:S(2)}) %copy-start) | copy-done | bytes 4194328
  91.8 3.4 %copy-done.3 = bf16[32,256,512]{2,1,0:T(8,128)(2,1)S(1)} copy-done((bf16[32,256,512]{2,1,0:T(8,128)(2,1)S(1)}, bf16[32,256,512]{2,1,0:T(8,128)(2,1)}, u32[]{:S(2)}) %copy-start.3) | copy-done | bytes 8388632
  95.2 16.2 %shard_map.77 = (bf16[256,512]{1,0:T(8,128)(2,1)}, bf16[256,512]{1,0:T(8,128)(2,1)S(1)}, bf16[16,256,256]{2,1,0:T(8,128)(2,1)S(1)}, bf16[16,256,256]{2,1,0:T(8,128)(2,1)S(1)}) custom-call(bf16[32,256,256]{2,1,0:T(8,128)(2,1)S(1)} %bitcast.38, bf16[32,256,512]{2,1,0:T(8,128)(2,1)S(1)} %copy-done.3, bf16[32,512,256]{2,1,0:T(8,128)(2,1)} %copy-done.4, ...), custom_call_target="tpu_custom_call" | custom-call | flops 4294967296 | bytes 25165824 | tf_op jit(solution)/shard_map/pallas_call | solution.py:131
  111.4 2.2 %collective-permute-start = (bf16[16,256,256]{2,1,0:T(8,128)(2,1)S(1)}, bf16[16,256,256]{2,1,0:T(8,128)(2,1)S(1)}, u32[]{:S(2)}, u32[]{:S(2)}) collective-permute-start(bf16[16,256,256]{2,1,0:T(8,128)(2,1)S(1)} %get-tuple-element.21), channel_id=1, source_target_pairs={{0,1},{1,0},{2,3},{3,2},{4,5},{5,4},{6,7},{7,6},{8,9},{9,8},{10,11... | collective-permute-start | bytes 6291464 | tf_op jit(solution)/shard_map/ppermute | solution.py:148
  113.6 3.9 %collective-permute-done = bf16[16,256,256]{2,1,0:T(8,128)(2,1)S(1)} collective-permute-done((bf16[16,256,256]{2,1,0:T(8,128)(2,1)S(1)}, bf16[16,256,256]{2,1,0:T(8,128)(2,1)S(1)}, u32[]{:S(2)}, u32[]{:S(2)}) %collective-permute-start) | collective-permute-done | bytes 2097184 | tf_op jit(solution)/shard_map/ppermute | solution.py:148
  117.4 2.0 %add_convert_fusion = bf16[16,256,256]{2,1,0:T(8,128)(2,1)} fusion(bf16[16,256,256]{2,1,0:T(8,128)(2,1)S(1)} %collective-permute-done, bf16[16,256,256]{2,1,0:T(8,128)(2,1)S(1)} %get-tuple-element.20), kind=kLoop, calls=%fused_computation | loop fusion | flops 4194304 | bytes 6291456 | tf_op jit(solution)/shard_map/convert_element_type | solution.py:150
  119.4 0.0 reduce-scatter.2.cloned.1.call-update
  119.5 0.1 pad_add_fusion.at
  119.6 2.2 %copy-done.1 = bf16[8192,256]{1,0:T(8,128)(2,1)S(1)} copy-done((bf16[8192,256]{1,0:T(8,128)(2,1)S(1)}, bf16[8192,256]{1,0:T(8,128)(2,1)}, u32[]{:S(2)}) %copy-start.1) | copy-done | bytes 4194328
  121.7 16.7 %shard_map.78 = (bf16[4,5,64,128]{3,2,1,0:T(8,128)(2,1)S(1)}, bf16[4,5,64,128]{3,2,1,0:T(8,128)(2,1)S(1)}, bf16[4,5,64,128]{3,2,1,0:T(8,128)(2,1)S(1)}, bf16[4,5...) custom-call(s32[160]{0:T(256)S(1)} %reshape.106.listed, ...), custom_call_target="tpu_custom_call" | custom-call | flops 671088640 | bytes 8388608 | tf_op jit(solution)/shard_map/pallas_call | solution.py:155
  138.4 3.1 %collective-permute-start.1 = (bf16[4,5,64,128]{3,2,1,0:T(8,128)(2,1)S(1)}, bf16[4,5,64,128]{3,2,1,0:T(8,128)(2,1)S(1)}, u32[]{:S(2)}, u32[]{:S(2)}) collective-permute-start(bf16[4,5,64,128]{3,2,1,0:T(8,128)(2,1)S(1)} %get-tuple-element.24), channel_id=1, source_target_pairs={{0,32},{32,64},{64,96},{96,0},{128,160},{160,192},{192,224},{224,1... | collective-permute-start | bytes 983048 | tf_op jit(solution)/shard_map/ppermute | solution.py:173
  141.5 4.4 %collective-permute-start.2 = (bf16[4,5,64,128]{3,2,1,0:T(8,128)(2,1)S(1)}, bf16[4,5,64,128]{3,2,1,0:T(8,128)(2,1)S(1)}, u32[]{:S(2)}, u32[]{:S(2)}) collective-permute-start(bf16[4,5,64,128]{3,2,1,0:T(8,128)(2,1)S(1)} %get-tuple-element.25), channel_id=1, source_target_pairs={{0,64},{32,96},{64,0},{96,32},{128,192},{160,224},{192,128},{224,1... | collective-permute-start | bytes 983048 | tf_op jit(solution)/shard_map/ppermute | solution.py:173
  145.9 3.3 %collective-permute-start.3 = (bf16[4,5,64,128]{3,2,1,0:T(8,128)(2,1)S(1)}, bf16[4,5,64,128]{3,2,1,0:T(8,128)(2,1)S(1)}, u32[]{:S(2)}, u32[]{:S(2)}) collective-permute-start(bf16[4,5,64,128]{3,2,1,0:T(8,128)(2,1)S(1)} %get-tuple-element.26), channel_id=1, source_target_pairs={{0,96},{32,0},{64,32},{96,64},{128,224},{160,128},{192,160},{224,1... | collective-permute-start | bytes 983048 | tf_op jit(solution)/shard_map/ppermute | solution.py:173
  149.3 3.1 %collective-permute-start.7 = (bf16[4,5,64,128]{3,2,1,0:T(8,128)(2,1)S(1)}, bf16[4,5,64,128]{3,2,1,0:T(8,128)(2,1)S(1)}, u32[]{:S(2)}, u32[]{:S(2)}) collective-permute-start(bf16[4,5,64,128]{3,2,1,0:T(8,128)(2,1)S(1)} %get-tuple-element.28), channel_id=1, source_target_pairs={{0,128},{32,160},{64,192},{96,224},{128,256},{160,288},{192,320},{... | collective-permute-start | bytes 983048 | tf_op jit(solution)/shard_map/ppermute | solution.py:173
  152.4 4.0 %collective-permute-start.8 = (bf16[4,5,64,128]{3,2,1,0:T(8,128)(2,1)S(1)}, bf16[4,5,64,128]{3,2,1,0:T(8,128)(2,1)S(1)}, u32[]{:S(2)}, u32[]{:S(2)}) collective-permute-start(bf16[4,5,64,128]{3,2,1,0:T(8,128)(2,1)S(1)} %get-tuple-element.29), channel_id=1, source_target_pairs={{0,256},{32,288},{64,320},{96,352},{128,384},{160,416},{192,448},{... | collective-permute-start | bytes 983048 | tf_op jit(solution)/shard_map/ppermute | solution.py:173
  156.4 0.0 collective-permute-done.1
  156.4 3.4 %collective-permute-start.9 = (bf16[4,5,64,128]{3,2,1,0:T(8,128)(2,1)S(1)}, bf16[4,5,64,128]{3,2,1,0:T(8,128)(2,1)S(1)}, u32[]{:S(2)}, u32[]{:S(2)}) collective-permute-start(bf16[4,5,64,128]{3,2,1,0:T(8,128)(2,1)S(1)} %get-tuple-element.30), channel_id=1, source_target_pairs={{0,384},{32,416},{64,448},{96,480},{128,0},{160,32},{192,64},{224,... | collective-permute-start | bytes 983048 | tf_op jit(solution)/shard_map/ppermute | solution.py:173
  159.8 0.0 collective-permute-done.2
  159.8 0.0 collective-permute-done.3
  159.8 0.2 fusion.6
  160.0 2.8 %collective-permute-start.4 = (bf16[5,64,128]{2,1,0:T(8,128)(2,1)S(1)}, bf16[5,64,128]{2,1,0:T(8,128)(2,1)S(1)}, u32[]{:S(2)}, u32[]{:S(2)}) collective-permute-start(bf16[5,64,128]{2,1,0:T(8,128)(2,1)S(1)} %get-tuple-element.31), channel_id=1, source_target_pairs={{0,128},{32,160},{64,192},{96,224},{128,256},{160,288},{192,320},{... | collective-permute-start | bytes 245768 | tf_op jit(solution)/shard_map/ppermute | solution.py:182
  162.8 3.7 %collective-permute-start.6 = (bf16[5,64,128]{2,1,0:T(8,128)(2,1)S(1)}, bf16[5,64,128]{2,1,0:T(8,128)(2,1)S(1)}, u32[]{:S(2)}, u32[]{:S(2)}) collective-permute-start(bf16[5,64,128]{2,1,0:T(8,128)(2,1)S(1)} %get-tuple-element.32), channel_id=1, source_target_pairs={{0,384},{32,416},{64,448},{96,480},{128,0},{160,32},{192,64},{224,... | collective-permute-start | bytes 245768 | tf_op jit(solution)/shard_map/ppermute | solution.py:182
  166.5 0.0 collective-permute-done.7
  166.5 3.1 %collective-permute-start.5 = (bf16[5,64,128]{2,1,0:T(8,128)(2,1)S(1)}, bf16[5,64,128]{2,1,0:T(8,128)(2,1)S(1)}, u32[]{:S(2)}, u32[]{:S(2)}) collective-permute-start(bf16[5,64,128]{2,1,0:T(8,128)(2,1)S(1)} %get-tuple-element.33), channel_id=1, source_target_pairs={{0,256},{32,288},{64,320},{96,352},{128,384},{160,416},{192,448},{... | collective-permute-start | bytes 245768 | tf_op jit(solution)/shard_map/ppermute | solution.py:182
  169.7 2.0 %collective-permute-done.9 = bf16[4,5,64,128]{3,2,1,0:T(8,128)(2,1)S(1)} collective-permute-done((bf16[4,5,64,128]{3,2,1,0:T(8,128)(2,1)S(1)}, bf16[4,5,64,128]{3,2,1,0:T(8,128)(2,1)S(1)}, u32[]{:S(2)}, u32[]{:S(2)}) %collective-permute-start.9) | collective-permute-done | bytes 327712 | tf_op jit(solution)/shard_map/ppermute | solution.py:173
  171.7 0.2 fusion.9
  171.8 2.0 %collective-permute-start.10 = (bf16[5,64,128]{2,1,0:T(8,128)(2,1)S(1)}, bf16[5,64,128]{2,1,0:T(8,128)(2,1)S(1)}, u32[]{:S(2)}, u32[]{:S(2)}) collective-permute-start(bf16[5,64,128]{2,1,0:T(8,128)(2,1)S(1)} %get-tuple-element.34), channel_id=1, source_target_pairs={{0,32},{32,64},{64,96},{96,0},{128,160},{160,192},{192,224},{224,1... | collective-permute-start | bytes 245768 | tf_op jit(solution)/shard_map/ppermute | solution.py:182
  173.9 4.4 %collective-permute-start.12 = (bf16[5,64,128]{2,1,0:T(8,128)(2,1)S(1)}, bf16[5,64,128]{2,1,0:T(8,128)(2,1)S(1)}, u32[]{:S(2)}, u32[]{:S(2)}) collective-permute-start(bf16[5,64,128]{2,1,0:T(8,128)(2,1)S(1)} %get-tuple-element.35), channel_id=1, source_target_pairs={{0,96},{32,0},{64,32},{96,64},{128,224},{160,128},{192,160},{224,1... | collective-permute-start | bytes 245768 | tf_op jit(solution)/shard_map/ppermute | solution.py:182
  178.3 0.0 collective-permute-done.4
  178.3 1.9 collective-permute-start.11
  180.3 0.0 collective-permute-done.5
  180.3 0.1 fusion.5
  180.4 5.5 %collective-permute-done.11 = bf16[5,64,128]{2,1,0:T(8,128)(2,1)S(1)} collective-permute-done((bf16[5,64,128]{2,1,0:T(8,128)(2,1)S(1)}, bf16[5,64,128]{2,1,0:T(8,128)(2,1)S(1)}, u32[]{:S(2)}, u32[]{:S(2)}) %collective-permute-start.11) | collective-permute-done | bytes 81952 | tf_op jit(solution)/shard_map/ppermute | solution.py:182
  185.9 0.1 fusion.2
  186.0 0.7 maximum_multiply_fusion
  (12 shorter events, 0.0 us)
Async XLA Ops:
  7.2 82.5 %copy-start.6 = (bf16[256,512]{1,0:T(8,128)(2,1)S(1)}, bf16[256,512]{1,0:T(8,128)(2,1)}, u32[]{:S(2)}) copy-start(bf16[256,512]{1,0:T(8,128)(2,1)} %og_ref.1) | copy-start | bytes 786436
  7.2 82.5 %all-gather.3.cloned.1.call-start = ((), (), s32[]{:S(2)}) async-start(), calls=%async_computation.2 | async-start | bytes 4325376 | tf_op jit(solution)/shard_map/all_gather | solution.py:116
  7.9 178.8 %reduce-scatter.2.cloned.1.call-start = ((), (), s32[]{:S(2)}) async-start(), calls=%async_computation.1 | async-start | bytes 2228224 | tf_op jit(solution)/shard_map/reduce_scatter | solution.py:149
  9.7 1.7 copy-start.5
  19.8 3.3 %copy-start.2 = (bf16[32,256,512]{2,1,0:T(8,128)(2,1)}, bf16[32,256,512]{2,1,0:T(8,128)(2,1)S(1)}, u32[]{:S(2)}) copy-start(bf16[32,256,512]{2,1,0:T(8,128)(2,1)S(1)} %get-tuple-element.17.up_ref) | copy-start | bytes 25165828
  23.1 3.2 %copy-start.4 = (bf16[32,512,256]{2,1,0:T(8,128)(2,1)}, bf16[32,512,256]{2,1,0:T(8,128)(2,1)S(1)}, u32[]{:S(2)}) copy-start(bf16[32,512,256]{2,1,0:T(8,128)(2,1)S(1)} %get-tuple-element.18.down_ref) | copy-start | bytes 25165828
  89.6 2.2 %copy-start = (bf16[8192,256]{1,0:T(8,128)(2,1)S(1)}, bf16[8192,256]{1,0:T(8,128)(2,1)}, u32[]{:S(2)}) copy-start(bf16[8192,256]{1,0:T(8,128)(2,1)} %all-gather.3.cloned.1.call-done) | copy-start | bytes 12582916
  91.8 3.4 %copy-start.3 = (bf16[32,256,512]{2,1,0:T(8,128)(2,1)S(1)}, bf16[32,256,512]{2,1,0:T(8,128)(2,1)}, u32[]{:S(2)}) copy-start(bf16[32,256,512]{2,1,0:T(8,128)(2,1)} %copy-done.2) | copy-start | bytes 25165828
  111.4 6.0 %collective-permute-start = (bf16[16,256,256]{2,1,0:T(8,128)(2,1)S(1)}, bf16[16,256,256]{2,1,0:T(8,128)(2,1)S(1)}, u32[]{:S(2)}, u32[]{:S(2)}) collective-permute-start(bf16[16,256,256]{2,1,0:T(8,128)(2,1)S(1)} %get-tuple-element.21), channel_id=1, source_target_pairs={{0,1},{1,0},{2,3},{3,2},{4,5},{5,4},{6,7},{7,6},{8,9},{9,8},{10,11... | collective-permute-start | bytes 6291464 | tf_op jit(solution)/shard_map/ppermute | solution.py:148
  119.6 2.2 %copy-start.1 = (bf16[8192,256]{1,0:T(8,128)(2,1)S(1)}, bf16[8192,256]{1,0:T(8,128)(2,1)}, u32[]{:S(2)}) copy-start(bf16[8192,256]{1,0:T(8,128)(2,1)} %all-gather.3.cloned.1.call-done) | copy-start | bytes 12582916
  138.4 18.0 %collective-permute-start.1 = (bf16[4,5,64,128]{3,2,1,0:T(8,128)(2,1)S(1)}, bf16[4,5,64,128]{3,2,1,0:T(8,128)(2,1)S(1)}, u32[]{:S(2)}, u32[]{:S(2)}) collective-permute-start(bf16[4,5,64,128]{3,2,1,0:T(8,128)(2,1)S(1)} %get-tuple-element.24), channel_id=1, source_target_pairs={{0,32},{32,64},{64,96},{96,0},{128,160},{160,192},{192,224},{224,1... | collective-permute-start | bytes 983048 | tf_op jit(solution)/shard_map/ppermute | solution.py:173
  141.5 18.3 %collective-permute-start.2 = (bf16[4,5,64,128]{3,2,1,0:T(8,128)(2,1)S(1)}, bf16[4,5,64,128]{3,2,1,0:T(8,128)(2,1)S(1)}, u32[]{:S(2)}, u32[]{:S(2)}) collective-permute-start(bf16[4,5,64,128]{3,2,1,0:T(8,128)(2,1)S(1)} %get-tuple-element.25), channel_id=1, source_target_pairs={{0,64},{32,96},{64,0},{96,32},{128,192},{160,224},{192,128},{224,1... | collective-permute-start | bytes 983048 | tf_op jit(solution)/shard_map/ppermute | solution.py:173
  145.9 13.9 %collective-permute-start.3 = (bf16[4,5,64,128]{3,2,1,0:T(8,128)(2,1)S(1)}, bf16[4,5,64,128]{3,2,1,0:T(8,128)(2,1)S(1)}, u32[]{:S(2)}, u32[]{:S(2)}) collective-permute-start(bf16[4,5,64,128]{3,2,1,0:T(8,128)(2,1)S(1)} %get-tuple-element.26), channel_id=1, source_target_pairs={{0,96},{32,0},{64,32},{96,64},{128,224},{160,128},{192,160},{224,1... | collective-permute-start | bytes 983048 | tf_op jit(solution)/shard_map/ppermute | solution.py:173
  149.3 17.2 %collective-permute-start.7 = (bf16[4,5,64,128]{3,2,1,0:T(8,128)(2,1)S(1)}, bf16[4,5,64,128]{3,2,1,0:T(8,128)(2,1)S(1)}, u32[]{:S(2)}, u32[]{:S(2)}) collective-permute-start(bf16[4,5,64,128]{3,2,1,0:T(8,128)(2,1)S(1)} %get-tuple-element.28), channel_id=1, source_target_pairs={{0,128},{32,160},{64,192},{96,224},{128,256},{160,288},{192,320},{... | collective-permute-start | bytes 983048 | tf_op jit(solution)/shard_map/ppermute | solution.py:173
  152.4 17.3 %collective-permute-start.8 = (bf16[4,5,64,128]{3,2,1,0:T(8,128)(2,1)S(1)}, bf16[4,5,64,128]{3,2,1,0:T(8,128)(2,1)S(1)}, u32[]{:S(2)}, u32[]{:S(2)}) collective-permute-start(bf16[4,5,64,128]{3,2,1,0:T(8,128)(2,1)S(1)} %get-tuple-element.29), channel_id=1, source_target_pairs={{0,256},{32,288},{64,320},{96,352},{128,384},{160,416},{192,448},{... | collective-permute-start | bytes 983048 | tf_op jit(solution)/shard_map/ppermute | solution.py:173
  156.4 15.3 %collective-permute-start.9 = (bf16[4,5,64,128]{3,2,1,0:T(8,128)(2,1)S(1)}, bf16[4,5,64,128]{3,2,1,0:T(8,128)(2,1)S(1)}, u32[]{:S(2)}, u32[]{:S(2)}) collective-permute-start(bf16[4,5,64,128]{3,2,1,0:T(8,128)(2,1)S(1)} %get-tuple-element.30), channel_id=1, source_target_pairs={{0,384},{32,416},{64,448},{96,480},{128,0},{160,32},{192,64},{224,... | collective-permute-start | bytes 983048 | tf_op jit(solution)/shard_map/ppermute | solution.py:173
  160.0 18.3 %collective-permute-start.4 = (bf16[5,64,128]{2,1,0:T(8,128)(2,1)S(1)}, bf16[5,64,128]{2,1,0:T(8,128)(2,1)S(1)}, u32[]{:S(2)}, u32[]{:S(2)}) collective-permute-start(bf16[5,64,128]{2,1,0:T(8,128)(2,1)S(1)} %get-tuple-element.31), channel_id=1, source_target_pairs={{0,128},{32,160},{64,192},{96,224},{128,256},{160,288},{192,320},{... | collective-permute-start | bytes 245768 | tf_op jit(solution)/shard_map/ppermute | solution.py:182
  162.8 17.5 %collective-permute-start.6 = (bf16[5,64,128]{2,1,0:T(8,128)(2,1)S(1)}, bf16[5,64,128]{2,1,0:T(8,128)(2,1)S(1)}, u32[]{:S(2)}, u32[]{:S(2)}) collective-permute-start(bf16[5,64,128]{2,1,0:T(8,128)(2,1)S(1)} %get-tuple-element.32), channel_id=1, source_target_pairs={{0,384},{32,416},{64,448},{96,480},{128,0},{160,32},{192,64},{224,... | collective-permute-start | bytes 245768 | tf_op jit(solution)/shard_map/ppermute | solution.py:182
  166.5 13.8 %collective-permute-start.5 = (bf16[5,64,128]{2,1,0:T(8,128)(2,1)S(1)}, bf16[5,64,128]{2,1,0:T(8,128)(2,1)S(1)}, u32[]{:S(2)}, u32[]{:S(2)}) collective-permute-start(bf16[5,64,128]{2,1,0:T(8,128)(2,1)S(1)} %get-tuple-element.33), channel_id=1, source_target_pairs={{0,256},{32,288},{64,320},{96,352},{128,384},{160,416},{192,448},{... | collective-permute-start | bytes 245768 | tf_op jit(solution)/shard_map/ppermute | solution.py:182
  171.8 8.6 %collective-permute-start.10 = (bf16[5,64,128]{2,1,0:T(8,128)(2,1)S(1)}, bf16[5,64,128]{2,1,0:T(8,128)(2,1)S(1)}, u32[]{:S(2)}, u32[]{:S(2)}) collective-permute-start(bf16[5,64,128]{2,1,0:T(8,128)(2,1)S(1)} %get-tuple-element.34), channel_id=1, source_target_pairs={{0,32},{32,64},{64,96},{96,0},{128,160},{160,192},{192,224},{224,1... | collective-permute-start | bytes 245768 | tf_op jit(solution)/shard_map/ppermute | solution.py:182
  173.9 6.5 %collective-permute-start.12 = (bf16[5,64,128]{2,1,0:T(8,128)(2,1)S(1)}, bf16[5,64,128]{2,1,0:T(8,128)(2,1)S(1)}, u32[]{:S(2)}, u32[]{:S(2)}) collective-permute-start(bf16[5,64,128]{2,1,0:T(8,128)(2,1)S(1)} %get-tuple-element.35), channel_id=1, source_target_pairs={{0,96},{32,0},{64,32},{96,64},{128,224},{160,128},{192,160},{224,1... | collective-permute-start | bytes 245768 | tf_op jit(solution)/shard_map/ppermute | solution.py:182
  178.3 7.5 %collective-permute-start.11 = (bf16[5,64,128]{2,1,0:T(8,128)(2,1)S(1)}, bf16[5,64,128]{2,1,0:T(8,128)(2,1)S(1)}, u32[]{:S(2)}, u32[]{:S(2)}) collective-permute-start(bf16[5,64,128]{2,1,0:T(8,128)(2,1)S(1)} %get-tuple-element.36), channel_id=1, source_target_pairs={{0,64},{32,96},{64,0},{96,32},{128,192},{160,224},{192,128},{224,1... | collective-permute-start | bytes 245768 | tf_op jit(solution)/shard_map/ppermute | solution.py:182
Sparse Core Ops, SparseCore 0:
  10.1 79.4 all-gather.2
  119.6 60.4 reduce-scatter.1

commit v2 on v0

v2 whole, which is shorter than its diff:
```python
import functools

import jax
import jax.numpy as jnp
import numpy as np
from jax import lax
from jax.experimental import pallas as pl
from jax.experimental.pallas import tpu as pltpu
from jax.sharding import PartitionSpec as P

SMEM = pl.BlockSpec(memory_space=pltpu.SMEM)
VMEM = pl.BlockSpec(memory_space=pltpu.VMEM)
MIB = 1 << 20
BF16, F32 = jnp.bfloat16, jnp.float32
NZ = 16

UP_OWN = {0: 0, 4: 2, 2: 4, 6: 6, 1: 9, 5: 11, 3: 13, 7: 15}
UP_OTHER = {4: 17, 2: 19, 6: 21, 1: 24, 5: 26, 3: 28, 7: 30}
DOWN = {1: 0, 5: 2, 3: 4, 7: 6, 4: 9, 2: 11, 6: 13}


def place_tables():
    up, down = np.zeros(2 * NZ, np.int32), np.zeros(2 * NZ, np.int32)
    for i in range(NZ):
        for e in range(2):
            if i < 8:
                up[2 * i + e] = UP_OWN[i] + e
            elif i == 8:
                up[2 * i + e] = (8, 23)[e]
            else:
                up[2 * i + e] = UP_OTHER[NZ - i] + 1 - e
            if i == 0:
                down[2 * i + e] = 8 + 16 * e
            elif i < 8:
                down[2 * i + e] = DOWN[i] + e
            elif i == 8:
                down[2 * i + e] = 15 + 16 * e
            else:
                down[2 * i + e] = 16 + DOWN[NZ - i] + 1 - e
    return up, down


def params(mib):
    return pltpu.CompilerParams(vmem_limit_bytes=mib * MIB)


def cost(flops, size):
    return pl.CostEstimate(flops=flops, bytes_accessed=size, transcendentals=0)


def shape(*dims, dtype=BF16):
    return jax.ShapeDtypeStruct(dims, dtype)


def key_of(dev, me):
    step = lax.rem(dev // 2 - me[0] + NZ, NZ)
    step = jnp.where(me[1] == 0, step, lax.rem(NZ - step, NZ))
    return 2 * step + (dev % 2 != me[1]).astype(jnp.int32)


def at(i, size):
    return pl.ds(pl.multiple_of(i * size, size), size)


def lay_weights(rows_per_dev, listed, cut, me, up_at, down_at, w_ref, up_ref, own_ref, other_ref, place):
    slots, blk = w_ref.shape[0], w_ref.shape[1]

    def note(p, carry):
        place[cut[p]] = p
        return carry

    lax.fori_loop(0, cut.shape[0], note, 0)
    for ref in (up_ref, own_ref, other_ref):
        ref[...] = jnp.zeros_like(ref)

    def put(s, carry):
        row, col = listed[2 * s], listed[2 * s + 1]

        @pl.when(row >= 0)
        def _():
            block = w_ref[s]
            up = up_at[key_of(row // rows_per_dev, me)]
            up_ref[at(up * rows_per_dev + row % rows_per_dev, blk), at(col, blk)] = block
            to = place[row]
            down = down_at[key_of(to // rows_per_dev, me)]
            a = to % rows_per_dev
            flipped = block.T

            @pl.when(down < 16)
            def _():
                own_ref[down, at(col, blk), at(a, blk)] = flipped

            @pl.when(down >= 16)
            def _():
                other_ref[down - 16, at(col, blk), at(a, blk)] = flipped

        return carry

    lax.fori_loop(0, slots, put, 0)


def times(up_ref, first, *x_refs):
    parts = []
    for ref in x_refs:
        parts += [ref[n] for n in range(ref.shape[0])] if len(ref.shape) == 3 else [ref[...]]
    x = jnp.concatenate(parts, axis=1)
    feats = parts[0].shape[1]
    return jnp.dot(x, up_ref[first * feats : (first + len(parts)) * feats], preferred_element_type=F32)


def forward_early(a_ref, g8_ref, up_ref, out_ref):
    out_ref[...] = times(up_ref, 0, a_ref, g8_ref)


def forward_late(so_far, l_ref, b_ref, up_ref, out_ref):
    out_ref[...] = so_far[...] + times(up_ref, 9, l_ref, b_ref)


def forward_last(so_far, s_ref, up_ref, og_ref, act_ref, pg_ref):
    hidden = so_far[...] + times(up_ref, 24, s_ref)
    sig = jax.nn.sigmoid(hidden)
    act_ref[...] = (hidden * sig).astype(BF16)
    pg_ref[...] = (og_ref[...].astype(F32) * sig * (1.0 + hidden * (1.0 - sig))).astype(BF16)


def back(first, pg_ref, pg2_ref, own_ref, sibling_ref, out_ref):
    for n in range(out_ref.shape[0]):
        out_ref[n] = (
            jnp.dot(pg_ref[...], own_ref[first + n], preferred_element_type=F32)
            + jnp.dot(pg2_ref[...], sibling_ref[first + n], preferred_element_type=F32)
        ).astype(out_ref.dtype)


def back_away(pg_ref, pg2_ref, own_ref, sibling_ref, out_ref, last_ref):
    back(0, pg_ref, pg2_ref, own_ref, sibling_ref, out_ref)
    last_ref[...] = (
        jnp.dot(pg_ref[...], own_ref[15], preferred_element_type=F32)
        + jnp.dot(pg2_ref[...], sibling_ref[15], preferred_element_type=F32)
    ).astype(BF16)


def f32(v):
    return v.astype(F32)


def add_first(d_ref, r1_ref, out_ref):
    for n in range(4):
        out_ref[n] = (d_ref[3 + n] + f32(r1_ref[4 + n])).astype(BF16)


def add_second(d_ref, r1_ref, r2_ref, r8_ref, out_ref):
    out_ref[0] = (d_ref[1] + f32(r1_ref[2]) + f32(r2_ref[2]) + f32(r8_ref[...])).astype(BF16)
    out_ref[1] = (d_ref[2] + f32(r1_ref[3]) + f32(r2_ref[3])).astype(BF16)


def add_third(r1_ref, r2_ref, r3_ref, out_ref):
    out_ref[...] = (f32(r1_ref[1]) + f32(r2_ref[1]) + f32(r3_ref[1])).astype(BF16)


def add_last(d_ref, r1_ref, r2_ref, r3_ref, r4_ref, out_ref):
    total = d_ref[0] + f32(r1_ref[0]) + f32(r2_ref[0]) + f32(r3_ref[0]) + f32(r4_ref[...])
    out_ref[...] = total.astype(BF16)


def weight_terms(rows_per_dev, listed, me, up_at, pg_ref, a_ref, g8_ref, l_ref, b_ref, s_ref, out_ref, flipped):
    slots, blk = out_ref.shape[0], out_ref.shape[1]
    flipped[...] = pg_ref[...].T

    def one(s, carry):
        row, col = listed[2 * s], listed[2 * s + 1]
        up = up_at[key_of(jnp.maximum(row, 0) // rows_per_dev, me)]
        lanes = at(jnp.maximum(row, 0) % rows_per_dev, blk)

        def term(x):
            out_ref[s] = jnp.dot(flipped[at(col, blk), :], x, preferred_element_type=F32).astype(BF16)

        def when(low, high):
            return pl.when((row >= 0) & (up >= low) & (up < high))

        @when(0, 8)
        def _():
            term(a_ref[up, :, lanes])

        @when(8, 9)
        def _():
            term(g8_ref[:, lanes])

        @when(9, 17)
        def _():
            term(l_ref[up - 9, :, lanes])

        @when(17, 24)
        def _():
            term(b_ref[up - 17, :, lanes])

        @when(24, 32)
        def _():
            term(s_ref[up - 24, :, lanes])

        @pl.when(row < 0)
        def _():
            out_ref[s] = jnp.zeros((blk, blk), BF16)

        return carry

    lax.fori_loop(0, slots, one, 0)


def add_terms(scale, in_ref, out_ref):
    for q in range(out_ref.shape[0]):
        total = f32(in_ref[0, q])
        for g in range(1, in_ref.shape[0]):
            total = total + f32(in_ref[g, q])
        out_ref[q] = total.T * scale


def kernel(body, out, smem=0, n_in=1, mib=16, flops=0, size=MIB, scratch=()):
    several = isinstance(out, tuple)
    return pl.pallas_call(
        body,
        out_shape=out,
        in_specs=[SMEM] * smem + [VMEM] * n_in,
        out_specs=(VMEM,) * len(out) if several else VMEM,
        scratch_shapes=scratch,
        compiler_params=params(mib),
        cost_estimate=cost(flops, size),
    )


def on_device(n_dp, tokens, up_blocks, block_list, row_cut, out_grad):
    tok_rows, feats = tokens.shape
    slots, blk = up_blocks.shape[1], up_blocks.shape[2]
    width = out_grad.shape[1]
    rows_per_dev = row_cut.shape[1]
    per = slots // n_dp
    listed = block_list.reshape(-1)
    cut = row_cut.reshape(-1)
    blk_at = lax.axis_index("blk")
    me = jnp.stack([blk_at // 2, blk_at % 2]).astype(jnp.int32)
    up_np, down_np = place_tables()
    up_at, down_at = jnp.asarray(up_np), jnp.asarray(down_np)
    shard = 2 * tok_rows * feats

    def other_core(v):
        return lax.ppermute(v, "blk", [(n, n ^ 1) for n in range(2 * NZ)])

    def steps(v, d):
        pairs = [(2 * z + c, 2 * ((z + (d, -d)[c]) % NZ) + c) for z in range(NZ) for c in range(2)]
        return lax.ppermute(v, "blk", pairs)

    def flops_of(shards):
        return 2 * shards * tok_rows * feats * width

    together = lax.optimization_barrier
    theirs = other_core(tokens)
    theirs, listed, cut = together((theirs, listed, cut))
    g0 = jnp.stack([tokens, theirs])
    g4 = steps(g0, -4)

    up_w, down_w, down_other = kernel(
        functools.partial(lay_weights, rows_per_dev),
        (shape(2 * NZ * feats, width),) + (shape(NZ, width, feats),) * 2,
        smem=5, mib=24, size=20 * MIB, scratch=[pltpu.SMEM((cut.shape[0],), jnp.int32)],
    )(listed, cut, me, up_at, down_at, up_blocks[0])
    g4, up_w, down_other = together((g4, up_w, down_other))
    down_sibling = other_core(down_other)

    g26 = steps(jnp.concatenate([g0, g4]), -2)
    g8 = steps(g4[0], -4)
    g26, g8 = together((g26, g8))
    early = jnp.concatenate([g0, g4, g26])
    late = steps(early, -1)
    early_other = other_core(jnp.concatenate([g4, g26, g8[None]]))

    hidden_shape = shape(tok_rows, width, dtype=F32)
    hidden = kernel(forward_early, hidden_shape, n_in=3, flops=flops_of(9), size=4 * MIB)(early, g8, up_w)
    late, hidden, early_other = together((late, hidden, early_other))
    late_other = other_core(late)
    hidden = kernel(forward_late, hidden_shape, n_in=4, flops=flops_of(15), size=6 * MIB)(
        hidden, late, early_other, up_w
    )
    act, pg = kernel(forward_last, (shape(tok_rows, width),) * 2, n_in=4, flops=flops_of(8), size=4 * MIB)(
        hidden, late_other, up_w, out_grad
    )
    pg2 = other_core(pg)

    d1, d8 = kernel(back_away, (shape(8, tok_rows, feats), shape(tok_rows, feats)), n_in=4, flops=flops_of(18), size=6 * MIB)(
        pg, pg2, down_w, down_sibling
    )
    r1 = steps(d1, 1)
    r8 = steps(d8, 4)
    d2 = kernel(functools.partial(back, 8), shape(7, tok_rows, feats, dtype=F32), n_in=4, flops=flops_of(14), size=6 * MIB)(
        pg, pg2, down_w, down_sibling
    )
    pg_after, d2 = together((pg, d2))
    terms = kernel(
        functools.partial(weight_terms, rows_per_dev), shape(slots, blk, blk), smem=3, n_in=6,
        flops=2 * slots * tok_rows * blk * blk, size=8 * MIB, scratch=[pltpu.VMEM((width, tok_rows), BF16)],
    )(listed, me, up_at, pg_after, early, g8, late, early_other, late_other)
    r1, r8, terms = together((r1, r8, terms))
    got = lax.all_to_all(terms, "dp", 0, 0, tiled=True)

    q26 = kernel(add_first, shape(4, tok_rows, feats), n_in=2)(d2, r1)
    r2 = steps(q26, 2)
    q4 = kernel(add_second, shape(2, tok_rows, feats), n_in=4)(d2, r1, r2, r8)
    r3 = steps(q4, 4)
    q0 = kernel(add_third, shape(tok_rows, feats), n_in=3)(r1, r2, r3)
    r4 = other_core(q0)
    in_grad = kernel(add_last, shape(tok_rows, feats), n_in=5)(d2, r1, r2, r3, r4)

    own_grads = kernel(
        functools.partial(add_terms, 1.0 / (tok_rows * n_dp) ** 0.5), shape(per, blk, blk, dtype=F32), size=3 * MIB
    )(got.reshape(n_dp, per, blk, blk))
    return act, in_grad, own_grads[None]


def solution(mesh):
    return jax.shard_map(
        functools.partial(on_device, mesh.shape["dp"]),
        mesh=mesh,
        in_specs=(
            P("dp", "blk"),
            P("blk", None, None, None),
            P("blk", None, None),
            P(),
            P("dp", "blk"),
        ),
        out_specs=(P("dp", "blk"), P("dp", "blk"), P("blk", "dp", None, None)),
        check_vma=False,
    )
```

time: 374 us -> 165 us (0.44); the launches traced: 368 us -> 165 us
  waiting for transfers between devices: 248 us -> 50.3 us
  starting transfers between devices: 8.41 us -> 69.5 us
  Pallas kernels: 0 us -> 35.2 us
  other arithmetic: 37 us -> 2.19 us
  matrix products: 29.3 us -> 0 us
  local copies, waits for them, and re-layouts: 31.6 us -> 6.41 us
  between operations: 14.1 us -> 0.91 us
    unnamed x3 -> x0, waiting for transfers between devices: 89.1 us -> none
    all_to_all x1, waiting for transfers between devices: 83.8 us -> 0.01 us  [on_device(): got = lax.all_to_all(terms, 'dp', 0, 0, tiled=True)]
    all_gather x1 -> x0, waiting for transfers between devices: 74.9 us -> none  [on_device(): gathered = lax.all_gather(tokens, 'blk', axis=1, tiled=True)]
    ppermute x0 -> x14, starting transfers between devices: none -> 63.2 us  [the longest x8 39.6 us: steps(): return lax.ppermute(v, 'blk', pairs)]
    ppermute x0 -> x14, waiting for transfers between devices: none -> 50.3 us  [the longest x8 44.9 us: steps(): return lax.ppermute(v, 'blk', pairs)]
    pallas_call x0 -> x12, Pallas kernels: none -> 35.2 us  [the longest x1 17 us: on_device(): kernel(functools.partial(weight_terms, rows_per_dev), shape(slots, blk, b...]
    dot_general x4 -> x0, matrix products: 29.3 us -> none  [the longest x1 9.64 us: on_device(): jnp.einsum('sto,sc->tco', per_slot, col_pick, precision=lax.Precision.HIG...]
    scatter-add x1 -> x0, other arithmetic: 24.2 us -> none  [on_device(): jax.ops.segment_sum(slot_terms, target, num_segments=row_count)]
  transfers between devices with their start and end apart: 3 -> 15, of which waited for: 3 -> 8; matrix products, arithmetic and copies ran while one was open for 4% -> 2% of each run, Pallas kernels for 0% -> 19%
where the time goes in v2:
time: 165 us
  starting transfers between devices  69.5 us (42%)
  waiting for transfers between devices  50.3 us (30%)
  Pallas kernels  35.2 us (21%)
  local copies, waits for them, and re-layouts  6.41 us (4%)
  other arithmetic  2.19 us (1%)
    ppermute x8, waiting for transfers between devices, steps(): return lax.ppermute(v, 'blk', pairs)  44.9 us
    ppermute x8, starting transfers between devices, steps(): return lax.ppermute(v, 'blk', pairs)  39.6 us
    ppermute x6, starting transfers between devices, other_core(): return lax.ppermute(v, 'blk', [(n, n ^ 1) for n in range(2 * NZ)])  23.6 us
    pallas_call x1, Pallas kernels, on_device(): kernel(functools.partial(weight_terms, rows_per_dev), shape(slots, blk, b...  17 us
    pallas_call x1, Pallas kernels, on_device(): kernel(functools.partial(lay_weights, rows_per_dev), (shape(2 * NZ * feat...  8.32 us
    all_to_all x1, starting transfers between devices, on_device(): got = lax.all_to_all(terms, 'dp', 0, 0, tiled=True)  6.32 us
    unnamed x14, local copies, waits for them, and re-layouts  6.16 us
    ppermute x6, waiting for transfers between devices, other_core(): return lax.ppermute(v, 'blk', [(n, n ^ 1) for n in range(2 * NZ)])  5.44 us
  transfers between devices with their start and end apart: 15, of which 8 were waited for; matrix products, arithmetic and copies ran while one was open for 2% of the time, Pallas kernels for 19%

profile of v2, /device:TPU:1, one launch (start us, length us, event | category | flops | bytes accessed | tf_op | source)
XLA Modules:
  0.0 164.5 jit_solution(455275500639715983)
XLA Ops:
  0.6 8.9 %collective-permute-start = (bf16[256,256]{1,0:T(8,128)(2,1)}, bf16[256,256]{1,0:T(8,128)(2,1)S(1)}, u32[]{:S(2)}, u32[]{:S(2)}) collective-permute-start(bf16[256,256]{1,0:T(8,128)(2,1)} %param.7), channel_id=1, source_target_pairs={{0,1},{1,0},{2,3},{3,2},{4,5},{5,4},{6,7},{7,6},{8,9},{9,8},{10,11... | collective-permute-start | bytes 393224 | tf_op jit(solution)/shard_map/ppermute | solution.py:245
  9.6 0.8 copy.12
  10.3 0.1 reshape.16.cut
  10.4 0.8 copy.11
  11.2 0.1 reshape.15.listed
  11.4 0.9 pad_maximum_fusion.3
  12.3 3.4 %collective-permute-start.1 = (bf16[2,256,256]{2,1,0:T(8,128)(2,1)S(1)}, bf16[2,256,256]{2,1,0:T(8,128)(2,1)S(1)}, u32[]{:S(2)}, u32[]{:S(2)}) collective-permute-start(bf16[2,256,256]{2,1,0:T(8,128)(2,1)S(1)} %pad_maximum_fusion.3), channel_id=1, source_target_pairs={{0,24},{1,9},{2,26},{3,11},{4,28},{5,13},{6,30},{7,15},{8,0},{9,17... | collective-permute-start | bytes 786440 | tf_op jit(solution)/shard_map/ppermute | solution.py:249
  15.8 0.1 pad_add_fusion.me
  15.8 1.7 %copy-done.1 = bf16[1,80,128,128]{3,2,1,0:T(8,128)(2,1)S(1)} copy-done((bf16[1,80,128,128]{3,2,1,0:T(8,128)(2,1)S(1)}, bf16[1,80,128,128]{3,2,1,0:T(8,128)(2,1)}, u32[]{:S(2)}) %copy-start.1) | copy-done | bytes 2621464
  17.6 0.7 copy-done.3
  18.2 0.7 copy-done.4
  18.9 8.3 %shard_map.94 = (bf16[8192,512]{1,0:T(8,128)(2,1)S(1)}, bf16[16,512,256]{2,1,0:T(8,128)(2,1)S(1)}, bf16[16,512,256]{2,1,0:T(8,128)(2,1)S(1)}) custom-call(s32[160]{0:T(256)S(1)} %reshape.15.listed, s32[64]{0:T(128)S(1)} %reshape.16.cut, s32[2]{0:T(128)S(1)} %pad_add_fusion.me, s32[32]{0:T(128)S(1)} %copy-done.3, s32[32]{0:T(128)S(1)} %copy-done.4, ...), custom_call_target="tpu_custom_call" | custom-call | bytes 20971520 | tf_op jit(solution)/shard_map/pallas_call | solution.py:260
  27.2 4.9 %collective-permute-start.8 = (bf16[16,512,256]{2,1,0:T(8,128)(2,1)S(1)}, bf16[16,512,256]{2,1,0:T(8,128)(2,1)S(1)}, u32[]{:S(2)}, u32[]{:S(2)}) collective-permute-start(bf16[16,512,256]{2,1,0:T(8,128)(2,1)S(1)} %get-tuple-element.41), channel_id=1, source_target_pairs={{0,1},{1,0},{2,3},{3,2},{4,5},{5,4},{6,7},{7,6},{8,9},{9,8},{10,11... | collective-permute-start | bytes 12582920 | tf_op jit(solution)/shard_map/ppermute | solution.py:245
  32.2 1.0 pad_maximum_fusion.2
  33.1 3.4 %collective-permute-start.2 = (bf16[4,256,256]{2,1,0:T(8,128)(2,1)S(1)}, bf16[4,256,256]{2,1,0:T(8,128)(2,1)S(1)}, u32[]{:S(2)}, u32[]{:S(2)}) collective-permute-start(bf16[4,256,256]{2,1,0:T(8,128)(2,1)S(1)} %pad_maximum_fusion.2), channel_id=1, source_target_pairs={{0,28},{1,5},{2,30},{3,7},{4,0},{5,9},{6,2},{7,11},{8,4},{9,13},{1... | collective-permute-start | bytes 1572872 | tf_op jit(solution)/shard_map/ppermute | solution.py:249
  36.5 5.9 %collective-permute-start.3 = (bf16[256,256]{1,0:T(8,128)(2,1)S(1)}, bf16[256,256]{1,0:T(8,128)(2,1)S(1)}, u32[]{:S(2)}, u32[]{:S(2)}) collective-permute-start(bf16[256,256]{1,0:T(8,128)(2,1)S(1)} %slice_bitcast_fusion), channel_id=1, source_target_pairs={{0,24},{1,9},{2,26},{3,11},{4,28},{5,13},{6,30},{7,15},{8,0},{9,17... | collective-permute-start | bytes 393224 | tf_op jit(solution)/shard_map/ppermute | solution.py:249
  42.4 9.3 %collective-permute-done.3.g8_ref = bf16[256,256]{1,0:T(8,128)(2,1)S(1)} collective-permute-done((bf16[256,256]{1,0:T(8,128)(2,1)S(1)}, bf16[256,256]{1,0:T(8,128)(2,1)S(1)}, u32[]{:S(2)}, u32[]{:S(2)}) %collective-permute-start.3) | collective-permute-done | bytes 131104 | tf_op jit(solution)/shard_map/ppermute | solution.py:249
  51.8 0.1 pad_maximum_fusion.a_ref
  51.9 10.4 %collective-permute-start.4 = (bf16[8,256,256]{2,1,0:T(8,128)(2,1)S(1)}, bf16[8,256,256]{2,1,0:T(8,128)(2,1)S(1)}, u32[]{:S(2)}, u32[]{:S(2)}) collective-permute-start(bf16[8,256,256]{2,1,0:T(8,128)(2,1)S(1)} %pad_maximum_fusion.a_ref), channel_id=1, source_target_pairs={{0,30},{1,3},{2,0},{3,5},{4,2},{5,7},{6,4},{7,9},{8,6},{9,11},{10,... | collective-permute-start | bytes 3145736 | tf_op jit(solution)/shard_map/ppermute | solution.py:249
  62.3 0.1 pad_maximum_fusion.1
  62.4 1.9 %collective-permute-start.5 = (bf16[7,256,256]{2,1,0:T(8,128)(2,1)S(1)}, bf16[7,256,256]{2,1,0:T(8,128)(2,1)S(1)}, u32[]{:S(2)}, u32[]{:S(2)}) collective-permute-start(bf16[7,256,256]{2,1,0:T(8,128)(2,1)S(1)} %pad_maximum_fusion.1), channel_id=1, source_target_pairs={{0,1},{1,0},{2,3},{3,2},{4,5},{5,4},{6,7},{7,6},{8,9},{9,8},{10,11... | collective-permute-start | bytes 2752520 | tf_op jit(solution)/shard_map/ppermute | solution.py:245
  64.3 0.8 shard_map.95.so_far
  65.1 1.7 %collective-permute-done.5.b_ref = bf16[7,256,256]{2,1,0:T(8,128)(2,1)S(1)} collective-permute-done((bf16[7,256,256]{2,1,0:T(8,128)(2,1)S(1)}, bf16[7,256,256]{2,1,0:T(8,128)(2,1)S(1)}, u32[]{:S(2)}, u32[]{:S(2)}) %collective-permute-start.5) | collective-permute-done | bytes 917536 | tf_op jit(solution)/shard_map/ppermute | solution.py:245
  66.8 9.8 %collective-permute-done.4.l_ref = bf16[8,256,256]{2,1,0:T(8,128)(2,1)S(1)} collective-permute-done((bf16[8,256,256]{2,1,0:T(8,128)(2,1)S(1)}, bf16[8,256,256]{2,1,0:T(8,128)(2,1)S(1)}, u32[]{:S(2)}, u32[]{:S(2)}) %collective-permute-start.4) | collective-permute-done | bytes 1048608 | tf_op jit(solution)/shard_map/ppermute | solution.py:249
  76.6 1.9 %collective-permute-start.6 = (bf16[8,256,256]{2,1,0:T(8,128)(2,1)S(1)}, bf16[8,256,256]{2,1,0:T(8,128)(2,1)S(1)}, u32[]{:S(2)}, u32[]{:S(2)}) collective-permute-start(bf16[8,256,256]{2,1,0:T(8,128)(2,1)S(1)} %collective-permute-done.4.l_ref), channel_id=1, source_target_pairs={{0,1},{1,0},{2,3},{3,2},{4,5},{5,4},{6,7},{7,6},{8,9},{9,8},{10,11... | collective-permute-start | bytes 3145736 | tf_op jit(solution)/shard_map/ppermute | solution.py:245
  78.5 1.2 shard_map.96.so_far
  79.7 1.4 collective-permute-done.6.s_ref
  81.1 1.5 shard_map.97
  82.7 2.0 %collective-permute-start.7 = (bf16[256,512]{1,0:T(8,128)(2,1)S(1)}, bf16[256,512]{1,0:T(8,128)(2,1)S(1)}, u32[]{:S(2)}, u32[]{:S(2)}) collective-permute-start(bf16[256,512]{1,0:T(8,128)(2,1)S(1)} %get-tuple-element.45.pg_ref), channel_id=1, source_target_pairs={{0,1},{1,0},{2,3},{3,2},{4,5},{5,4},{6,7},{7,6},{8,9},{9,8},{10,11... | collective-permute-start | bytes 786440 | tf_op jit(solution)/shard_map/ppermute | solution.py:245
  84.7 1.4 collective-permute-done.7.pg2_ref
  86.1 1.4 shard_map.99
  87.5 3.4 %collective-permute-start.9 = (bf16[8,256,256]{2,1,0:T(8,128)(2,1)S(1)}, bf16[8,256,256]{2,1,0:T(8,128)(2,1)S(1)}, u32[]{:S(2)}, u32[]{:S(2)}) collective-permute-start(bf16[8,256,256]{2,1,0:T(8,128)(2,1)S(1)} %get-tuple-element.43), channel_id=1, source_target_pairs={{0,2},{1,31},{2,4},{3,1},{4,6},{5,3},{6,8},{7,5},{8,10},{9,7},{10,... | collective-permute-start | bytes 3145736 | tf_op jit(solution)/shard_map/ppermute | solution.py:249
  90.8 6.5 %collective-permute-start.10 = (bf16[256,256]{1,0:T(8,128)(2,1)S(1)}, bf16[256,256]{1,0:T(8,128)(2,1)S(1)}, u32[]{:S(2)}, u32[]{:S(2)}) collective-permute-start(bf16[256,256]{1,0:T(8,128)(2,1)S(1)} %get-tuple-element.44), channel_id=1, source_target_pairs={{0,8},{1,25},{2,10},{3,27},{4,12},{5,29},{6,14},{7,31},{8,16},{9,1... | collective-permute-start | bytes 393224 | tf_op jit(solution)/shard_map/ppermute | solution.py:249
  97.4 1.1 shard_map.98.d_ref
  98.5 17.0 %shard_map.100 = bf16[80,128,128]{2,1,0:T(8,128)(2,1)S(1)} custom-call(s32[160]{0:T(256)S(1)} %reshape.15.listed, s32[2]{0:T(128)S(1)} %pad_add_fusion.me, s32[32]{0:T(128)S(1)} %copy-done.3, bf16[256,512]{1,0:T(8,128)(2,1)S(1)} %get-tuple-element.45.pg_ref, bf16[8,256,256]{2,1,0:T(8,128)(2,1)S(1)} %pad_maximum_fusion.a_ref, ...), custom_call_target="tpu_custom_call" | custom-call | flops 671088640 | bytes 8388608 | tf_op jit(solution)/shard_map/pallas_call | solution.py:296
  115.5 1.6 copy-done
  117.1 6.3 %all-to-all-start = ((bf16[80,128,128]{2,1,0:T(8,128)(2,1)}), bf16[80,128,128]{2,1,0:T(8,128)(2,1)}, u32[]{:S(2)}, u32[]{:S(2)}) async-start(bf16[80,128,128]{2,1,0:T(8,128)(2,1)} %copy-done), calls=%async_computation | async-start | bytes 5242880 | tf_op jit(solution)/shard_map/all_to_all | solution.py:301
  123.4 0.1 shard_map.101
  123.5 1.9 %collective-permute-start.11 = (bf16[4,256,256]{2,1,0:T(8,128)(2,1)S(1)}, bf16[4,256,256]{2,1,0:T(8,128)(2,1)S(1)}, u32[]{:S(2)}, u32[]{:S(2)}) collective-permute-start(bf16[4,256,256]{2,1,0:T(8,128)(2,1)S(1)} %shard_map.101), channel_id=1, source_target_pairs={{0,4},{1,29},{2,6},{3,31},{4,8},{5,1},{6,10},{7,3},{8,12},{9,5},{1... | collective-permute-start | bytes 1572872 | tf_op jit(solution)/shard_map/ppermute | solution.py:249
  125.5 11.7 %collective-permute-done.11.r2_ref = bf16[4,256,256]{2,1,0:T(8,128)(2,1)S(1)} collective-permute-done((bf16[4,256,256]{2,1,0:T(8,128)(2,1)S(1)}, bf16[4,256,256]{2,1,0:T(8,128)(2,1)S(1)}, u32[]{:S(2)}, u32[]{:S(2)}) %collective-permute-start.11) | collective-permute-done | bytes 524320 | tf_op jit(solution)/shard_map/ppermute | solution.py:249
  137.1 0.1 shard_map.102
  137.2 4.6 %collective-permute-start.12 = (bf16[2,256,256]{2,1,0:T(8,128)(2,1)S(1)}, bf16[2,256,256]{2,1,0:T(8,128)(2,1)S(1)}, u32[]{:S(2)}, u32[]{:S(2)}) collective-permute-start(bf16[2,256,256]{2,1,0:T(8,128)(2,1)S(1)} %shard_map.102), channel_id=1, source_target_pairs={{0,8},{1,25},{2,10},{3,27},{4,12},{5,29},{6,14},{7,31},{8,16},{9,1... | collective-permute-start | bytes 786440 | tf_op jit(solution)/shard_map/ppermute | solution.py:249
  141.9 14.1 %collective-permute-done.12.r3_ref = bf16[2,256,256]{2,1,0:T(8,128)(2,1)S(1)} collective-permute-done((bf16[2,256,256]{2,1,0:T(8,128)(2,1)S(1)}, bf16[2,256,256]{2,1,0:T(8,128)(2,1)S(1)}, u32[]{:S(2)}, u32[]{:S(2)}) %collective-permute-start.12) | collective-permute-done | bytes 262176 | tf_op jit(solution)/shard_map/ppermute | solution.py:249
  156.0 0.1 shard_map.103
  156.0 3.9 %collective-permute-start.13 = (bf16[256,256]{1,0:T(8,128)(2,1)S(1)}, bf16[256,256]{1,0:T(8,128)(2,1)S(1)}, u32[]{:S(2)}, u32[]{:S(2)}) collective-permute-start(bf16[256,256]{1,0:T(8,128)(2,1)S(1)} %shard_map.103), channel_id=1, source_target_pairs={{0,1},{1,0},{2,3},{3,2},{4,5},{5,4},{6,7},{7,6},{8,9},{9,8},{10,11... | collective-permute-start | bytes 393224 | tf_op jit(solution)/shard_map/ppermute | solution.py:245
  160.0 1.0 collective-permute-done.13.r4_ref
  160.9 0.7 shard_map.104
  161.7 2.9 %shard_map.105 = f32[5,128,128]{2,1,0:T(8,128)} custom-call(bf16[16,5,128,128]{3,2,1,0:T(8,128)(2,1)} %bitcast.7.in_ref), custom_call_target="tpu_custom_call" | custom-call | bytes 3145728 | tf_op jit(solution)/shard_map/pallas_call | solution.py:311
  (16 shorter events, 0.0 us)
Async XLA Ops:
  0.6 51.1 %copy-start.5 = (bf16[256,256]{1,0:T(8,128)(2,1)S(1)}, bf16[256,256]{1,0:T(8,128)(2,1)}, u32[]{:S(2)}) copy-start(bf16[256,256]{1,0:T(8,128)(2,1)} %param.7) | copy-start | bytes 393220
  0.6 10.7 %collective-permute-start = (bf16[256,256]{1,0:T(8,128)(2,1)}, bf16[256,256]{1,0:T(8,128)(2,1)S(1)}, u32[]{:S(2)}, u32[]{:S(2)}) collective-permute-start(bf16[256,256]{1,0:T(8,128)(2,1)} %param.7), channel_id=1, source_target_pairs={{0,1},{1,0},{2,3},{3,2},{4,5},{5,4},{6,7},{7,6},{8,9},{9,8},{10,11... | collective-permute-start | bytes 393224 | tf_op jit(solution)/shard_map/ppermute | solution.py:245
  12.3 14.9 %collective-permute-start.1 = (bf16[2,256,256]{2,1,0:T(8,128)(2,1)S(1)}, bf16[2,256,256]{2,1,0:T(8,128)(2,1)S(1)}, u32[]{:S(2)}, u32[]{:S(2)}) collective-permute-start(bf16[2,256,256]{2,1,0:T(8,128)(2,1)S(1)} %pad_maximum_fusion.3), channel_id=1, source_target_pairs={{0,24},{1,9},{2,26},{3,11},{4,28},{5,13},{6,30},{7,15},{8,0},{9,17... | collective-permute-start | bytes 786440 | tf_op jit(solution)/shard_map/ppermute | solution.py:249
  15.8 1.7 %copy-start.1 = (bf16[1,80,128,128]{3,2,1,0:T(8,128)(2,1)S(1)}, bf16[1,80,128,128]{3,2,1,0:T(8,128)(2,1)}, u32[]{:S(2)}) copy-start(bf16[1,80,128,128]{3,2,1,0:T(8,128)(2,1)} %param.8) | copy-start | bytes 7864324
  17.6 0.7 copy-start.3
  18.2 0.7 copy-start.4
  27.2 58.8 %collective-permute-start.8 = (bf16[16,512,256]{2,1,0:T(8,128)(2,1)S(1)}, bf16[16,512,256]{2,1,0:T(8,128)(2,1)S(1)}, u32[]{:S(2)}, u32[]{:S(2)}) collective-permute-start(bf16[16,512,256]{2,1,0:T(8,128)(2,1)S(1)} %get-tuple-element.41), channel_id=1, source_target_pairs={{0,1},{1,0},{2,3},{3,2},{4,5},{5,4},{6,7},{7,6},{8,9},{9,8},{10,11... | collective-permute-start | bytes 12582920 | tf_op jit(solution)/shard_map/ppermute | solution.py:245
  33.1 18.6 %collective-permute-start.2 = (bf16[4,256,256]{2,1,0:T(8,128)(2,1)S(1)}, bf16[4,256,256]{2,1,0:T(8,128)(2,1)S(1)}, u32[]{:S(2)}, u32[]{:S(2)}) collective-permute-start(bf16[4,256,256]{2,1,0:T(8,128)(2,1)S(1)} %pad_maximum_fusion.2), channel_id=1, source_target_pairs={{0,28},{1,5},{2,30},{3,7},{4,0},{5,9},{6,2},{7,11},{8,4},{9,13},{1... | collective-permute-start | bytes 1572872 | tf_op jit(solution)/shard_map/ppermute | solution.py:249
  36.5 15.2 %collective-permute-start.3 = (bf16[256,256]{1,0:T(8,128)(2,1)S(1)}, bf16[256,256]{1,0:T(8,128)(2,1)S(1)}, u32[]{:S(2)}, u32[]{:S(2)}) collective-permute-start(bf16[256,256]{1,0:T(8,128)(2,1)S(1)} %slice_bitcast_fusion), channel_id=1, source_target_pairs={{0,24},{1,9},{2,26},{3,11},{4,28},{5,13},{6,30},{7,15},{8,0},{9,17... | collective-permute-start | bytes 393224 | tf_op jit(solution)/shard_map/ppermute | solution.py:249
  51.9 24.7 %collective-permute-start.4 = (bf16[8,256,256]{2,1,0:T(8,128)(2,1)S(1)}, bf16[8,256,256]{2,1,0:T(8,128)(2,1)S(1)}, u32[]{:S(2)}, u32[]{:S(2)}) collective-permute-start(bf16[8,256,256]{2,1,0:T(8,128)(2,1)S(1)} %pad_maximum_fusion.a_ref), channel_id=1, source_target_pairs={{0,30},{1,3},{2,0},{3,5},{4,2},{5,7},{6,4},{7,9},{8,6},{9,11},{10,... | collective-permute-start | bytes 3145736 | tf_op jit(solution)/shard_map/ppermute | solution.py:249
  62.4 4.4 %collective-permute-start.5 = (bf16[7,256,256]{2,1,0:T(8,128)(2,1)S(1)}, bf16[7,256,256]{2,1,0:T(8,128)(2,1)S(1)}, u32[]{:S(2)}, u32[]{:S(2)}) collective-permute-start(bf16[7,256,256]{2,1,0:T(8,128)(2,1)S(1)} %pad_maximum_fusion.1), channel_id=1, source_target_pairs={{0,1},{1,0},{2,3},{3,2},{4,5},{5,4},{6,7},{7,6},{8,9},{9,8},{10,11... | collective-permute-start | bytes 2752520 | tf_op jit(solution)/shard_map/ppermute | solution.py:245
  65.1 16.0 %copy-start.2 = (bf16[256,512]{1,0:T(8,128)(2,1)S(1)}, bf16[256,512]{1,0:T(8,128)(2,1)}, u32[]{:S(2)}) copy-start(bf16[256,512]{1,0:T(8,128)(2,1)} %og_ref.1) | copy-start | bytes 786436
  76.6 4.5 %collective-permute-start.6 = (bf16[8,256,256]{2,1,0:T(8,128)(2,1)S(1)}, bf16[8,256,256]{2,1,0:T(8,128)(2,1)S(1)}, u32[]{:S(2)}, u32[]{:S(2)}) collective-permute-start(bf16[8,256,256]{2,1,0:T(8,128)(2,1)S(1)} %collective-permute-done.4.l_ref), channel_id=1, source_target_pairs={{0,1},{1,0},{2,3},{3,2},{4,5},{5,4},{6,7},{7,6},{8,9},{9,8},{10,11... | collective-permute-start | bytes 3145736 | tf_op jit(solution)/shard_map/ppermute | solution.py:245
  82.7 3.4 %collective-permute-start.7 = (bf16[256,512]{1,0:T(8,128)(2,1)S(1)}, bf16[256,512]{1,0:T(8,128)(2,1)S(1)}, u32[]{:S(2)}, u32[]{:S(2)}) collective-permute-start(bf16[256,512]{1,0:T(8,128)(2,1)S(1)} %get-tuple-element.45.pg_ref), channel_id=1, source_target_pairs={{0,1},{1,0},{2,3},{3,2},{4,5},{5,4},{6,7},{7,6},{8,9},{9,8},{10,11... | collective-permute-start | bytes 786440 | tf_op jit(solution)/shard_map/ppermute | solution.py:245
  87.5 29.6 %collective-permute-start.9 = (bf16[8,256,256]{2,1,0:T(8,128)(2,1)S(1)}, bf16[8,256,256]{2,1,0:T(8,128)(2,1)S(1)}, u32[]{:S(2)}, u32[]{:S(2)}) collective-permute-start(bf16[8,256,256]{2,1,0:T(8,128)(2,1)S(1)} %get-tuple-element.43), channel_id=1, source_target_pairs={{0,2},{1,31},{2,4},{3,1},{4,6},{5,3},{6,8},{7,5},{8,10},{9,7},{10,... | collective-permute-start | bytes 3145736 | tf_op jit(solution)/shard_map/ppermute | solution.py:249
  90.8 26.3 %collective-permute-start.10 = (bf16[256,256]{1,0:T(8,128)(2,1)S(1)}, bf16[256,256]{1,0:T(8,128)(2,1)S(1)}, u32[]{:S(2)}, u32[]{:S(2)}) collective-permute-start(bf16[256,256]{1,0:T(8,128)(2,1)S(1)} %get-tuple-element.44), channel_id=1, source_target_pairs={{0,8},{1,25},{2,10},{3,27},{4,12},{5,29},{6,14},{7,31},{8,16},{9,1... | collective-permute-start | bytes 393224 | tf_op jit(solution)/shard_map/ppermute | solution.py:249
  115.5 1.6 copy-start
  117.1 44.6 %all-to-all-start = ((bf16[80,128,128]{2,1,0:T(8,128)(2,1)}), bf16[80,128,128]{2,1,0:T(8,128)(2,1)}, u32[]{:S(2)}, u32[]{:S(2)}) async-start(bf16[80,128,128]{2,1,0:T(8,128)(2,1)} %copy-done), calls=%async_computation | async-start | bytes 5242880 | tf_op jit(solution)/shard_map/all_to_all | solution.py:301
  123.5 13.6 %collective-permute-start.11 = (bf16[4,256,256]{2,1,0:T(8,128)(2,1)S(1)}, bf16[4,256,256]{2,1,0:T(8,128)(2,1)S(1)}, u32[]{:S(2)}, u32[]{:S(2)}) collective-permute-start(bf16[4,256,256]{2,1,0:T(8,128)(2,1)S(1)} %shard_map.101), channel_id=1, source_target_pairs={{0,4},{1,29},{2,6},{3,31},{4,8},{5,1},{6,10},{7,3},{8,12},{9,5},{1... | collective-permute-start | bytes 1572872 | tf_op jit(solution)/shard_map/ppermute | solution.py:249
  137.2 18.8 %collective-permute-start.12 = (bf16[2,256,256]{2,1,0:T(8,128)(2,1)S(1)}, bf16[2,256,256]{2,1,0:T(8,128)(2,1)S(1)}, u32[]{:S(2)}, u32[]{:S(2)}) collective-permute-start(bf16[2,256,256]{2,1,0:T(8,128)(2,1)S(1)} %shard_map.102), channel_id=1, source_target_pairs={{0,8},{1,25},{2,10},{3,27},{4,12},{5,29},{6,14},{7,31},{8,16},{9,1... | collective-permute-start | bytes 786440 | tf_op jit(solution)/shard_map/ppermute | solution.py:249
  156.0 4.9 %collective-permute-start.13 = (bf16[256,256]{1,0:T(8,128)(2,1)S(1)}, bf16[256,256]{1,0:T(8,128)(2,1)S(1)}, u32[]{:S(2)}, u32[]{:S(2)}) collective-permute-start(bf16[256,256]{1,0:T(8,128)(2,1)S(1)} %shard_map.103), channel_id=1, source_target_pairs={{0,1},{1,0},{2,3},{3,2},{4,5},{5,4},{6,7},{7,6},{8,9},{9,8},{10,11... | collective-permute-start | bytes 393224 | tf_op jit(solution)/shard_map/ppermute | solution.py:245

commit v3 on v2

v3 whole, which is shorter than its diff:
```python
import functools

import jax
import jax.numpy as jnp
from jax import lax
from jax.experimental import pallas as pl
from jax.experimental.pallas import tpu as pltpu
from jax.sharding import PartitionSpec as P

SMEM = pl.BlockSpec(memory_space=pltpu.SMEM)
VMEM = pl.BlockSpec(memory_space=pltpu.VMEM)
HBM = pl.BlockSpec(memory_space=pltpu.HBM)
MIB = 1 << 20
BF16, F32 = jnp.bfloat16, jnp.float32
NZ = 16


def params(mib):
    return pltpu.CompilerParams(vmem_limit_bytes=mib * MIB)


def cost(flops, size):
    return pl.CostEstimate(flops=flops, bytes_accessed=size, transcendentals=0)


def shape(*dims, dtype=BF16):
    return jax.ShapeDtypeStruct(dims, dtype)


def my_place():
    here = lax.axis_index("blk")
    return here // 2, lax.rem(here, 2)


def place_of(dev, me):
    z, core = me
    step = lax.rem(dev // 2 - z + NZ, NZ)
    chosen = (step >= NZ // 2).astype(jnp.int32)
    i = jnp.where(step < NZ // 2, step, NZ - 1 - step)
    order = 4 * lax.rem(i, 2) + i // 4 + 2 * lax.rem(i // 2, 2)
    return chosen == core, 2 * order + (lax.rem(dev, 2) != chosen).astype(jnp.int32)


def in_hbm(v):
    return pltpu.with_memory_space_constraint(v, pltpu.HBM)


def at(i, size):
    return pl.ds(pl.multiple_of(i * size, size), size)


def lay_weights(listed_hbm, cut_hbm, w_hbm, up_ref, own_ref, other_ref, listed, cut, place, w_ref, sems):
    copies = [
        pltpu.make_async_copy(src, dst, sems.at[n])
        for n, (src, dst) in enumerate(((listed_hbm, listed), (cut_hbm, cut), (w_hbm, w_ref)))
    ]
    for copy in copies:
        copy.start()
    slots, blk = w_ref.shape[0], w_ref.shape[1]
    rows_per_dev, devs = cut.shape
    me = my_place()

    def note(k, carry):
        for a in range(rows_per_dev):
            place[cut[a, k]] = k * rows_per_dev + a
        return carry

    for ref in (up_ref, own_ref, other_ref):
        ref[...] = jnp.zeros_like(ref)
    for copy in copies:
        copy.wait()
    lax.fori_loop(0, devs, note, 0)

    def put(s, carry):
        row, col = listed[0, s], listed[1, s]

        @pl.when(row >= 0)
        def _():
            block = w_ref[s]
            mine, n = place_of(row // rows_per_dev, me)
            n = jnp.where(mine, n, n + NZ)
            up_ref[at(n * rows_per_dev + lax.rem(row, rows_per_dev), blk), at(col, blk)] = block
            to = place[row]
            mine, n = place_of(to // rows_per_dev, me)
            a = lax.rem(to, rows_per_dev)
            flipped = block.T

            @pl.when(mine)
            def _():
                own_ref[n, at(col, blk), at(a, blk)] = flipped

            @pl.when(jnp.logical_not(mine))
            def _():
                other_ref[n, at(col, blk), at(a, blk)] = flipped

        return carry

    lax.fori_loop(0, slots, put, 0)


def join_first(t_ref, x_ref, y_ref, out_ref):
    core = my_place()[1]

    @pl.when(core == 0)
    def _():
        out_ref[0] = t_ref[...]

    @pl.when(core != 0)
    def _():
        out_ref[0] = y_ref[...]

    out_ref[1] = x_ref[...]


def join(a_ref, b_ref, out_ref):
    n = a_ref.shape[0]
    out_ref[:n] = a_ref[...]
    out_ref[n:] = b_ref[...]


def times(up_ref, first, *x_refs):
    parts = []
    for ref in x_refs:
        parts += [ref[n] for n in range(ref.shape[0])] if len(ref.shape) == 3 else [ref[...]]
    x = jnp.concatenate(parts, axis=1)
    feats = parts[0].shape[1]
    return jnp.dot(x, up_ref[first * feats : (first + len(parts)) * feats], preferred_element_type=F32)


def forward_early(a_ref, up_ref, out_ref):
    out_ref[...] = times(up_ref, 0, a_ref)


def forward_late(so_far, l_ref, b_ref, up_ref, out_ref):
    out_ref[...] = so_far[...] + times(up_ref, 8, l_ref, b_ref)


def forward_last(so_far, s_ref, up_ref, og_ref, act_ref, pg_ref):
    hidden = so_far[...] + times(up_ref, 24, s_ref)
    sig = jax.nn.sigmoid(hidden)
    act_ref[...] = (hidden * sig).astype(BF16)
    pg_ref[...] = (og_ref[...].astype(F32) * sig * (1.0 + hidden * (1.0 - sig))).astype(BF16)


def back(first, pg_ref, pg2_ref, own_ref, sibling_ref, out_ref):
    for n in range(out_ref.shape[0]):
        out_ref[n] = (
            jnp.dot(pg_ref[...], own_ref[first + n], preferred_element_type=F32)
            + jnp.dot(pg2_ref[...], sibling_ref[first + n], preferred_element_type=F32)
        ).astype(out_ref.dtype)


def f32(v):
    return v.astype(F32)


def add_first(d_ref, r1_ref, out_ref):
    for n in range(4):
        out_ref[n] = (d_ref[4 + n] + f32(r1_ref[4 + n])).astype(BF16)


def add_second(d_ref, r1_ref, r2_ref, out_ref):
    for n in range(2):
        out_ref[n] = (d_ref[2 + n] + f32(r1_ref[2 + n]) + f32(r2_ref[2 + n])).astype(BF16)


def add_third(d_ref, r1_ref, r2_ref, r3_ref, same_ref, cross_ref):
    for n, out_ref in enumerate((same_ref, cross_ref)):
        out_ref[...] = (d_ref[n] + f32(r1_ref[n]) + f32(r2_ref[n]) + f32(r3_ref[n])).astype(BF16)


def add_last(same_ref, cross_ref, moved_ref, out_ref):
    core = my_place()[1]

    @pl.when(core == 0)
    def _():
        out_ref[...] = (f32(same_ref[...]) + f32(cross_ref[...])).astype(BF16)

    @pl.when(core != 0)
    def _():
        out_ref[...] = (f32(moved_ref[...]) + f32(cross_ref[...])).astype(BF16)


def weight_terms(listed_hbm, pg_ref, a_ref, l_ref, b_ref, s_ref, out_ref, listed, flipped, dense, sem):
    fetch = pltpu.make_async_copy(listed_hbm, listed, sem)
    fetch.start()
    slots, blk = out_ref.shape[0], out_ref.shape[1]
    rows_per_dev = dense.shape[2] // blk
    me = my_place()
    flipped[...] = pg_ref[...].T
    for m, ref in enumerate((a_ref, l_ref, b_ref, s_ref)):
        for n in range(ref.shape[0]):
            dense[8 * m + n] = jnp.dot(flipped[...], ref[n], preferred_element_type=F32).astype(BF16)

    fetch.wait()

    def one(s, carry):
        row, col = listed[0, s], listed[1, s]
        used = row >= 0
        row, col = jnp.maximum(row, 0), jnp.maximum(col, 0)
        mine, n = place_of(row // rows_per_dev, me)
        n = jnp.where(mine, n, n + NZ)
        block = dense[n, at(col, blk), at(lax.rem(row, rows_per_dev), blk)]
        out_ref[s] = jnp.where(used, block, jnp.zeros_like(block))
        return carry

    lax.fori_loop(0, slots, one, 0, unroll=4)


def add_terms(scale, in_ref, out_ref):
    for q in range(out_ref.shape[0]):
        total = f32(in_ref[0, q])
        for g in range(1, in_ref.shape[0]):
            total = total + f32(in_ref[g, q])
        out_ref[q] = total.T * scale


def kernel(body, out, ins=(), n_in=1, mib=16, flops=0, size=MIB, scratch=()):
    several = isinstance(out, tuple)
    return pl.pallas_call(
        body,
        out_shape=out,
        in_specs=list(ins) + [VMEM] * n_in,
        out_specs=(VMEM,) * len(out) if several else VMEM,
        scratch_shapes=scratch,
        compiler_params=params(mib),
        cost_estimate=cost(flops, size),
    )


def on_device(n_dp, tokens, up_blocks, block_list, row_cut, out_grad):
    tok_rows, feats = tokens.shape
    slots, blk = up_blocks.shape[1], up_blocks.shape[2]
    width = out_grad.shape[1]
    rows_per_dev = row_cut.shape[1]
    per = slots // n_dp
    listed, cut = block_list[0].T, row_cut.T
    around = range(NZ)
    together = lax.optimization_barrier

    def send(v, pairs):
        return lax.ppermute(v, "blk", pairs)

    def other_core(v):
        return send(v, [(n, n ^ 1) for n in range(2 * NZ)])

    def steps(v, d):
        return send(v, [(2 * z + c, 2 * ((z + (d, -d)[c]) % NZ) + c) for z in around for c in range(2)])

    def flops_of(shards):
        return 2 * shards * tok_rows * feats * width

    def shards(n, dtype=BF16):
        return shape(n, tok_rows, feats, dtype=dtype)

    cross_pairs = [(2 * z + 1, 2 * z) for z in around] + [(2 * z, 2 * ((z + 1) % NZ) + 1) for z in around]
    along_pairs = [(2 * z + 1, 2 * ((z + 1) % NZ) + 1) for z in around]

    crossed, along = send(tokens, cross_pairs), send(tokens, along_pairs)
    g0 = kernel(join_first, shards(2), n_in=3)(tokens, crossed, along)
    g0, listed = together((g0, listed))
    g4 = steps(g0, -4)
    up_w, down_w, down_other = kernel(
        lay_weights,
        (shape(2 * NZ * feats, width),) + (shape(NZ, width, feats),) * 2,
        ins=[HBM] * 3, n_in=0, mib=24, size=20 * MIB,
        scratch=[
            pltpu.SMEM(listed.shape, jnp.int32), pltpu.SMEM(cut.shape, jnp.int32), pltpu.SMEM((cut.size,), jnp.int32),
            pltpu.VMEM((slots, blk, blk), BF16), pltpu.SemaphoreType.DMA((3,)),
        ],
    )(in_hbm(listed), in_hbm(cut), in_hbm(up_blocks[0]))
    g4, up_w, down_other = together((g4, up_w, down_other))
    down_sibling = other_core(down_other)

    g04 = kernel(join, shards(4), n_in=2)(g0, g4)
    early = kernel(join, shards(8), n_in=2)(g04, steps(g04, -2))
    late = steps(early, -1)
    hidden_shape = shape(tok_rows, width, dtype=F32)
    hidden = kernel(forward_early, hidden_shape, n_in=2, flops=flops_of(8), size=4 * MIB)(early, up_w)
    early_other = other_core(early)
    late, hidden, early_other = together((late, hidden, early_other))
    late_other = other_core(late)
    hidden = kernel(forward_late, hidden_shape, n_in=4, flops=flops_of(16), size=6 * MIB)(
        hidden, late, early_other, up_w
    )
    act, pg = kernel(forward_last, (shape(tok_rows, width),) * 2, n_in=4, flops=flops_of(8), size=4 * MIB)(
        hidden, late_other, up_w, out_grad
    )
    pg2 = other_core(pg)

    d1 = kernel(functools.partial(back, 8), shards(8), n_in=4, flops=flops_of(16), size=6 * MIB)(
        pg, pg2, down_w, down_sibling
    )
    pg_after, d1 = together((pg, d1))
    r1 = steps(d1, 1)
    d2 = kernel(functools.partial(back, 0), shards(8, F32), n_in=4, flops=flops_of(16), size=6 * MIB)(
        pg, pg2, down_w, down_sibling
    )
    pg_after, d2 = together((pg_after, d2))
    terms = kernel(
        weight_terms, shape(slots, blk, blk), ins=[HBM], n_in=5, mib=14,
        flops=flops_of(32), size=16 * MIB,
        scratch=[
            pltpu.SMEM(listed.shape, jnp.int32), pltpu.VMEM((width, tok_rows), BF16),
            pltpu.VMEM((2 * NZ, width, feats), BF16), pltpu.SemaphoreType.DMA,
        ],
    )(in_hbm(listed), pg_after, early, late, early_other, late_other)
    r1, terms = together((r1, terms))
    got = lax.all_to_all(terms, "dp", 0, 0, tiled=True)
    q26 = kernel(add_first, shards(4), n_in=2)(d2, r1)
    r2 = steps(q26, 2)
    q4 = kernel(add_second, shards(2), n_in=3, flops=10**11)(d2, r1, r2)
    r3 = steps(q4, 4)
    one = shape(tok_rows, feats)
    same, cross = kernel(add_third, (one, one), n_in=4)(d2, r1, r2, r3)
    crossed = send(cross, [(b, a) for a, b in cross_pairs])
    moved = send(same, [(b, a) for a, b in along_pairs])
    in_grad = kernel(add_last, one, n_in=3)(same, crossed, moved)

    own_grads = kernel(
        functools.partial(add_terms, 1.0 / (tok_rows * n_dp) ** 0.5), shape(per, blk, blk, dtype=F32), size=3 * MIB
    )(got.reshape(n_dp, per, blk, blk))
    return act, in_grad, own_grads[None]


def solution(mesh):
    return jax.shard_map(
        functools.partial(on_device, mesh.shape["dp"]),
        mesh=mesh,
        in_specs=(
            P("dp", "blk"),
            P("blk", None, None, None),
            P("blk", None, None),
            P(),
            P("dp", "blk"),
        ),
        out_specs=(P("dp", "blk"), P("dp", "blk"), P("blk", "dp", None, None)),
        check_vma=False,
    )
```

time: 165 us -> 157 us (0.952)
  waiting for transfers between devices: 50.3 us -> 69.9 us
  starting transfers between devices: 69.5 us -> 57.9 us
  Pallas kernels: 35.2 us -> 25.4 us
  local copies, waits for them, and re-layouts: 6.41 us -> 2.4 us
  other arithmetic: 2.19 us -> 0 us
    ppermute x14, waiting for transfers between devices: 50.3 us -> 69.9 us  [send(): return lax.ppermute(v, 'blk', pairs)]
    ppermute x14, starting transfers between devices: 63.2 us -> 51.4 us  [send(): return lax.ppermute(v, 'blk', pairs)]
    pallas_call x10 -> x13, Pallas kernels: 30.7 us -> 20.9 us  [the longest x1 6.82 us: on_device(): kernel(lay_weights, (shape(2 * NZ * feats, width),) + (shape(NZ, width, f...]
    unnamed x14 -> x6, local copies, waits for them, and re-layouts: 6.16 us -> 2.4 us
  transfers between devices with their start and end apart: 15 -> 15, of which waited for: 8 -> 12; matrix products, arithmetic and copies ran while one was open for 2% -> 0% of each run, Pallas kernels for 19% -> 13%
where the time goes in v3:
time: 157 us; the launch traced here: 156 us
  waiting for transfers between devices  69.9 us (45%)
  starting transfers between devices  57.9 us (37%)
  Pallas kernels  25.4 us (16%)
  local copies, waits for them, and re-layouts  2.4 us (2%)
    ppermute x14, waiting for transfers between devices, send(): return lax.ppermute(v, 'blk', pairs)  69.9 us
    ppermute x14, starting transfers between devices, send(): return lax.ppermute(v, 'blk', pairs)  51.4 us
    pallas_call x1, Pallas kernels, on_device(): kernel(lay_weights, (shape(2 * NZ * feats, width),) + (shape(NZ, width, f...  6.82 us
    all_to_all x1, starting transfers between devices, on_device(): got = lax.all_to_all(terms, 'dp', 0, 0, tiled=True)  6.52 us
    pallas_call x1, Pallas kernels, on_device(): kernel(weight_terms, shape(slots, blk, blk), ins=[HBM], n_in=5, mib=14, f...  5.7 us
  transfers between devices with their start and end apart: 15, of which 12 were waited for; matrix products, arithmetic and copies ran while one was open for 0% of the time, Pallas kernels for 13%

profile of v3, /device:TPU:1, one launch (start us, length us, event | category | flops | bytes accessed | tf_op | source)
XLA Modules:
  0.0 156.4 jit_solution(9375031771070412539)
XLA Ops:
  0.6 8.8 %collective-permute-start = (bf16[256,256]{1,0:T(8,128)(2,1)}, bf16[256,256]{1,0:T(8,128)(2,1)S(1)}, u32[]{:S(2)}, u32[]{:S(2)}) collective-permute-start(bf16[256,256]{1,0:T(8,128)(2,1)} %t_ref.1), channel_id=1, source_target_pairs={{1,0},{3,2},{5,4},{7,6},{9,8},{11,10},{13,12},{15,14},{17,16},{19,... | collective-permute-start | bytes 393224 | tf_op jit(solution)/shard_map/ppermute | solution.py:242
  9.4 1.9 %collective-permute-start.1 = (bf16[256,256]{1,0:T(8,128)(2,1)}, bf16[256,256]{1,0:T(8,128)(2,1)S(1)}, u32[]{:S(2)}, u32[]{:S(2)}) collective-permute-start(bf16[256,256]{1,0:T(8,128)(2,1)} %t_ref.1), channel_id=1, source_target_pairs={{1,3},{3,5},{5,7},{7,9},{9,11},{11,13},{13,15},{15,17},{17,19},{19... | collective-permute-start | bytes 393224 | tf_op jit(solution)/shard_map/ppermute | solution.py:242
  11.4 4.6 %collective-permute-done.x_ref = bf16[256,256]{1,0:T(8,128)(2,1)S(1)} collective-permute-done((bf16[256,256]{1,0:T(8,128)(2,1)}, bf16[256,256]{1,0:T(8,128)(2,1)S(1)}, u32[]{:S(2)}, u32[]{:S(2)}) %collective-permute-start) | collective-permute-done | bytes 131104 | tf_op jit(solution)/shard_map/ppermute | solution.py:242
  16.0 1.7 %collective-permute-done.1.y_ref = bf16[256,256]{1,0:T(8,128)(2,1)S(1)} collective-permute-done((bf16[256,256]{1,0:T(8,128)(2,1)}, bf16[256,256]{1,0:T(8,128)(2,1)S(1)}, u32[]{:S(2)}, u32[]{:S(2)}) %collective-permute-start.1) | collective-permute-done | bytes 131104 | tf_op jit(solution)/shard_map/ppermute | solution.py:242
  17.7 0.9 copy-done.2
  18.7 2.3 %collective-permute-start.2 = (bf16[2,256,256]{2,1,0:T(8,128)(2,1)S(1)}, bf16[2,256,256]{2,1,0:T(8,128)(2,1)S(1)}, u32[]{:S(2)}, u32[]{:S(2)}) collective-permute-start(bf16[2,256,256]{2,1,0:T(8,128)(2,1)S(1)} %shard_map.76.a_ref), channel_id=1, source_target_pairs={{0,24},{1,9},{2,26},{3,11},{4,28},{5,13},{6,30},{7,15},{8,0},{9,17... | collective-permute-start | bytes 786440 | tf_op jit(solution)/shard_map/ppermute | solution.py:242
  20.9 6.8 %shard_map.77 = (bf16[8192,512]{1,0:T(8,128)(2,1)S(1)}, bf16[16,512,256]{2,1,0:T(8,128)(2,1)S(1)}, bf16[16,512,256]{2,1,0:T(8,128)(2,1)S(1)}) custom-call(s32[2,80]{1,0:T(2,128)} %bitcast.10, s32[2,32]{1,0:T(2,128)} %bitcast.9, bf16[80,128,128]{2,1,0:T(8,128)(2,1)} %bitcast.7), custom_call_target="tpu_custom_call" | custom-call | bytes 20971520 | tf_op jit(solution)/shard_map/pallas_call | solution.py:263
  27.8 10.3 %collective-permute-done.2.b_ref = bf16[2,256,256]{2,1,0:T(8,128)(2,1)S(1)} collective-permute-done((bf16[2,256,256]{2,1,0:T(8,128)(2,1)S(1)}, bf16[2,256,256]{2,1,0:T(8,128)(2,1)S(1)}, u32[]{:S(2)}, u32[]{:S(2)}) %collective-permute-start.2) | collective-permute-done | bytes 262176 | tf_op jit(solution)/shard_map/ppermute | solution.py:242
  38.1 1.9 %collective-permute-start.8 = (bf16[16,512,256]{2,1,0:T(8,128)(2,1)S(1)}, bf16[16,512,256]{2,1,0:T(8,128)(2,1)S(1)}, u32[]{:S(2)}, u32[]{:S(2)}) collective-permute-start(bf16[16,512,256]{2,1,0:T(8,128)(2,1)S(1)} %get-tuple-element.36), channel_id=1, source_target_pairs={{0,1},{1,0},{2,3},{3,2},{4,5},{5,4},{6,7},{7,6},{8,9},{9,8},{10,11... | collective-permute-start | bytes 12582920 | tf_op jit(solution)/shard_map/ppermute | solution.py:242
  40.1 1.9 %collective-permute-start.3 = (bf16[4,256,256]{2,1,0:T(8,128)(2,1)S(1)}, bf16[4,256,256]{2,1,0:T(8,128)(2,1)S(1)}, u32[]{:S(2)}, u32[]{:S(2)}) collective-permute-start(bf16[4,256,256]{2,1,0:T(8,128)(2,1)S(1)} %shard_map.78.a_ref), channel_id=1, source_target_pairs={{0,28},{1,5},{2,30},{3,7},{4,0},{5,9},{6,2},{7,11},{8,4},{9,13},{1... | collective-permute-start | bytes 1572872 | tf_op jit(solution)/shard_map/ppermute | solution.py:242
  42.0 13.6 %collective-permute-done.3.b_ref = bf16[4,256,256]{2,1,0:T(8,128)(2,1)S(1)} collective-permute-done((bf16[4,256,256]{2,1,0:T(8,128)(2,1)S(1)}, bf16[4,256,256]{2,1,0:T(8,128)(2,1)S(1)}, u32[]{:S(2)}, u32[]{:S(2)}) %collective-permute-start.3) | collective-permute-done | bytes 524320 | tf_op jit(solution)/shard_map/ppermute | solution.py:242
  55.6 0.1 shard_map.79.a_ref
  55.6 1.9 %collective-permute-start.5 = (bf16[8,256,256]{2,1,0:T(8,128)(2,1)S(1)}, bf16[8,256,256]{2,1,0:T(8,128)(2,1)S(1)}, u32[]{:S(2)}, u32[]{:S(2)}) collective-permute-start(bf16[8,256,256]{2,1,0:T(8,128)(2,1)S(1)} %shard_map.79.a_ref), channel_id=1, source_target_pairs={{0,1},{1,0},{2,3},{3,2},{4,5},{5,4},{6,7},{7,6},{8,9},{9,8},{10,11... | collective-permute-start | bytes 3145736 | tf_op jit(solution)/shard_map/ppermute | solution.py:242
  57.6 2.0 %collective-permute-start.4 = (bf16[8,256,256]{2,1,0:T(8,128)(2,1)S(1)}, bf16[8,256,256]{2,1,0:T(8,128)(2,1)S(1)}, u32[]{:S(2)}, u32[]{:S(2)}) collective-permute-start(bf16[8,256,256]{2,1,0:T(8,128)(2,1)S(1)} %shard_map.79.a_ref), channel_id=1, source_target_pairs={{0,30},{1,3},{2,0},{3,5},{4,2},{5,7},{6,4},{7,9},{8,6},{9,11},{10,... | collective-permute-start | bytes 3145736 | tf_op jit(solution)/shard_map/ppermute | solution.py:242
  59.5 0.7 shard_map.80.so_far
  60.2 0.0 copy-start.1
  60.2 0.0 collective-permute-done.5.b_ref
  60.2 14.6 %collective-permute-done.4.l_ref = bf16[8,256,256]{2,1,0:T(8,128)(2,1)S(1)} collective-permute-done((bf16[8,256,256]{2,1,0:T(8,128)(2,1)S(1)}, bf16[8,256,256]{2,1,0:T(8,128)(2,1)S(1)}, u32[]{:S(2)}, u32[]{:S(2)}) %collective-permute-start.4) | collective-permute-done | bytes 1048608 | tf_op jit(solution)/shard_map/ppermute | solution.py:242
  74.8 2.3 %collective-permute-start.6 = (bf16[8,256,256]{2,1,0:T(8,128)(2,1)S(1)}, bf16[8,256,256]{2,1,0:T(8,128)(2,1)S(1)}, u32[]{:S(2)}, u32[]{:S(2)}) collective-permute-start(bf16[8,256,256]{2,1,0:T(8,128)(2,1)S(1)} %collective-permute-done.4.l_ref), channel_id=1, source_target_pairs={{0,1},{1,0},{2,3},{3,2},{4,5},{5,4},{6,7},{7,6},{8,9},{9,8},{10,11... | collective-permute-start | bytes 3145736 | tf_op jit(solution)/shard_map/ppermute | solution.py:242
  77.1 1.2 shard_map.81.so_far
  78.4 1.0 collective-permute-done.6.s_ref
  79.4 0.0 copy-done.1
  79.4 1.5 shard_map.82
  80.9 2.3 %collective-permute-start.7 = (bf16[256,512]{1,0:T(8,128)(2,1)S(1)}, bf16[256,512]{1,0:T(8,128)(2,1)S(1)}, u32[]{:S(2)}, u32[]{:S(2)}) collective-permute-start(bf16[256,512]{1,0:T(8,128)(2,1)S(1)} %get-tuple-element.40.pg_ref), channel_id=1, source_target_pairs={{0,1},{1,0},{2,3},{3,2},{4,5},{5,4},{6,7},{7,6},{8,9},{9,8},{10,11... | collective-permute-start | bytes 786440 | tf_op jit(solution)/shard_map/ppermute | solution.py:242
  83.2 1.1 collective-permute-done.7.pg2_ref
  84.4 0.0 collective-permute-done.8.sibling_ref
  84.4 1.2 shard_map.83
  85.6 5.3 %collective-permute-start.9 = (bf16[8,256,256]{2,1,0:T(8,128)(2,1)S(1)}, bf16[8,256,256]{2,1,0:T(8,128)(2,1)S(1)}, u32[]{:S(2)}, u32[]{:S(2)}) collective-permute-start(bf16[8,256,256]{2,1,0:T(8,128)(2,1)S(1)} %shard_map.83), channel_id=1, source_target_pairs={{0,2},{1,31},{2,4},{3,1},{4,6},{5,3},{6,8},{7,5},{8,10},{9,7},{10,... | collective-permute-start | bytes 3145736 | tf_op jit(solution)/shard_map/ppermute | solution.py:242
  91.0 1.2 shard_map.84.d_ref
  92.2 5.7 %shard_map.85 = bf16[80,128,128]{2,1,0:T(8,128)(2,1)S(1)} custom-call(s32[2,80]{1,0:T(2,128)} %bitcast.11, bf16[256,512]{1,0:T(8,128)(2,1)S(1)} %get-tuple-element.40.pg_ref, bf16[8,256,256]{2,1,0:T(8,128)(2,1)S(1)} %shard_map.79.a_ref, bf16[8,256,256]{2,1,0:T(8,128)(2,1)S(1)} %collective-permute-done.4.l_ref, ...), custom_call_target="tpu_custom_call" | custom-call | flops 2147483648 | bytes 16777216 | tf_op jit(solution)/shard_map/pallas_call | solution.py:300
  97.9 0.0 copy-start
  97.9 1.5 copy-done
  99.4 3.3 %collective-permute-done.9.r1_ref = bf16[8,256,256]{2,1,0:T(8,128)(2,1)S(1)} collective-permute-done((bf16[8,256,256]{2,1,0:T(8,128)(2,1)S(1)}, bf16[8,256,256]{2,1,0:T(8,128)(2,1)S(1)}, u32[]{:S(2)}, u32[]{:S(2)}) %collective-permute-start.9) | collective-permute-done | bytes 1048608 | tf_op jit(solution)/shard_map/ppermute | solution.py:242
  102.7 0.9 shard_map.86
  103.6 3.8 %collective-permute-start.10 = (bf16[4,256,256]{2,1,0:T(8,128)(2,1)}, bf16[4,256,256]{2,1,0:T(8,128)(2,1)}, u32[]{:S(2)}, u32[]{:S(2)}) collective-permute-start(bf16[4,256,256]{2,1,0:T(8,128)(2,1)} %shard_map.86), channel_id=1, source_target_pairs={{0,4},{1,29},{2,6},{3,31},{4,8},{5,1},{6,10},{7,3},{8,12},{9,5},{1... | collective-permute-start | bytes 1572872 | tf_op jit(solution)/shard_map/ppermute | solution.py:242
  107.4 6.5 %all-to-all-start = ((bf16[80,128,128]{2,1,0:T(8,128)(2,1)}), bf16[80,128,128]{2,1,0:T(8,128)(2,1)}, u32[]{:S(2)}, u32[]{:S(2)}) async-start(bf16[80,128,128]{2,1,0:T(8,128)(2,1)} %copy-done), calls=%async_computation | async-start | bytes 5242880 | tf_op jit(solution)/shard_map/all_to_all | solution.py:309
  113.9 4.9 %collective-permute-done.10.r2_ref = bf16[4,256,256]{2,1,0:T(8,128)(2,1)} collective-permute-done((bf16[4,256,256]{2,1,0:T(8,128)(2,1)}, bf16[4,256,256]{2,1,0:T(8,128)(2,1)}, u32[]{:S(2)}, u32[]{:S(2)}) %collective-permute-start.10) | collective-permute-done | bytes 524320 | tf_op jit(solution)/shard_map/ppermute | solution.py:242
  118.8 1.1 shard_map.87
  119.9 6.7 %collective-permute-start.11 = (bf16[2,256,256]{2,1,0:T(8,128)(2,1)S(1)}, bf16[2,256,256]{2,1,0:T(8,128)(2,1)S(1)}, u32[]{:S(2)}, u32[]{:S(2)}) collective-permute-start(bf16[2,256,256]{2,1,0:T(8,128)(2,1)S(1)} %shard_map.87), channel_id=1, source_target_pairs={{0,8},{1,25},{2,10},{3,27},{4,12},{5,29},{6,14},{7,31},{8,16},{9,1... | collective-permute-start | bytes 786440 | tf_op jit(solution)/shard_map/ppermute | solution.py:242
  126.7 8.6 %collective-permute-done.11.r3_ref = bf16[2,256,256]{2,1,0:T(8,128)(2,1)S(1)} collective-permute-done((bf16[2,256,256]{2,1,0:T(8,128)(2,1)S(1)}, bf16[2,256,256]{2,1,0:T(8,128)(2,1)S(1)}, u32[]{:S(2)}, u32[]{:S(2)}) %collective-permute-start.11) | collective-permute-done | bytes 262176 | tf_op jit(solution)/shard_map/ppermute | solution.py:242
  135.3 1.2 shard_map.88
  136.4 8.3 %collective-permute-start.12 = (bf16[256,256]{1,0:T(8,128)(2,1)S(1)}, bf16[256,256]{1,0:T(8,128)(2,1)S(1)}, u32[]{:S(2)}, u32[]{:S(2)}) collective-permute-start(bf16[256,256]{1,0:T(8,128)(2,1)S(1)} %get-tuple-element.43), channel_id=1, source_target_pairs={{0,1},{2,3},{4,5},{6,7},{8,9},{10,11},{12,13},{14,15},{16,17},{18,... | collective-permute-start | bytes 393224 | tf_op jit(solution)/shard_map/ppermute | solution.py:242
  144.7 1.9 %collective-permute-start.13 = (bf16[256,256]{1,0:T(8,128)(2,1)S(1)}, bf16[256,256]{1,0:T(8,128)(2,1)S(1)}, u32[]{:S(2)}, u32[]{:S(2)}) collective-permute-start(bf16[256,256]{1,0:T(8,128)(2,1)S(1)} %get-tuple-element.42.same_ref), channel_id=1, source_target_pairs={{3,1},{5,3},{7,5},{9,7},{11,9},{13,11},{15,13},{17,15},{19,17},{21... | collective-permute-start | bytes 393224 | tf_op jit(solution)/shard_map/ppermute | solution.py:242
  146.7 1.4 collective-permute-done.12.cross_ref
  148.0 4.8 %collective-permute-done.13.moved_ref = bf16[256,256]{1,0:T(8,128)(2,1)S(1)} collective-permute-done((bf16[256,256]{1,0:T(8,128)(2,1)S(1)}, bf16[256,256]{1,0:T(8,128)(2,1)S(1)}, u32[]{:S(2)}, u32[]{:S(2)}) %collective-permute-start.13) | collective-permute-done | bytes 131104 | tf_op jit(solution)/shard_map/ppermute | solution.py:242
  152.8 0.7 shard_map.89
  153.5 0.0 all-to-all-done
  153.5 2.9 %shard_map.90 = f32[5,128,128]{2,1,0:T(8,128)} custom-call(bf16[16,5,128,128]{3,2,1,0:T(8,128)(2,1)} %bitcast.4.in_ref), custom_call_target="tpu_custom_call" | custom-call | bytes 3145728 | tf_op jit(solution)/shard_map/pallas_call | solution.py:320
  (3 shorter events, 0.1 us)
Async XLA Ops:
  0.6 15.4 %collective-permute-start = (bf16[256,256]{1,0:T(8,128)(2,1)}, bf16[256,256]{1,0:T(8,128)(2,1)S(1)}, u32[]{:S(2)}, u32[]{:S(2)}) collective-permute-start(bf16[256,256]{1,0:T(8,128)(2,1)} %t_ref.1), channel_id=1, source_target_pairs={{1,0},{3,2},{5,4},{7,6},{9,8},{11,10},{13,12},{15,14},{17,16},{19,... | collective-permute-start | bytes 393224 | tf_op jit(solution)/shard_map/ppermute | solution.py:242
  9.4 8.3 %collective-permute-start.1 = (bf16[256,256]{1,0:T(8,128)(2,1)}, bf16[256,256]{1,0:T(8,128)(2,1)S(1)}, u32[]{:S(2)}, u32[]{:S(2)}) collective-permute-start(bf16[256,256]{1,0:T(8,128)(2,1)} %t_ref.1), channel_id=1, source_target_pairs={{1,3},{3,5},{5,7},{7,9},{9,11},{11,13},{13,15},{15,17},{17,19},{19... | collective-permute-start | bytes 393224 | tf_op jit(solution)/shard_map/ppermute | solution.py:242
  17.7 0.9 copy-start.2
  18.7 19.5 %collective-permute-start.2 = (bf16[2,256,256]{2,1,0:T(8,128)(2,1)S(1)}, bf16[2,256,256]{2,1,0:T(8,128)(2,1)S(1)}, u32[]{:S(2)}, u32[]{:S(2)}) collective-permute-start(bf16[2,256,256]{2,1,0:T(8,128)(2,1)S(1)} %shard_map.76.a_ref), channel_id=1, source_target_pairs={{0,24},{1,9},{2,26},{3,11},{4,28},{5,13},{6,30},{7,15},{8,0},{9,17... | collective-permute-start | bytes 786440 | tf_op jit(solution)/shard_map/ppermute | solution.py:242
  38.1 46.3 %collective-permute-start.8 = (bf16[16,512,256]{2,1,0:T(8,128)(2,1)S(1)}, bf16[16,512,256]{2,1,0:T(8,128)(2,1)S(1)}, u32[]{:S(2)}, u32[]{:S(2)}) collective-permute-start(bf16[16,512,256]{2,1,0:T(8,128)(2,1)S(1)} %get-tuple-element.36), channel_id=1, source_target_pairs={{0,1},{1,0},{2,3},{3,2},{4,5},{5,4},{6,7},{7,6},{8,9},{9,8},{10,11... | collective-permute-start | bytes 12582920 | tf_op jit(solution)/shard_map/ppermute | solution.py:242
  40.1 15.5 %collective-permute-start.3 = (bf16[4,256,256]{2,1,0:T(8,128)(2,1)S(1)}, bf16[4,256,256]{2,1,0:T(8,128)(2,1)S(1)}, u32[]{:S(2)}, u32[]{:S(2)}) collective-permute-start(bf16[4,256,256]{2,1,0:T(8,128)(2,1)S(1)} %shard_map.78.a_ref), channel_id=1, source_target_pairs={{0,28},{1,5},{2,30},{3,7},{4,0},{5,9},{6,2},{7,11},{8,4},{9,13},{1... | collective-permute-start | bytes 1572872 | tf_op jit(solution)/shard_map/ppermute | solution.py:242
  55.6 4.6 %collective-permute-start.5 = (bf16[8,256,256]{2,1,0:T(8,128)(2,1)S(1)}, bf16[8,256,256]{2,1,0:T(8,128)(2,1)S(1)}, u32[]{:S(2)}, u32[]{:S(2)}) collective-permute-start(bf16[8,256,256]{2,1,0:T(8,128)(2,1)S(1)} %shard_map.79.a_ref), channel_id=1, source_target_pairs={{0,1},{1,0},{2,3},{3,2},{4,5},{5,4},{6,7},{7,6},{8,9},{9,8},{10,11... | collective-permute-start | bytes 3145736 | tf_op jit(solution)/shard_map/ppermute | solution.py:242
  57.6 17.3 %collective-permute-start.4 = (bf16[8,256,256]{2,1,0:T(8,128)(2,1)S(1)}, bf16[8,256,256]{2,1,0:T(8,128)(2,1)S(1)}, u32[]{:S(2)}, u32[]{:S(2)}) collective-permute-start(bf16[8,256,256]{2,1,0:T(8,128)(2,1)S(1)} %shard_map.79.a_ref), channel_id=1, source_target_pairs={{0,30},{1,3},{2,0},{3,5},{4,2},{5,7},{6,4},{7,9},{8,6},{9,11},{10,... | collective-permute-start | bytes 3145736 | tf_op jit(solution)/shard_map/ppermute | solution.py:242
  60.2 19.2 %copy-start.1 = (bf16[256,512]{1,0:T(8,128)(2,1)S(1)}, bf16[256,512]{1,0:T(8,128)(2,1)}, u32[]{:S(2)}) copy-start(bf16[256,512]{1,0:T(8,128)(2,1)} %og_ref.1) | copy-start | bytes 786436
  74.8 4.6 %collective-permute-start.6 = (bf16[8,256,256]{2,1,0:T(8,128)(2,1)S(1)}, bf16[8,256,256]{2,1,0:T(8,128)(2,1)S(1)}, u32[]{:S(2)}, u32[]{:S(2)}) collective-permute-start(bf16[8,256,256]{2,1,0:T(8,128)(2,1)S(1)} %collective-permute-done.4.l_ref), channel_id=1, source_target_pairs={{0,1},{1,0},{2,3},{3,2},{4,5},{5,4},{6,7},{7,6},{8,9},{9,8},{10,11... | collective-permute-start | bytes 3145736 | tf_op jit(solution)/shard_map/ppermute | solution.py:242
  80.9 3.4 %collective-permute-start.7 = (bf16[256,512]{1,0:T(8,128)(2,1)S(1)}, bf16[256,512]{1,0:T(8,128)(2,1)S(1)}, u32[]{:S(2)}, u32[]{:S(2)}) collective-permute-start(bf16[256,512]{1,0:T(8,128)(2,1)S(1)} %get-tuple-element.40.pg_ref), channel_id=1, source_target_pairs={{0,1},{1,0},{2,3},{3,2},{4,5},{5,4},{6,7},{7,6},{8,9},{9,8},{10,11... | collective-permute-start | bytes 786440 | tf_op jit(solution)/shard_map/ppermute | solution.py:242
  85.6 17.1 %collective-permute-start.9 = (bf16[8,256,256]{2,1,0:T(8,128)(2,1)S(1)}, bf16[8,256,256]{2,1,0:T(8,128)(2,1)S(1)}, u32[]{:S(2)}, u32[]{:S(2)}) collective-permute-start(bf16[8,256,256]{2,1,0:T(8,128)(2,1)S(1)} %shard_map.83), channel_id=1, source_target_pairs={{0,2},{1,31},{2,4},{3,1},{4,6},{5,3},{6,8},{7,5},{8,10},{9,7},{10,... | collective-permute-start | bytes 3145736 | tf_op jit(solution)/shard_map/ppermute | solution.py:242
  97.9 1.5 copy-start
  103.6 15.2 %collective-permute-start.10 = (bf16[4,256,256]{2,1,0:T(8,128)(2,1)}, bf16[4,256,256]{2,1,0:T(8,128)(2,1)}, u32[]{:S(2)}, u32[]{:S(2)}) collective-permute-start(bf16[4,256,256]{2,1,0:T(8,128)(2,1)} %shard_map.86), channel_id=1, source_target_pairs={{0,4},{1,29},{2,6},{3,31},{4,8},{5,1},{6,10},{7,3},{8,12},{9,5},{1... | collective-permute-start | bytes 1572872 | tf_op jit(solution)/shard_map/ppermute | solution.py:242
  107.4 46.1 %all-to-all-start = ((bf16[80,128,128]{2,1,0:T(8,128)(2,1)}), bf16[80,128,128]{2,1,0:T(8,128)(2,1)}, u32[]{:S(2)}, u32[]{:S(2)}) async-start(bf16[80,128,128]{2,1,0:T(8,128)(2,1)} %copy-done), calls=%async_computation | async-start | bytes 5242880 | tf_op jit(solution)/shard_map/all_to_all | solution.py:309
  119.9 15.3 %collective-permute-start.11 = (bf16[2,256,256]{2,1,0:T(8,128)(2,1)S(1)}, bf16[2,256,256]{2,1,0:T(8,128)(2,1)S(1)}, u32[]{:S(2)}, u32[]{:S(2)}) collective-permute-start(bf16[2,256,256]{2,1,0:T(8,128)(2,1)S(1)} %shard_map.87), channel_id=1, source_target_pairs={{0,8},{1,25},{2,10},{3,27},{4,12},{5,29},{6,14},{7,31},{8,16},{9,1... | collective-permute-start | bytes 786440 | tf_op jit(solution)/shard_map/ppermute | solution.py:242
  136.4 11.6 %collective-permute-start.12 = (bf16[256,256]{1,0:T(8,128)(2,1)S(1)}, bf16[256,256]{1,0:T(8,128)(2,1)S(1)}, u32[]{:S(2)}, u32[]{:S(2)}) collective-permute-start(bf16[256,256]{1,0:T(8,128)(2,1)S(1)} %get-tuple-element.43), channel_id=1, source_target_pairs={{0,1},{2,3},{4,5},{6,7},{8,9},{10,11},{12,13},{14,15},{16,17},{18,... | collective-permute-start | bytes 393224 | tf_op jit(solution)/shard_map/ppermute | solution.py:242
  144.7 8.1 %collective-permute-start.13 = (bf16[256,256]{1,0:T(8,128)(2,1)S(1)}, bf16[256,256]{1,0:T(8,128)(2,1)S(1)}, u32[]{:S(2)}, u32[]{:S(2)}) collective-permute-start(bf16[256,256]{1,0:T(8,128)(2,1)S(1)} %get-tuple-element.42.same_ref), channel_id=1, source_target_pairs={{3,1},{5,3},{7,5},{9,7},{11,9},{13,11},{15,13},{17,15},{19,17},{21... | collective-permute-start | bytes 393224 | tf_op jit(solution)/shard_map/ppermute | solution.py:242

commit v4 on v3

--- a/solution.py
+++ b/solution.py
@@ -13,6 +13,7 @@
 MIB = 1 << 20
 BF16, F32 = jnp.bfloat16, jnp.float32
 NZ = 16
+JOIN = 80 * 10**9
 
 
 def params(mib):
@@ -37,8 +38,8 @@
     step = lax.rem(dev // 2 - z + NZ, NZ)
     chosen = (step >= NZ // 2).astype(jnp.int32)
     i = jnp.where(step < NZ // 2, step, NZ - 1 - step)
-    order = 4 * lax.rem(i, 2) + i // 4 + 2 * lax.rem(i // 2, 2)
-    return chosen == core, 2 * order + (lax.rem(dev, 2) != chosen).astype(jnp.int32)
+    stream = (lax.rem(dev, 2) != chosen).astype(jnp.int32)
+    return chosen == core, 8 * lax.rem(i, 2) + 4 * stream + i // 4 + 2 * lax.rem(i // 2, 2)
 
 
 def in_hbm(v):
@@ -98,18 +99,29 @@
     lax.fori_loop(0, slots, put, 0)
 
 
-def join_first(t_ref, x_ref, y_ref, out_ref):
+def pair_up(a_ref, b_ref, out_ref):
+    out_ref[0] = a_ref[...]
+    out_ref[1] = b_ref[...]
+
+
+def chosen_base(core_0_ref, core_1_ref, use):
     core = my_place()[1]
 
     @pl.when(core == 0)
     def _():
-        out_ref[0] = t_ref[...]
+        use(core_0_ref)
 
     @pl.when(core != 0)
     def _():
-        out_ref[0] = y_ref[...]
-
-    out_ref[1] = x_ref[...]
+        use(core_1_ref)
+
+
+def join_base(stream, pair_ref, hop_ref, g4_ref, out_ref):
+    def put(ref):
+        out_ref[0] = ref[stream]
+
+    chosen_base(pair_ref, hop_ref, put)
+    out_ref[1] = g4_ref[...]
 
 
 def join(a_ref, b_ref, out_ref):
@@ -127,16 +139,20 @@
     return jnp.dot(x, up_ref[first * feats : (first + len(parts)) * feats], preferred_element_type=F32)
 
 
-def forward_early(a_ref, up_ref, out_ref):
-    out_ref[...] = times(up_ref, 0, a_ref)
-
-
-def forward_late(so_far, l_ref, b_ref, up_ref, out_ref):
-    out_ref[...] = so_far[...] + times(up_ref, 8, l_ref, b_ref)
-
-
-def forward_last(so_far, s_ref, up_ref, og_ref, act_ref, pg_ref):
-    hidden = so_far[...] + times(up_ref, 24, s_ref)
+def forward_early(a_ref, b_ref, up_ref, out_ref):
+    out_ref[...] = times(up_ref, 0, a_ref, b_ref)
+
+
+def forward_next(so_far, la_ref, a_ref, b_ref, up_ref, out_ref):
+    out_ref[...] = so_far[...] + times(up_ref, 8, la_ref) + times(up_ref, 16, a_ref, b_ref)
+
+
+def forward_late(so_far, lb_ref, la_ref, up_ref, out_ref):
+    out_ref[...] = so_far[...] + times(up_ref, 12, lb_ref) + times(up_ref, 24, la_ref)
+
+
+def forward_last(so_far, lb_ref, up_ref, og_ref, act_ref, pg_ref):
+    hidden = so_far[...] + times(up_ref, 28, lb_ref)
     sig = jax.nn.sigmoid(hidden)
     act_ref[...] = (hidden * sig).astype(BF16)
     pg_ref[...] = (og_ref[...].astype(F32) * sig * (1.0 + hidden * (1.0 - sig))).astype(BF16)
@@ -155,42 +171,44 @@
 
 
 def add_first(d_ref, r1_ref, out_ref):
-    for n in range(4):
-        out_ref[n] = (d_ref[4 + n] + f32(r1_ref[4 + n])).astype(BF16)
+    for n in range(2):
+        out_ref[n] = (d_ref[2 + n] + f32(r1_ref[2 + n])).astype(BF16)
 
 
 def add_second(d_ref, r1_ref, r2_ref, out_ref):
-    for n in range(2):
-        out_ref[n] = (d_ref[2 + n] + f32(r1_ref[2 + n]) + f32(r2_ref[2 + n])).astype(BF16)
-
-
-def add_third(d_ref, r1_ref, r2_ref, r3_ref, same_ref, cross_ref):
-    for n, out_ref in enumerate((same_ref, cross_ref)):
-        out_ref[...] = (d_ref[n] + f32(r1_ref[n]) + f32(r2_ref[n]) + f32(r3_ref[n])).astype(BF16)
-
-
-def add_last(same_ref, cross_ref, moved_ref, out_ref):
-    core = my_place()[1]
-
-    @pl.when(core == 0)
-    def _():
-        out_ref[...] = (f32(same_ref[...]) + f32(cross_ref[...])).astype(BF16)
-
-    @pl.when(core != 0)
-    def _():
-        out_ref[...] = (f32(moved_ref[...]) + f32(cross_ref[...])).astype(BF16)
-
-
-def weight_terms(listed_hbm, pg_ref, a_ref, l_ref, b_ref, s_ref, out_ref, listed, flipped, dense, sem):
+    out_ref[...] = (d_ref[1] + f32(r1_ref[1]) + f32(r2_ref[1])).astype(BF16)
+
+
+def add_base(da_ref, r1a_ref, r2a_ref, db_ref, r1b_ref, r2b_ref, out_ref):
+    out_ref[0] = (da_ref[0] + f32(r1a_ref[0]) + f32(r2a_ref[0])).astype(BF16)
+    out_ref[1] = (db_ref[0] + f32(r1b_ref[0]) + f32(r2b_ref[0])).astype(BF16)
+
+
+def add_cross(base_ref, hop_ref, r3b_ref, out_ref):
+    def put(ref):
+        out_ref[...] = (f32(ref[1]) + f32(r3b_ref[...])).astype(BF16)
+
+    chosen_base(base_ref, hop_ref, put)
+
+
+def add_last(base_ref, hop_ref, r3a_ref, cross_ref, out_ref):
+    def put(ref):
+        out_ref[...] = (f32(ref[0]) + f32(r3a_ref[...]) + f32(cross_ref[...])).astype(BF16)
+
+    chosen_base(base_ref, hop_ref, put)
+
+
+def weight_terms(listed_hbm, pg_ref, *refs):
+    x_refs, (out_ref, listed, flipped, dense, sem) = refs[:8], refs[8:]
     fetch = pltpu.make_async_copy(listed_hbm, listed, sem)
     fetch.start()
     slots, blk = out_ref.shape[0], out_ref.shape[1]
     rows_per_dev = dense.shape[2] // blk
     me = my_place()
     flipped[...] = pg_ref[...].T
-    for m, ref in enumerate((a_ref, l_ref, b_ref, s_ref)):
+    for m, ref in enumerate(x_refs):
         for n in range(ref.shape[0]):
-            dense[8 * m + n] = jnp.dot(flipped[...], ref[n], preferred_element_type=F32).astype(BF16)
+            dense[4 * m + n] = jnp.dot(flipped[...], ref[n], preferred_element_type=F32).astype(BF16)
 
     fetch.wait()
 
@@ -244,8 +262,12 @@
     def other_core(v):
         return send(v, [(n, n ^ 1) for n in range(2 * NZ)])
 
-    def steps(v, d):
-        return send(v, [(2 * z + c, 2 * ((z + (d, -d)[c]) % NZ) + c) for z in around for c in range(2)])
+    def steps(v, d, d1=None):
+        by = (d, -(d if d1 is None else d1))
+        return send(v, [(2 * z + c, 2 * ((z + by[c]) % NZ) + c) for z in around for c in range(2)])
+
+    def hop(v, d):
+        return send(v, [(2 * z + 1, 2 * ((z + d) % NZ) + 1) for z in around])
 
     def flops_of(shards):
         return 2 * shards * tok_rows * feats * width
@@ -253,13 +275,12 @@
     def shards(n, dtype=BF16):
         return shape(n, tok_rows, feats, dtype=dtype)
 
-    cross_pairs = [(2 * z + 1, 2 * z) for z in around] + [(2 * z, 2 * ((z + 1) % NZ) + 1) for z in around]
-    along_pairs = [(2 * z + 1, 2 * ((z + 1) % NZ) + 1) for z in around]
-
-    crossed, along = send(tokens, cross_pairs), send(tokens, along_pairs)
-    g0 = kernel(join_first, shards(2), n_in=3)(tokens, crossed, along)
-    g0, listed = together((g0, listed))
-    g4 = steps(g0, -4)
+    g4a = steps(tokens, -4, -5)
+    theirs = other_core(tokens)
+    g4b = steps(theirs, -4, -5)
+    pair = kernel(pair_up, shards(2), n_in=2)(tokens, theirs)
+    pair, listed = together((pair, listed))
+    base = hop(pair, 1)
     up_w, down_w, down_other = kernel(
         lay_weights,
         (shape(2 * NZ * feats, width),) + (shape(NZ, width, feats),) * 2,
@@ -269,57 +290,98 @@
             pltpu.VMEM((slots, blk, blk), BF16), pltpu.SemaphoreType.DMA((3,)),
         ],
     )(in_hbm(listed), in_hbm(cut), in_hbm(up_blocks[0]))
-    g4, up_w, down_other = together((g4, up_w, down_other))
+    g4a, up_w = together((g4a, up_w))
     down_sibling = other_core(down_other)
 
-    g04 = kernel(join, shards(4), n_in=2)(g0, g4)
-    early = kernel(join, shards(8), n_in=2)(g04, steps(g04, -2))
-    late = steps(early, -1)
+    def based(n, g):
+        return kernel(functools.partial(join_base, n), shards(2), n_in=3, flops=n * JOIN, size=0)(pair, base, g)
+
+    g04a = based(0, g4a)
+    g26a = steps(g04a, -2)
+    g4b, g04a = together((g4b, g04a))
+    g04b = based(1, g4b)
+    g26b = steps(g04b, -2)
+    g26a, g04b = together((g26a, g04b))
+    ea = kernel(join, shards(4), n_in=2, size=0)(g04a, g26a)
+    la = steps(ea, -1)
+    g26b, ea, down_sibling = together((g26b, ea, down_sibling))
+    eb = kernel(join, shards(4), n_in=2, flops=JOIN, size=0)(g04b, g26b)
+    lb = steps(eb, -1)
+    la, ea, eb = together((la, ea, eb))
+    ea2, eb2 = other_core(ea), other_core(eb)
+
     hidden_shape = shape(tok_rows, width, dtype=F32)
-    hidden = kernel(forward_early, hidden_shape, n_in=2, flops=flops_of(8), size=4 * MIB)(early, up_w)
-    early_other = other_core(early)
-    late, hidden, early_other = together((late, hidden, early_other))
-    late_other = other_core(late)
-    hidden = kernel(forward_late, hidden_shape, n_in=4, flops=flops_of(16), size=6 * MIB)(
-        hidden, late, early_other, up_w
-    )
-    act, pg = kernel(forward_last, (shape(tok_rows, width),) * 2, n_in=4, flops=flops_of(8), size=4 * MIB)(
-        hidden, late_other, up_w, out_grad
+
+    def more(body, *operands):
+        return kernel(body, hidden_shape, n_in=len(operands), size=0)(*operands)
+
+    hidden = more(forward_early, ea, eb, up_w)
+    la2 = other_core(la)
+    hidden = more(forward_next, hidden, la, ea2, eb2, up_w)
+    lb2 = other_core(lb)
+    hidden = more(forward_late, hidden, lb, la2, up_w)
+    act, pg = kernel(forward_last, (shape(tok_rows, width),) * 2, n_in=4, flops=flops_of(4), size=4 * MIB)(
+        hidden, lb2, up_w, out_grad
     )
     pg2 = other_core(pg)
 
-    d1 = kernel(functools.partial(back, 8), shards(8), n_in=4, flops=flops_of(16), size=6 * MIB)(
-        pg, pg2, down_w, down_sibling
-    )
-    pg_after, d1 = together((pg, d1))
-    r1 = steps(d1, 1)
-    d2 = kernel(functools.partial(back, 0), shards(8, F32), n_in=4, flops=flops_of(16), size=6 * MIB)(
-        pg, pg2, down_w, down_sibling
-    )
-    pg_after, d2 = together((pg_after, d2))
+    def back_of(first, dtype):
+        return kernel(functools.partial(back, first), shards(4, dtype), n_in=4, flops=flops_of(8), size=4 * MIB)(
+            pg, pg2, down_w, down_sibling
+        )
+
+    d1b = back_of(12, BF16)
+    r1b = steps(d1b, 1)
+    pg, d1b = together((pg, d1b))
+    d1a = back_of(8, BF16)
+    r1a = steps(d1a, 1)
+    pg, d1a = together((pg, d1a))
+    d2b, d2a = back_of(4, F32), back_of(0, F32)
+    pg_after, d2b, d2a = together((pg, d2b, d2a))
     terms = kernel(
-        weight_terms, shape(slots, blk, blk), ins=[HBM], n_in=5, mib=14,
+        weight_terms, shape(slots, blk, blk), ins=[HBM], n_in=9, mib=14,
         flops=flops_of(32), size=16 * MIB,
         scratch=[
             pltpu.SMEM(listed.shape, jnp.int32), pltpu.VMEM((width, tok_rows), BF16),
             pltpu.VMEM((2 * NZ, width, feats), BF16), pltpu.SemaphoreType.DMA,
         ],
-    )(in_hbm(listed), pg_after, early, late, early_other, late_other)
-    r1, terms = together((r1, terms))
+    )(in_hbm(listed), pg_after, ea, eb, la, lb, ea2, eb2, la2, lb2)
+    r1b, terms = together((r1b, terms))
+
+    def in_turn(body, out, turn, *operands, flops=0):
+        n = len(operands)
+
+        def ordered(*refs):
+            body(*refs[:n], refs[n + 1])
+            refs[n + 2][...] = refs[n][...]
+
+        return kernel(ordered, (out, shape(8, blk, dtype=F32)), n_in=n + 1, flops=flops)(*operands, turn)
+
+    one = shape(tok_rows, feats)
+    turn = jnp.zeros((8, blk), F32)
+    q, turn = in_turn(add_first, shards(2), turn, d2b, r1b)
+    r2b = steps(q, 2)
+    r1a, turn = together((r1a, turn))
+    q, turn = in_turn(add_first, shards(2), turn, d2a, r1a)
+    r2a = steps(q, 2)
+    terms, turn = together((terms, turn))
     got = lax.all_to_all(terms, "dp", 0, 0, tiled=True)
-    q26 = kernel(add_first, shards(4), n_in=2)(d2, r1)
-    r2 = steps(q26, 2)
-    q4 = kernel(add_second, shards(2), n_in=3, flops=10**11)(d2, r1, r2)
-    r3 = steps(q4, 4)
-    one = shape(tok_rows, feats)
-    same, cross = kernel(add_third, (one, one), n_in=4)(d2, r1, r2, r3)
-    crossed = send(cross, [(b, a) for a, b in cross_pairs])
-    moved = send(same, [(b, a) for a, b in along_pairs])
-    in_grad = kernel(add_last, one, n_in=3)(same, crossed, moved)
-
+    r2b, turn = together((r2b, turn))
+    q, turn = in_turn(add_second, one, turn, d2b, r1b, r2b, flops=10**11)
+    r3b = steps(q, 4, 5)
+    r2a, turn = together((r2a, turn))
+    q, turn = in_turn(add_second, one, turn, d2a, r1a, r2a)
+    r3a = steps(q, 4, 5)
+    sums = kernel(add_base, shards(2), n_in=6, size=0)(d2a, r1a, r2a, d2b, r1b, r2b)
+    moved = hop(sums, -1)
     own_grads = kernel(
         functools.partial(add_terms, 1.0 / (tok_rows * n_dp) ** 0.5), shape(per, blk, blk, dtype=F32), size=3 * MIB
     )(got.reshape(n_dp, per, blk, blk))
+    r3b, r3a, turn = together((r3b, r3a, turn))
+    q, turn = in_turn(add_cross, one, turn, sums, moved, r3b)
+    cross = other_core(q)
+    cross, own_grads, turn = together((cross, own_grads, turn))
+    in_grad, _ = in_turn(add_last, one, turn, sums, moved, r3a, cross)
     return act, in_grad, own_grads[None]
 
 

time: 157 us -> 150 us (0.955)
  waiting for transfers between devices: 69.9 us -> 26.4 us
  starting transfers between devices: 57.9 us -> 89.3 us
  Pallas kernels: 25.4 us -> 28.2 us
    ppermute x14 -> x22, waiting for transfers between devices: 69.9 us -> 22.4 us  [send(): return lax.ppermute(v, 'blk', pairs)]
    ppermute x14 -> x22, starting transfers between devices: 51.4 us -> 82.5 us  [send(): return lax.ppermute(v, 'blk', pairs)]
    all_to_all x1, waiting for transfers between devices: 0.01 us -> 3.99 us  [on_device(): got = lax.all_to_all(terms, 'dp', 0, 0, tiled=True)]
    pallas_call x12 -> x20, Pallas kernels: 14.1 us -> 16.2 us  [the longest x1 5.63 us: on_device(): kernel(weight_terms, shape(slots, blk, blk), ins=[HBM], n_in=9, mib=14, f...]
    unnamed x6 -> x8, local copies, waits for them, and re-layouts: 2.4 us -> 3.35 us
  transfers between devices with their start and end apart: 15 -> 23, of which waited for: 12 -> 9; matrix products, arithmetic and copies ran while one was open for 0% -> 0% of each run, Pallas kernels for 13% -> 17%
where the time goes in v4:
time: 150 us; the launch traced here: 148 us
  starting transfers between devices  89.3 us (60%)
  Pallas kernels  28.2 us (19%)
  waiting for transfers between devices  26.4 us (18%)
  local copies, waits for them, and re-layouts  3.35 us (2%)
    ppermute x22, starting transfers between devices, send(): return lax.ppermute(v, 'blk', pairs)  82.5 us
    ppermute x22, waiting for transfers between devices, send(): return lax.ppermute(v, 'blk', pairs)  22.4 us
    pallas_call x1, Pallas kernels, on_device(): kernel(lay_weights, (shape(2 * NZ * feats, width),) + (shape(NZ, width, f...  7.86 us
    all_to_all x1, starting transfers between devices, on_device(): got = lax.all_to_all(terms, 'dp', 0, 0, tiled=True)  6.81 us
    pallas_call x1, Pallas kernels, on_device(): kernel(weight_terms, shape(slots, blk, blk), ins=[HBM], n_in=9, mib=14, f...  5.63 us
    all_to_all x1, waiting for transfers between devices, on_device(): got = lax.all_to_all(terms, 'dp', 0, 0, tiled=True)  3.99 us
    unnamed x8, local copies, waits for them, and re-layouts  3.35 us
    pallas_call x6, Pallas kernels, in_turn(): kernel(ordered, (out, shape(8, blk, dtype=F32)), n_in=n + 1, flops=flops)  3.28 us
  transfers between devices with their start and end apart: 23, of which 9 were waited for; matrix products, arithmetic and copies ran while one was open for 0% of the time, Pallas kernels for 17%

profile of v4, /device:TPU:1, one launch (start us, length us, event | category | flops | bytes accessed | tf_op | source)
XLA Modules:
  0.0 148.3 jit_solution(2350131779535929864)
XLA Ops:
  0.6 8.8 %collective-permute-start = (bf16[256,256]{1,0:T(8,128)(2,1)}, bf16[256,256]{1,0:T(8,128)(2,1)S(1)}, u32[]{:S(2)}, u32[]{:S(2)}) collective-permute-start(bf16[256,256]{1,0:T(8,128)(2,1)} %a_ref.1), channel_id=1, source_target_pairs={{0,1},{1,0},{2,3},{3,2},{4,5},{5,4},{6,7},{7,6},{8,9},{9,8},{10,11... | collective-permute-start | bytes 393224 | tf_op jit(solution)/shard_map/ppermute | solution.py:260
  9.4 1.2 collective-permute-done.b_ref
  10.6 0.9 shard_map.76.pair_ref
  11.5 1.9 %collective-permute-start.2 = (bf16[2,256,256]{2,1,0:T(8,128)(2,1)S(1)}, bf16[2,256,256]{2,1,0:T(8,128)(2,1)S(1)}, u32[]{:S(2)}, u32[]{:S(2)}) collective-permute-start(bf16[2,256,256]{2,1,0:T(8,128)(2,1)S(1)} %shard_map.76.pair_ref), channel_id=1, source_target_pairs={{1,3},{3,5},{5,7},{7,9},{9,11},{11,13},{13,15},{15,17},{17,19},{19... | collective-permute-start | bytes 786440 | tf_op jit(solution)/shard_map/ppermute | solution.py:260
  13.5 6.4 %collective-permute-start.3 = (bf16[256,256]{1,0:T(8,128)(2,1)}, bf16[256,256]{1,0:T(8,128)(2,1)S(1)}, u32[]{:S(2)}, u32[]{:S(2)}) collective-permute-start(bf16[256,256]{1,0:T(8,128)(2,1)} %a_ref.1), channel_id=1, source_target_pairs={{0,24},{1,11},{2,26},{3,13},{4,28},{5,15},{6,30},{7,17},{8,0},{9,1... | collective-permute-start | bytes 393224 | tf_op jit(solution)/shard_map/ppermute | solution.py:260
  19.9 7.5 %collective-permute-start.1 = (bf16[256,256]{1,0:T(8,128)(2,1)S(1)}, bf16[256,256]{1,0:T(8,128)(2,1)S(1)}, u32[]{:S(2)}, u32[]{:S(2)}) collective-permute-start(bf16[256,256]{1,0:T(8,128)(2,1)S(1)} %collective-permute-done.b_ref), channel_id=1, source_target_pairs={{0,24},{1,11},{2,26},{3,13},{4,28},{5,15},{6,30},{7,17},{8,0},{9,1... | collective-permute-start | bytes 393224 | tf_op jit(solution)/shard_map/ppermute | solution.py:260
  27.4 7.9 %shard_map.77 = (bf16[8192,512]{1,0:T(8,128)(2,1)S(1)}, bf16[16,512,256]{2,1,0:T(8,128)(2,1)S(1)}, bf16[16,512,256]{2,1,0:T(8,128)(2,1)S(1)}) custom-call(s32[2,80]{1,0:T(2,128)} %bitcast.10, s32[2,32]{1,0:T(2,128)} %bitcast.9, bf16[80,128,128]{2,1,0:T(8,128)(2,1)} %bitcast.7), custom_call_target="tpu_custom_call" | custom-call | bytes 20971520 | tf_op jit(solution)/shard_map/pallas_call | solution.py:284
  35.3 1.9 %collective-permute-start.7 = (bf16[16,512,256]{2,1,0:T(8,128)(2,1)S(1)}, bf16[16,512,256]{2,1,0:T(8,128)(2,1)S(1)}, u32[]{:S(2)}, u32[]{:S(2)}) collective-permute-start(bf16[16,512,256]{2,1,0:T(8,128)(2,1)S(1)} %get-tuple-element.61), channel_id=1, source_target_pairs={{0,1},{1,0},{2,3},{3,2},{4,5},{5,4},{6,7},{7,6},{8,9},{9,8},{10,11... | collective-permute-start | bytes 12582920 | tf_op jit(solution)/shard_map/ppermute | solution.py:260
  37.2 4.1 %collective-permute-start.4 = (bf16[2,256,256]{2,1,0:T(8,128)(2,1)S(1)}, bf16[2,256,256]{2,1,0:T(8,128)(2,1)S(1)}, u32[]{:S(2)}, u32[]{:S(2)}) collective-permute-start(bf16[2,256,256]{2,1,0:T(8,128)(2,1)S(1)} %shard_map.78.a_ref), channel_id=1, source_target_pairs={{0,28},{1,5},{2,30},{3,7},{4,0},{5,9},{6,2},{7,11},{8,4},{9,13},{1... | collective-permute-start | bytes 786440 | tf_op jit(solution)/shard_map/ppermute | solution.py:260
  41.4 1.9 %collective-permute-start.6 = (bf16[2,256,256]{2,1,0:T(8,128)(2,1)S(1)}, bf16[2,256,256]{2,1,0:T(8,128)(2,1)S(1)}, u32[]{:S(2)}, u32[]{:S(2)}) collective-permute-start(bf16[2,256,256]{2,1,0:T(8,128)(2,1)S(1)} %shard_map.79.a_ref), channel_id=1, source_target_pairs={{0,28},{1,5},{2,30},{3,7},{4,0},{5,9},{6,2},{7,11},{8,4},{9,13},{1... | collective-permute-start | bytes 786440 | tf_op jit(solution)/shard_map/ppermute | solution.py:260
  43.3 4.2 %collective-permute-done.4.b_ref = bf16[2,256,256]{2,1,0:T(8,128)(2,1)S(1)} collective-permute-done((bf16[2,256,256]{2,1,0:T(8,128)(2,1)S(1)}, bf16[2,256,256]{2,1,0:T(8,128)(2,1)S(1)}, u32[]{:S(2)}, u32[]{:S(2)}) %collective-permute-start.4) | collective-permute-done | bytes 262176 | tf_op jit(solution)/shard_map/ppermute | solution.py:260
  47.5 4.7 %collective-permute-start.5 = (bf16[4,256,256]{2,1,0:T(8,128)(2,1)S(1)}, bf16[4,256,256]{2,1,0:T(8,128)(2,1)S(1)}, u32[]{:S(2)}, u32[]{:S(2)}) collective-permute-start(bf16[4,256,256]{2,1,0:T(8,128)(2,1)S(1)} %shard_map.80.a_ref.refs_0_), channel_id=1, source_target_pairs={{0,30},{1,3},{2,0},{3,5},{4,2},{5,7},{6,4},{7,9},{8,6},{9,11},{10,... | collective-permute-start | bytes 1572872 | tf_op jit(solution)/shard_map/ppermute | solution.py:260
  52.3 1.0 collective-permute-done.6.b_ref
  53.3 3.4 %collective-permute-start.10 = (bf16[4,256,256]{2,1,0:T(8,128)(2,1)S(1)}, bf16[4,256,256]{2,1,0:T(8,128)(2,1)S(1)}, u32[]{:S(2)}, u32[]{:S(2)}) collective-permute-start(bf16[4,256,256]{2,1,0:T(8,128)(2,1)S(1)} %shard_map.81.b_ref.refs_1_), channel_id=1, source_target_pairs={{0,30},{1,3},{2,0},{3,5},{4,2},{5,7},{6,4},{7,9},{8,6},{9,11},{10,... | collective-permute-start | bytes 1572872 | tf_op jit(solution)/shard_map/ppermute | solution.py:260
  56.7 3.1 %collective-permute-done.5.la_ref.refs_2_ = bf16[4,256,256]{2,1,0:T(8,128)(2,1)S(1)} collective-permute-done((bf16[4,256,256]{2,1,0:T(8,128)(2,1)S(1)}, bf16[4,256,256]{2,1,0:T(8,128)(2,1)S(1)}, u32[]{:S(2)}, u32[]{:S(2)}) %collective-permute-start.5) | collective-permute-done | bytes 524320 | tf_op jit(solution)/shard_map/ppermute | solution.py:260
  59.8 5.4 %collective-permute-start.8 = (bf16[4,256,256]{2,1,0:T(8,128)(2,1)S(1)}, bf16[4,256,256]{2,1,0:T(8,128)(2,1)S(1)}, u32[]{:S(2)}, u32[]{:S(2)}) collective-permute-start(bf16[4,256,256]{2,1,0:T(8,128)(2,1)S(1)} %shard_map.80.a_ref.refs_0_), channel_id=1, source_target_pairs={{0,1},{1,0},{2,3},{3,2},{4,5},{5,4},{6,7},{7,6},{8,9},{9,8},{10,11... | collective-permute-start | bytes 1572872 | tf_op jit(solution)/shard_map/ppermute | solution.py:260
  65.2 1.9 %collective-permute-start.9 = (bf16[4,256,256]{2,1,0:T(8,128)(2,1)S(1)}, bf16[4,256,256]{2,1,0:T(8,128)(2,1)S(1)}, u32[]{:S(2)}, u32[]{:S(2)}) collective-permute-start(bf16[4,256,256]{2,1,0:T(8,128)(2,1)S(1)} %shard_map.81.b_ref.refs_1_), channel_id=1, source_target_pairs={{0,1},{1,0},{2,3},{3,2},{4,5},{5,4},{6,7},{7,6},{8,9},{9,8},{10,11... | collective-permute-start | bytes 1572872 | tf_op jit(solution)/shard_map/ppermute | solution.py:260
  67.2 2.4 %collective-permute-start.11 = (bf16[4,256,256]{2,1,0:T(8,128)(2,1)S(1)}, bf16[4,256,256]{2,1,0:T(8,128)(2,1)S(1)}, u32[]{:S(2)}, u32[]{:S(2)}) collective-permute-start(bf16[4,256,256]{2,1,0:T(8,128)(2,1)S(1)} %collective-permute-done.5.la_ref.refs_2_), channel_id=1, source_target_pairs={{0,1},{1,0},{2,3},{3,2},{4,5},{5,4},{6,7},{7,6},{8,9},{9,8},{10,11... | collective-permute-start | bytes 1572872 | tf_op jit(solution)/shard_map/ppermute | solution.py:260
  69.6 1.9 %collective-permute-start.12 = (bf16[4,256,256]{2,1,0:T(8,128)(2,1)S(1)}, bf16[4,256,256]{2,1,0:T(8,128)(2,1)S(1)}, u32[]{:S(2)}, u32[]{:S(2)}) collective-permute-start(bf16[4,256,256]{2,1,0:T(8,128)(2,1)S(1)} %collective-permute-done.10.lb_ref.refs_3_), channel_id=1, source_target_pairs={{0,1},{1,0},{2,3},{3,2},{4,5},{5,4},{6,7},{7,6},{8,9},{9,8},{10,11... | collective-permute-start | bytes 1572872 | tf_op jit(solution)/shard_map/ppermute | solution.py:260
  72.2 1.0 shard_map.83.so_far
  74.2 1.3 shard_map.85
  75.4 2.4 %collective-permute-start.13 = (bf16[256,512]{1,0:T(8,128)(2,1)S(1)}, bf16[256,512]{1,0:T(8,128)(2,1)S(1)}, u32[]{:S(2)}, u32[]{:S(2)}) collective-permute-start(bf16[256,512]{1,0:T(8,128)(2,1)S(1)} %get-tuple-element.77.pg_ref), channel_id=1, source_target_pairs={{0,1},{1,0},{2,3},{3,2},{4,5},{5,4},{6,7},{7,6},{8,9},{9,8},{10,11... | collective-permute-start | bytes 786440 | tf_op jit(solution)/shard_map/ppermute | solution.py:260
  77.8 1.1 collective-permute-done.13.pg2_ref
  79.0 0.7 shard_map.86
  79.7 5.3 %collective-permute-start.15 = (bf16[4,256,256]{2,1,0:T(8,128)(2,1)S(1)}, bf16[4,256,256]{2,1,0:T(8,128)(2,1)S(1)}, u32[]{:S(2)}, u32[]{:S(2)}) collective-permute-start(bf16[4,256,256]{2,1,0:T(8,128)(2,1)S(1)} %shard_map.86), channel_id=1, source_target_pairs={{0,2},{1,31},{2,4},{3,1},{4,6},{5,3},{6,8},{7,5},{8,10},{9,7},{10,... | collective-permute-start | bytes 1572872 | tf_op jit(solution)/shard_map/ppermute | solution.py:260
  85.0 0.7 shard_map.87
  85.7 1.9 %collective-permute-start.14 = (bf16[4,256,256]{2,1,0:T(8,128)(2,1)S(1)}, bf16[4,256,256]{2,1,0:T(8,128)(2,1)S(1)}, u32[]{:S(2)}, u32[]{:S(2)}) collective-permute-start(bf16[4,256,256]{2,1,0:T(8,128)(2,1)S(1)} %shard_map.87), channel_id=1, source_target_pairs={{0,2},{1,31},{2,4},{3,1},{4,6},{5,3},{6,8},{7,5},{8,10},{9,7},{10,... | collective-permute-start | bytes 1572872 | tf_op jit(solution)/shard_map/ppermute | solution.py:260
  88.4 0.7 shard_map.88.refs_0_.db_ref
  89.1 5.6 %shard_map.90 = bf16[80,128,128]{2,1,0:T(8,128)(2,1)S(1)} custom-call(s32[2,80]{1,0:T(2,128)} %bitcast.11, bf16[256,512]{1,0:T(8,128)(2,1)S(1)} %get-tuple-element.77.pg_ref, bf16[4,256,256]{2,1,0:T(8,128)(2,1)S(1)} %shard_map.80.a_ref.refs_0_, bf16[4,256,256]{2,1,0:T(8,128)(2,1)S(1)} %shard_map.81.b_ref.refs_1_, ...), custom_call_target="tpu_custom_call" | custom-call | flops 2147483648 | bytes 16777216 | tf_op jit(solution)/shard_map/pallas_call | solution.py:341
  94.7 1.5 copy-done
  96.2 0.7 shard_map.91
  97.0 1.9 %collective-permute-start.17 = (bf16[2,256,256]{2,1,0:T(8,128)(2,1)}, bf16[2,256,256]{2,1,0:T(8,128)(2,1)}, u32[]{:S(2)}, u32[]{:S(2)}) collective-permute-start(bf16[2,256,256]{2,1,0:T(8,128)(2,1)} %get-tuple-element.83), channel_id=1, source_target_pairs={{0,4},{1,29},{2,6},{3,31},{4,8},{5,1},{6,10},{7,3},{8,12},{9,5},{1... | collective-permute-start | bytes 786440 | tf_op jit(solution)/shard_map/ppermute | solution.py:260
  98.9 0.7 shard_map.92
  99.7 1.9 %collective-permute-start.16 = (bf16[2,256,256]{2,1,0:T(8,128)(2,1)}, bf16[2,256,256]{2,1,0:T(8,128)(2,1)S(1)}, u32[]{:S(2)}, u32[]{:S(2)}) collective-permute-start(bf16[2,256,256]{2,1,0:T(8,128)(2,1)} %get-tuple-element.82), channel_id=1, source_target_pairs={{0,4},{1,29},{2,6},{3,31},{4,8},{5,1},{6,10},{7,3},{8,12},{9,5},{1... | collective-permute-start | bytes 786440 | tf_op jit(solution)/shard_map/ppermute | solution.py:260
  101.6 6.8 %all-to-all-start = ((bf16[80,128,128]{2,1,0:T(8,128)(2,1)}), bf16[80,128,128]{2,1,0:T(8,128)(2,1)}, u32[]{:S(2)}, u32[]{:S(2)}) async-start(bf16[80,128,128]{2,1,0:T(8,128)(2,1)} %copy-done), calls=%async_computation | async-start | bytes 5242880 | tf_op jit(solution)/shard_map/all_to_all | solution.py:368
  108.4 1.0 shard_map.93
  109.4 2.2 %collective-permute-done.16.r2a_ref.refs_2_ = bf16[2,256,256]{2,1,0:T(8,128)(2,1)S(1)} collective-permute-done((bf16[2,256,256]{2,1,0:T(8,128)(2,1)}, bf16[2,256,256]{2,1,0:T(8,128)(2,1)S(1)}, u32[]{:S(2)}, u32[]{:S(2)}) %collective-permute-start.16) | collective-permute-done | bytes 262176 | tf_op jit(solution)/shard_map/ppermute | solution.py:260
  112.3 0.9 copy-done.2
  113.2 1.0 shard_map.94.refs_0_
  114.2 5.9 %collective-permute-start.18 = (bf16[2,256,256]{2,1,0:T(8,128)(2,1)S(1)}, bf16[2,256,256]{2,1,0:T(8,128)(2,1)S(1)}, u32[]{:S(2)}, u32[]{:S(2)}) collective-permute-start(bf16[2,256,256]{2,1,0:T(8,128)(2,1)S(1)} %shard_map.94.refs_0_), channel_id=1, source_target_pairs={{1,31},{3,1},{5,3},{7,5},{9,7},{11,9},{13,11},{15,13},{17,15},{19,... | collective-permute-start | bytes 786440 | tf_op jit(solution)/shard_map/ppermute | solution.py:260
  120.2 4.0 %collective-permute-start.20 = (bf16[256,256]{1,0:T(8,128)(2,1)S(1)}, bf16[256,256]{1,0:T(8,128)(2,1)S(1)}, u32[]{:S(2)}, u32[]{:S(2)}) collective-permute-start(bf16[256,256]{1,0:T(8,128)(2,1)S(1)} %get-tuple-element.93), channel_id=1, source_target_pairs={{0,8},{1,23},{2,10},{3,25},{4,12},{5,27},{6,14},{7,29},{8,16},{9,3... | collective-permute-start | bytes 393224 | tf_op jit(solution)/shard_map/ppermute | solution.py:260
  124.2 4.9 %collective-permute-start.19 = (bf16[256,256]{1,0:T(8,128)(2,1)S(1)}, bf16[256,256]{1,0:T(8,128)(2,1)S(1)}, u32[]{:S(2)}, u32[]{:S(2)}) collective-permute-start(bf16[256,256]{1,0:T(8,128)(2,1)S(1)} %get-tuple-element.91), channel_id=1, source_target_pairs={{0,8},{1,23},{2,10},{3,25},{4,12},{5,27},{6,14},{7,29},{8,16},{9,3... | collective-permute-start | bytes 393224 | tf_op jit(solution)/shard_map/ppermute | solution.py:260
  129.2 5.1 %collective-permute-done.20.refs_2_ = bf16[256,256]{1,0:T(8,128)(2,1)S(1)} collective-permute-done((bf16[256,256]{1,0:T(8,128)(2,1)S(1)}, bf16[256,256]{1,0:T(8,128)(2,1)S(1)}, u32[]{:S(2)}, u32[]{:S(2)}) %collective-permute-start.20) | collective-permute-done | bytes 131104 | tf_op jit(solution)/shard_map/ppermute | solution.py:260
  134.3 4.5 %collective-permute-done.19.refs_2_ = bf16[256,256]{1,0:T(8,128)(2,1)S(1)} collective-permute-done((bf16[256,256]{1,0:T(8,128)(2,1)S(1)}, bf16[256,256]{1,0:T(8,128)(2,1)S(1)}, u32[]{:S(2)}, u32[]{:S(2)}) %collective-permute-start.19) | collective-permute-done | bytes 131104 | tf_op jit(solution)/shard_map/ppermute | solution.py:260
  138.8 1.9 %collective-permute-start.21 = (bf16[256,256]{1,0:T(8,128)(2,1)S(1)}, bf16[256,256]{1,0:T(8,128)(2,1)S(1)}, u32[]{:S(2)}, u32[]{:S(2)}) collective-permute-start(bf16[256,256]{1,0:T(8,128)(2,1)S(1)} %get-tuple-element.98), channel_id=1, source_target_pairs={{0,1},{1,0},{2,3},{3,2},{4,5},{5,4},{6,7},{7,6},{8,9},{9,8},{10,11... | collective-permute-start | bytes 393224 | tf_op jit(solution)/shard_map/ppermute | solution.py:260
  140.7 4.0 %all-to-all-done = bf16[80,128,128]{2,1,0:T(8,128)(2,1)} async-done(((bf16[80,128,128]{2,1,0:T(8,128)(2,1)}), bf16[80,128,128]{2,1,0:T(8,128)(2,1)}, u32[]{:S(2)}, u32[]{:S(2)}) %all-to-all-start) | async-done | bytes 2621472 | tf_op jit(solution)/shard_map/all_to_all | solution.py:368
  144.7 2.9 %shard_map.97 = f32[5,128,128]{2,1,0:T(8,128)} custom-call(bf16[16,5,128,128]{3,2,1,0:T(8,128)(2,1)} %bitcast.4.in_ref), custom_call_target="tpu_custom_call" | custom-call | bytes 3145728 | tf_op jit(solution)/shard_map/pallas_call | solution.py:377
  147.6 0.7 shard_map.98
  (30 shorter events, 3.3 us)
Async XLA Ops:
  0.6 10.0 %collective-permute-start = (bf16[256,256]{1,0:T(8,128)(2,1)}, bf16[256,256]{1,0:T(8,128)(2,1)S(1)}, u32[]{:S(2)}, u32[]{:S(2)}) collective-permute-start(bf16[256,256]{1,0:T(8,128)(2,1)} %a_ref.1), channel_id=1, source_target_pairs={{0,1},{1,0},{2,3},{3,2},{4,5},{5,4},{6,7},{7,6},{8,9},{9,8},{10,11... | collective-permute-start | bytes 393224 | tf_op jit(solution)/shard_map/ppermute | solution.py:260
  11.5 25.7 %collective-permute-start.2 = (bf16[2,256,256]{2,1,0:T(8,128)(2,1)S(1)}, bf16[2,256,256]{2,1,0:T(8,128)(2,1)S(1)}, u32[]{:S(2)}, u32[]{:S(2)}) collective-permute-start(bf16[2,256,256]{2,1,0:T(8,128)(2,1)S(1)} %shard_map.76.pair_ref), channel_id=1, source_target_pairs={{1,3},{3,5},{5,7},{7,9},{9,11},{11,13},{13,15},{15,17},{17,19},{19... | collective-permute-start | bytes 786440 | tf_op jit(solution)/shard_map/ppermute | solution.py:260
  13.5 21.8 %collective-permute-start.3 = (bf16[256,256]{1,0:T(8,128)(2,1)}, bf16[256,256]{1,0:T(8,128)(2,1)S(1)}, u32[]{:S(2)}, u32[]{:S(2)}) collective-permute-start(bf16[256,256]{1,0:T(8,128)(2,1)} %a_ref.1), channel_id=1, source_target_pairs={{0,24},{1,11},{2,26},{3,13},{4,28},{5,15},{6,30},{7,17},{8,0},{9,1... | collective-permute-start | bytes 393224 | tf_op jit(solution)/shard_map/ppermute | solution.py:260
  19.9 21.4 %collective-permute-start.1 = (bf16[256,256]{1,0:T(8,128)(2,1)S(1)}, bf16[256,256]{1,0:T(8,128)(2,1)S(1)}, u32[]{:S(2)}, u32[]{:S(2)}) collective-permute-start(bf16[256,256]{1,0:T(8,128)(2,1)S(1)} %collective-permute-done.b_ref), channel_id=1, source_target_pairs={{0,24},{1,11},{2,26},{3,13},{4,28},{5,15},{6,30},{7,17},{8,0},{9,1... | collective-permute-start | bytes 393224 | tf_op jit(solution)/shard_map/ppermute | solution.py:260
  35.3 18.0 %collective-permute-start.7 = (bf16[16,512,256]{2,1,0:T(8,128)(2,1)S(1)}, bf16[16,512,256]{2,1,0:T(8,128)(2,1)S(1)}, u32[]{:S(2)}, u32[]{:S(2)}) collective-permute-start(bf16[16,512,256]{2,1,0:T(8,128)(2,1)S(1)} %get-tuple-element.61), channel_id=1, source_target_pairs={{0,1},{1,0},{2,3},{3,2},{4,5},{5,4},{6,7},{7,6},{8,9},{9,8},{10,11... | collective-permute-start | bytes 12582920 | tf_op jit(solution)/shard_map/ppermute | solution.py:260
  37.2 10.2 %collective-permute-start.4 = (bf16[2,256,256]{2,1,0:T(8,128)(2,1)S(1)}, bf16[2,256,256]{2,1,0:T(8,128)(2,1)S(1)}, u32[]{:S(2)}, u32[]{:S(2)}) collective-permute-start(bf16[2,256,256]{2,1,0:T(8,128)(2,1)S(1)} %shard_map.78.a_ref), channel_id=1, source_target_pairs={{0,28},{1,5},{2,30},{3,7},{4,0},{5,9},{6,2},{7,11},{8,4},{9,13},{1... | collective-permute-start | bytes 786440 | tf_op jit(solution)/shard_map/ppermute | solution.py:260
  41.4 11.9 %collective-permute-start.6 = (bf16[2,256,256]{2,1,0:T(8,128)(2,1)S(1)}, bf16[2,256,256]{2,1,0:T(8,128)(2,1)S(1)}, u32[]{:S(2)}, u32[]{:S(2)}) collective-permute-start(bf16[2,256,256]{2,1,0:T(8,128)(2,1)S(1)} %shard_map.79.a_ref), channel_id=1, source_target_pairs={{0,28},{1,5},{2,30},{3,7},{4,0},{5,9},{6,2},{7,11},{8,4},{9,13},{1... | collective-permute-start | bytes 786440 | tf_op jit(solution)/shard_map/ppermute | solution.py:260
  47.5 12.3 %collective-permute-start.5 = (bf16[4,256,256]{2,1,0:T(8,128)(2,1)S(1)}, bf16[4,256,256]{2,1,0:T(8,128)(2,1)S(1)}, u32[]{:S(2)}, u32[]{:S(2)}) collective-permute-start(bf16[4,256,256]{2,1,0:T(8,128)(2,1)S(1)} %shard_map.80.a_ref.refs_0_), channel_id=1, source_target_pairs={{0,30},{1,3},{2,0},{3,5},{4,2},{5,7},{6,4},{7,9},{8,6},{9,11},{10,... | collective-permute-start | bytes 1572872 | tf_op jit(solution)/shard_map/ppermute | solution.py:260
  53.3 16.3 %collective-permute-start.10 = (bf16[4,256,256]{2,1,0:T(8,128)(2,1)S(1)}, bf16[4,256,256]{2,1,0:T(8,128)(2,1)S(1)}, u32[]{:S(2)}, u32[]{:S(2)}) collective-permute-start(bf16[4,256,256]{2,1,0:T(8,128)(2,1)S(1)} %shard_map.81.b_ref.refs_1_), channel_id=1, source_target_pairs={{0,30},{1,3},{2,0},{3,5},{4,2},{5,7},{6,4},{7,9},{8,6},{9,11},{10,... | collective-permute-start | bytes 1572872 | tf_op jit(solution)/shard_map/ppermute | solution.py:260
  59.8 12.4 %collective-permute-start.8 = (bf16[4,256,256]{2,1,0:T(8,128)(2,1)S(1)}, bf16[4,256,256]{2,1,0:T(8,128)(2,1)S(1)}, u32[]{:S(2)}, u32[]{:S(2)}) collective-permute-start(bf16[4,256,256]{2,1,0:T(8,128)(2,1)S(1)} %shard_map.80.a_ref.refs_0_), channel_id=1, source_target_pairs={{0,1},{1,0},{2,3},{3,2},{4,5},{5,4},{6,7},{7,6},{8,9},{9,8},{10,11... | collective-permute-start | bytes 1572872 | tf_op jit(solution)/shard_map/ppermute | solution.py:260
  65.2 7.0 %collective-permute-start.9 = (bf16[4,256,256]{2,1,0:T(8,128)(2,1)S(1)}, bf16[4,256,256]{2,1,0:T(8,128)(2,1)S(1)}, u32[]{:S(2)}, u32[]{:S(2)}) collective-permute-start(bf16[4,256,256]{2,1,0:T(8,128)(2,1)S(1)} %shard_map.81.b_ref.refs_1_), channel_id=1, source_target_pairs={{0,1},{1,0},{2,3},{3,2},{4,5},{5,4},{6,7},{7,6},{8,9},{9,8},{10,11... | collective-permute-start | bytes 1572872 | tf_op jit(solution)/shard_map/ppermute | solution.py:260
  67.2 6.1 %collective-permute-start.11 = (bf16[4,256,256]{2,1,0:T(8,128)(2,1)S(1)}, bf16[4,256,256]{2,1,0:T(8,128)(2,1)S(1)}, u32[]{:S(2)}, u32[]{:S(2)}) collective-permute-start(bf16[4,256,256]{2,1,0:T(8,128)(2,1)S(1)} %collective-permute-done.5.la_ref.refs_2_), channel_id=1, source_target_pairs={{0,1},{1,0},{2,3},{3,2},{4,5},{5,4},{6,7},{7,6},{8,9},{9,8},{10,11... | collective-permute-start | bytes 1572872 | tf_op jit(solution)/shard_map/ppermute | solution.py:260
  69.6 4.4 %collective-permute-start.12 = (bf16[4,256,256]{2,1,0:T(8,128)(2,1)S(1)}, bf16[4,256,256]{2,1,0:T(8,128)(2,1)S(1)}, u32[]{:S(2)}, u32[]{:S(2)}) collective-permute-start(bf16[4,256,256]{2,1,0:T(8,128)(2,1)S(1)} %collective-permute-done.10.lb_ref.refs_3_), channel_id=1, source_target_pairs={{0,1},{1,0},{2,3},{3,2},{4,5},{5,4},{6,7},{7,6},{8,9},{9,8},{10,11... | collective-permute-start | bytes 1572872 | tf_op jit(solution)/shard_map/ppermute | solution.py:260
  73.2 1.0 copy-start.3
  75.4 3.5 %collective-permute-start.13 = (bf16[256,512]{1,0:T(8,128)(2,1)S(1)}, bf16[256,512]{1,0:T(8,128)(2,1)S(1)}, u32[]{:S(2)}, u32[]{:S(2)}) collective-permute-start(bf16[256,512]{1,0:T(8,128)(2,1)S(1)} %get-tuple-element.77.pg_ref), channel_id=1, source_target_pairs={{0,1},{1,0},{2,3},{3,2},{4,5},{5,4},{6,7},{7,6},{8,9},{9,8},{10,11... | collective-permute-start | bytes 786440 | tf_op jit(solution)/shard_map/ppermute | solution.py:260
  79.7 16.5 %collective-permute-start.15 = (bf16[4,256,256]{2,1,0:T(8,128)(2,1)S(1)}, bf16[4,256,256]{2,1,0:T(8,128)(2,1)S(1)}, u32[]{:S(2)}, u32[]{:S(2)}) collective-permute-start(bf16[4,256,256]{2,1,0:T(8,128)(2,1)S(1)} %shard_map.86), channel_id=1, source_target_pairs={{0,2},{1,31},{2,4},{3,1},{4,6},{5,3},{6,8},{7,5},{8,10},{9,7},{10,... | collective-permute-start | bytes 1572872 | tf_op jit(solution)/shard_map/ppermute | solution.py:260
  85.7 13.2 %collective-permute-start.14 = (bf16[4,256,256]{2,1,0:T(8,128)(2,1)S(1)}, bf16[4,256,256]{2,1,0:T(8,128)(2,1)S(1)}, u32[]{:S(2)}, u32[]{:S(2)}) collective-permute-start(bf16[4,256,256]{2,1,0:T(8,128)(2,1)S(1)} %shard_map.87), channel_id=1, source_target_pairs={{0,2},{1,31},{2,4},{3,1},{4,6},{5,3},{6,8},{7,5},{8,10},{9,7},{10,... | collective-permute-start | bytes 1572872 | tf_op jit(solution)/shard_map/ppermute | solution.py:260
  94.7 1.5 %copy-start = (bf16[80,128,128]{2,1,0:T(8,128)(2,1)}, bf16[80,128,128]{2,1,0:T(8,128)(2,1)S(1)}, u32[]{:S(2)}) copy-start(bf16[80,128,128]{2,1,0:T(8,128)(2,1)S(1)} %shard_map.90) | copy-start | bytes 7864324
  97.0 11.4 %collective-permute-start.17 = (bf16[2,256,256]{2,1,0:T(8,128)(2,1)}, bf16[2,256,256]{2,1,0:T(8,128)(2,1)}, u32[]{:S(2)}, u32[]{:S(2)}) collective-permute-start(bf16[2,256,256]{2,1,0:T(8,128)(2,1)} %get-tuple-element.83), channel_id=1, source_target_pairs={{0,4},{1,29},{2,6},{3,31},{4,8},{5,1},{6,10},{7,3},{8,12},{9,5},{1... | collective-permute-start | bytes 786440 | tf_op jit(solution)/shard_map/ppermute | solution.py:260
  99.7 11.9 %collective-permute-start.16 = (bf16[2,256,256]{2,1,0:T(8,128)(2,1)}, bf16[2,256,256]{2,1,0:T(8,128)(2,1)S(1)}, u32[]{:S(2)}, u32[]{:S(2)}) collective-permute-start(bf16[2,256,256]{2,1,0:T(8,128)(2,1)} %get-tuple-element.82), channel_id=1, source_target_pairs={{0,4},{1,29},{2,6},{3,31},{4,8},{5,1},{6,10},{7,3},{8,12},{9,5},{1... | collective-permute-start | bytes 786440 | tf_op jit(solution)/shard_map/ppermute | solution.py:260
  101.6 43.2 %all-to-all-start = ((bf16[80,128,128]{2,1,0:T(8,128)(2,1)}), bf16[80,128,128]{2,1,0:T(8,128)(2,1)}, u32[]{:S(2)}, u32[]{:S(2)}) async-start(bf16[80,128,128]{2,1,0:T(8,128)(2,1)} %copy-done), calls=%async_computation | async-start | bytes 5242880 | tf_op jit(solution)/shard_map/all_to_all | solution.py:368
  111.6 0.7 copy-start.1
  112.3 0.9 copy-start.2
  114.2 24.5 %collective-permute-start.18 = (bf16[2,256,256]{2,1,0:T(8,128)(2,1)S(1)}, bf16[2,256,256]{2,1,0:T(8,128)(2,1)S(1)}, u32[]{:S(2)}, u32[]{:S(2)}) collective-permute-start(bf16[2,256,256]{2,1,0:T(8,128)(2,1)S(1)} %shard_map.94.refs_0_), channel_id=1, source_target_pairs={{1,31},{3,1},{5,3},{7,5},{9,7},{11,9},{13,11},{15,13},{17,15},{19,... | collective-permute-start | bytes 786440 | tf_op jit(solution)/shard_map/ppermute | solution.py:260
  120.2 14.1 %collective-permute-start.20 = (bf16[256,256]{1,0:T(8,128)(2,1)S(1)}, bf16[256,256]{1,0:T(8,128)(2,1)S(1)}, u32[]{:S(2)}, u32[]{:S(2)}) collective-permute-start(bf16[256,256]{1,0:T(8,128)(2,1)S(1)} %get-tuple-element.93), channel_id=1, source_target_pairs={{0,8},{1,23},{2,10},{3,25},{4,12},{5,27},{6,14},{7,29},{8,16},{9,3... | collective-permute-start | bytes 393224 | tf_op jit(solution)/shard_map/ppermute | solution.py:260
  124.2 14.5 %collective-permute-start.19 = (bf16[256,256]{1,0:T(8,128)(2,1)S(1)}, bf16[256,256]{1,0:T(8,128)(2,1)S(1)}, u32[]{:S(2)}, u32[]{:S(2)}) collective-permute-start(bf16[256,256]{1,0:T(8,128)(2,1)S(1)} %get-tuple-element.91), channel_id=1, source_target_pairs={{0,8},{1,23},{2,10},{3,25},{4,12},{5,27},{6,14},{7,29},{8,16},{9,3... | collective-permute-start | bytes 393224 | tf_op jit(solution)/shard_map/ppermute | solution.py:260
  138.8 8.8 %collective-permute-start.21 = (bf16[256,256]{1,0:T(8,128)(2,1)S(1)}, bf16[256,256]{1,0:T(8,128)(2,1)S(1)}, u32[]{:S(2)}, u32[]{:S(2)}) collective-permute-start(bf16[256,256]{1,0:T(8,128)(2,1)S(1)} %get-tuple-element.98), channel_id=1, source_target_pairs={{0,1},{1,0},{2,3},{3,2},{4,5},{5,4},{6,7},{7,6},{8,9},{9,8},{10,11... | collective-permute-start | bytes 393224 | tf_op jit(solution)/shard_map/ppermute | solution.py:260

commit v5 on v4

--- a/solution.py
+++ b/solution.py
@@ -14,6 +14,9 @@
 BF16, F32 = jnp.bfloat16, jnp.float32
 NZ = 16
 JOIN = 80 * 10**9
+FIRST = 200 * 10**9
+SECOND = 0
+TURN = 10 * 10**9
 
 
 def params(mib):
@@ -175,40 +178,32 @@
         out_ref[n] = (d_ref[2 + n] + f32(r1_ref[2 + n])).astype(BF16)
 
 
-def add_second(d_ref, r1_ref, r2_ref, out_ref):
-    out_ref[...] = (d_ref[1] + f32(r1_ref[1]) + f32(r2_ref[1])).astype(BF16)
-
-
-def add_base(da_ref, r1a_ref, r2a_ref, db_ref, r1b_ref, r2b_ref, out_ref):
-    out_ref[0] = (da_ref[0] + f32(r1a_ref[0]) + f32(r2a_ref[0])).astype(BF16)
-    out_ref[1] = (db_ref[0] + f32(r1b_ref[0]) + f32(r2b_ref[0])).astype(BF16)
-
-
-def add_cross(base_ref, hop_ref, r3b_ref, out_ref):
+def add_second(d_ref, r1_ref, r2_ref, next_ref, base_ref):
+    for n, out_ref in enumerate((base_ref, next_ref)):
+        out_ref[...] = (d_ref[n] + f32(r1_ref[n]) + f32(r2_ref[n])).astype(BF16)
+
+
+def add_cross(base_ref, hop_ref, r3_ref, out_ref):
     def put(ref):
-        out_ref[...] = (f32(ref[1]) + f32(r3b_ref[...])).astype(BF16)
+        out_ref[...] = (f32(ref[...]) + f32(r3_ref[...])).astype(out_ref.dtype)
 
     chosen_base(base_ref, hop_ref, put)
 
 
-def add_last(base_ref, hop_ref, r3a_ref, cross_ref, out_ref):
-    def put(ref):
-        out_ref[...] = (f32(ref[0]) + f32(r3a_ref[...]) + f32(cross_ref[...])).astype(BF16)
-
-    chosen_base(base_ref, hop_ref, put)
+def add_last(own_ref, cross_ref, out_ref):
+    out_ref[...] = (own_ref[...] + f32(cross_ref[...])).astype(BF16)
 
 
 def weight_terms(listed_hbm, pg_ref, *refs):
-    x_refs, (out_ref, listed, flipped, dense, sem) = refs[:8], refs[8:]
+    x_refs, (out_ref, listed, flipped, dense, sem) = refs[:-5], refs[-5:]
     fetch = pltpu.make_async_copy(listed_hbm, listed, sem)
     fetch.start()
     slots, blk = out_ref.shape[0], out_ref.shape[1]
     rows_per_dev = dense.shape[2] // blk
     me = my_place()
     flipped[...] = pg_ref[...].T
-    for m, ref in enumerate(x_refs):
-        for n in range(ref.shape[0]):
-            dense[4 * m + n] = jnp.dot(flipped[...], ref[n], preferred_element_type=F32).astype(BF16)
+    for n, (ref, m) in enumerate([(ref, m) for ref in x_refs for m in range(ref.shape[0])]):
+        dense[n] = jnp.dot(flipped[...], ref[m], preferred_element_type=F32).astype(BF16)
 
     fetch.wait()
 
@@ -279,8 +274,17 @@
     theirs = other_core(tokens)
     g4b = steps(theirs, -4, -5)
     pair = kernel(pair_up, shards(2), n_in=2)(tokens, theirs)
-    pair, listed = together((pair, listed))
     base = hop(pair, 1)
+
+    def based(n, g):
+        return kernel(functools.partial(join_base, n), shards(2), n_in=3, flops=n * JOIN, size=0)(pair, base, g)
+
+    g04a = based(0, g4a)
+    g26a = steps(g04a, -2)
+    g4b, g04a = together((g4b, g04a))
+    g04b = based(1, g4b)
+    g26b = steps(g04b, -2)
+    g04b, listed = together((g04b, listed))
     up_w, down_w, down_other = kernel(
         lay_weights,
         (shape(2 * NZ * feats, width),) + (shape(NZ, width, feats),) * 2,
@@ -290,21 +294,11 @@
             pltpu.VMEM((slots, blk, blk), BF16), pltpu.SemaphoreType.DMA((3,)),
         ],
     )(in_hbm(listed), in_hbm(cut), in_hbm(up_blocks[0]))
-    g4a, up_w = together((g4a, up_w))
+    g26a, g04b, up_w = together((g26a, g04b, up_w))
     down_sibling = other_core(down_other)
-
-    def based(n, g):
-        return kernel(functools.partial(join_base, n), shards(2), n_in=3, flops=n * JOIN, size=0)(pair, base, g)
-
-    g04a = based(0, g4a)
-    g26a = steps(g04a, -2)
-    g4b, g04a = together((g4b, g04a))
-    g04b = based(1, g4b)
-    g26b = steps(g04b, -2)
-    g26a, g04b = together((g26a, g04b))
     ea = kernel(join, shards(4), n_in=2, size=0)(g04a, g26a)
     la = steps(ea, -1)
-    g26b, ea, down_sibling = together((g26b, ea, down_sibling))
+    g26b, ea = together((g26b, ea))
     eb = kernel(join, shards(4), n_in=2, flops=JOIN, size=0)(g04b, g26b)
     lb = steps(eb, -1)
     la, ea, eb = together((la, ea, eb))
@@ -335,9 +329,8 @@
     pg, d1b = together((pg, d1b))
     d1a = back_of(8, BF16)
     r1a = steps(d1a, 1)
-    pg, d1a = together((pg, d1a))
     d2b, d2a = back_of(4, F32), back_of(0, F32)
-    pg_after, d2b, d2a = together((pg, d2b, d2a))
+    pg, d1a, d2b, d2a = together((pg, d1a, d2b, d2a))
     terms = kernel(
         weight_terms, shape(slots, blk, blk), ins=[HBM], n_in=9, mib=14,
         flops=flops_of(32), size=16 * MIB,
@@ -345,43 +338,40 @@
             pltpu.SMEM(listed.shape, jnp.int32), pltpu.VMEM((width, tok_rows), BF16),
             pltpu.VMEM((2 * NZ, width, feats), BF16), pltpu.SemaphoreType.DMA,
         ],
-    )(in_hbm(listed), pg_after, ea, eb, la, lb, ea2, eb2, la2, lb2)
-    r1b, terms = together((r1b, terms))
-
+    )(in_hbm(listed), pg, ea, eb, la, lb, ea2, eb2, la2, lb2)
+    got = lax.all_to_all(terms, "dp", 0, 0, tiled=True)
     def in_turn(body, out, turn, *operands, flops=0):
         n = len(operands)
 
         def ordered(*refs):
-            body(*refs[:n], refs[n + 1])
-            refs[n + 2][...] = refs[n][...]
-
-        return kernel(ordered, (out, shape(8, blk, dtype=F32)), n_in=n + 1, flops=flops)(*operands, turn)
+            body(*refs[:n], *refs[n + 1 : -1])
+            refs[-1][...] = refs[n][...]
+
+        return kernel(ordered, out + (shape(8, blk, dtype=F32),), n_in=n + 1, flops=flops, size=0)(*operands, turn)
 
     one = shape(tok_rows, feats)
     turn = jnp.zeros((8, blk), F32)
-    q, turn = in_turn(add_first, shards(2), turn, d2b, r1b)
+    q, turn = in_turn(add_first, (shards(2),), turn, d2b, r1b, flops=FIRST)
     r2b = steps(q, 2)
     r1a, turn = together((r1a, turn))
-    q, turn = in_turn(add_first, shards(2), turn, d2a, r1a)
+    q, turn = in_turn(add_first, (shards(2),), turn, d2a, r1a, flops=SECOND)
     r2a = steps(q, 2)
-    terms, turn = together((terms, turn))
-    got = lax.all_to_all(terms, "dp", 0, 0, tiled=True)
     r2b, turn = together((r2b, turn))
-    q, turn = in_turn(add_second, one, turn, d2b, r1b, r2b, flops=10**11)
+    q, sum_b, turn = in_turn(add_second, (one, one), turn, d2b, r1b, r2b)
     r3b = steps(q, 4, 5)
+    moved_b = hop(sum_b, -1)
     r2a, turn = together((r2a, turn))
-    q, turn = in_turn(add_second, one, turn, d2a, r1a, r2a)
+    q, sum_a, turn = in_turn(add_second, (one, one), turn, d2a, r1a, r2a, flops=SECOND)
     r3a = steps(q, 4, 5)
-    sums = kernel(add_base, shards(2), n_in=6, size=0)(d2a, r1a, r2a, d2b, r1b, r2b)
-    moved = hop(sums, -1)
+    moved_a = hop(sum_a, -1)
+    q, turn = in_turn(add_cross, (one,), turn, sum_b, moved_b, r3b)
+    cross = other_core(q)
     own_grads = kernel(
-        functools.partial(add_terms, 1.0 / (tok_rows * n_dp) ** 0.5), shape(per, blk, blk, dtype=F32), size=3 * MIB
+        functools.partial(add_terms, 1.0 / (tok_rows * n_dp) ** 0.5), shape(per, blk, blk, dtype=F32), size=0
     )(got.reshape(n_dp, per, blk, blk))
-    r3b, r3a, turn = together((r3b, r3a, turn))
-    q, turn = in_turn(add_cross, one, turn, sums, moved, r3b)
-    cross = other_core(q)
-    cross, own_grads, turn = together((cross, own_grads, turn))
-    in_grad, _ = in_turn(add_last, one, turn, sums, moved, r3a, cross)
+    total = kernel(add_cross, shape(tok_rows, feats, dtype=F32), n_in=3, flops=TURN, size=0)(sum_a, moved_a, r3a)
+    cross, own_grads, total, turn = together((cross, own_grads, total, turn))
+    in_grad, _ = in_turn(add_last, (one,), turn, total, cross)
     return act, in_grad, own_grads[None]
 
 

time: 150 us -> 153 us (1.020)
  starting transfers between devices: 89.3 us -> 101 us
  waiting for transfers between devices: 26.4 us -> 22.1 us
  Pallas kernels: 28.2 us -> 25.6 us
    ppermute x22 -> x23, starting transfers between devices: 82.5 us -> 94 us  [send(): return lax.ppermute(v, 'blk', pairs)]
    all_to_all x1, waiting for transfers between devices: 3.99 us -> 0.01 us  [on_device(): got = lax.all_to_all(terms, 'dp', 0, 0, tiled=True)]
    unnamed x8 -> x6, local copies, waits for them, and re-layouts: 3.35 us -> 2.66 us
    ppermute x22 -> x23, waiting for transfers between devices: 22.4 us -> 22.1 us  [send(): return lax.ppermute(v, 'blk', pairs)]
  transfers between devices with their start and end apart: 23 -> 24, of which waited for: 9 -> 6; matrix products, arithmetic and copies ran while one was open for 0% -> 0% of each run, Pallas kernels for 17% -> 16%
where the time goes in v5:
time: 153 us; the launch traced here: 152 us
  starting transfers between devices  101 us (66%)
  Pallas kernels  25.6 us (17%)
  waiting for transfers between devices  22.1 us (14%)
  local copies, waits for them, and re-layouts  2.66 us (2%)
    ppermute x23, starting transfers between devices, send(): return lax.ppermute(v, 'blk', pairs)  94 us
    ppermute x23, waiting for transfers between devices, send(): return lax.ppermute(v, 'blk', pairs)  22.1 us
    all_to_all x1, starting transfers between devices, on_device(): got = lax.all_to_all(terms, 'dp', 0, 0, tiled=True)  6.8 us
    pallas_call x1, Pallas kernels, on_device(): kernel(lay_weights, (shape(2 * NZ * feats, width),) + (shape(NZ, width, f...  6.61 us
    pallas_call x1, Pallas kernels, on_device(): kernel(weight_terms, shape(slots, blk, blk), ins=[HBM], n_in=9, mib=14, f...  5.63 us
    pallas_call x4, Pallas kernels, back_of(): kernel(functools.partial(back, first), shards(4, dtype), n_in=4, flops=fl...  3.61 us
    pallas_call x6, Pallas kernels, in_turn(): kernel(ordered, out + (shape(8, blk, dtype=F32),), n_in=n + 1, flops=flop...  3.08 us
  transfers between devices with their start and end apart: 24, of which 6 were waited for; matrix products, arithmetic and copies ran while one was open for 0% of the time, Pallas kernels for 16%

profile of v5, /device:TPU:1, one launch (start us, length us, event | category | flops | bytes accessed | tf_op | source)
XLA Modules:
  0.0 152.4 jit_solution(17137286276020483009)
XLA Ops:
  0.6 8.8 %collective-permute-start = (bf16[256,256]{1,0:T(8,128)(2,1)}, bf16[256,256]{1,0:T(8,128)(2,1)S(1)}, u32[]{:S(2)}, u32[]{:S(2)}) collective-permute-start(bf16[256,256]{1,0:T(8,128)(2,1)} %a_ref.1), channel_id=1, source_target_pairs={{0,1},{1,0},{2,3},{3,2},{4,5},{5,4},{6,7},{7,6},{8,9},{9,8},{10,11... | collective-permute-start | bytes 393224 | tf_op jit(solution)/shard_map/ppermute | solution.py:255
  9.4 1.2 collective-permute-done.b_ref
  10.6 0.9 copy-done.2
  11.5 1.9 %collective-permute-start.2 = (bf16[2,256,256]{2,1,0:T(8,128)(2,1)S(1)}, bf16[2,256,256]{2,1,0:T(8,128)(2,1)S(1)}, u32[]{:S(2)}, u32[]{:S(2)}) collective-permute-start(bf16[2,256,256]{2,1,0:T(8,128)(2,1)S(1)} %shard_map.76.pair_ref), channel_id=1, source_target_pairs={{1,3},{3,5},{5,7},{7,9},{9,11},{11,13},{13,15},{15,17},{17,19},{19... | collective-permute-start | bytes 786440 | tf_op jit(solution)/shard_map/ppermute | solution.py:255
  13.5 6.4 %collective-permute-start.3 = (bf16[256,256]{1,0:T(8,128)(2,1)}, bf16[256,256]{1,0:T(8,128)(2,1)S(1)}, u32[]{:S(2)}, u32[]{:S(2)}) collective-permute-start(bf16[256,256]{1,0:T(8,128)(2,1)} %a_ref.1), channel_id=1, source_target_pairs={{0,24},{1,11},{2,26},{3,13},{4,28},{5,15},{6,30},{7,17},{8,0},{9,1... | collective-permute-start | bytes 393224 | tf_op jit(solution)/shard_map/ppermute | solution.py:255
  19.9 7.5 %collective-permute-start.1 = (bf16[256,256]{1,0:T(8,128)(2,1)S(1)}, bf16[256,256]{1,0:T(8,128)(2,1)S(1)}, u32[]{:S(2)}, u32[]{:S(2)}) collective-permute-start(bf16[256,256]{1,0:T(8,128)(2,1)S(1)} %collective-permute-done.b_ref), channel_id=1, source_target_pairs={{0,24},{1,11},{2,26},{3,13},{4,28},{5,15},{6,30},{7,17},{8,0},{9,1... | collective-permute-start | bytes 393224 | tf_op jit(solution)/shard_map/ppermute | solution.py:255
  27.4 5.5 %collective-permute-start.4 = (bf16[2,256,256]{2,1,0:T(8,128)(2,1)S(1)}, bf16[2,256,256]{2,1,0:T(8,128)(2,1)S(1)}, u32[]{:S(2)}, u32[]{:S(2)}) collective-permute-start(bf16[2,256,256]{2,1,0:T(8,128)(2,1)S(1)} %shard_map.77.a_ref), channel_id=1, source_target_pairs={{0,28},{1,5},{2,30},{3,7},{4,0},{5,9},{6,2},{7,11},{8,4},{9,13},{1... | collective-permute-start | bytes 786440 | tf_op jit(solution)/shard_map/ppermute | solution.py:255
  32.9 1.5 collective-permute-done.1.g4_ref
  34.4 5.9 %collective-permute-start.6 = (bf16[2,256,256]{2,1,0:T(8,128)(2,1)S(1)}, bf16[2,256,256]{2,1,0:T(8,128)(2,1)S(1)}, u32[]{:S(2)}, u32[]{:S(2)}) collective-permute-start(bf16[2,256,256]{2,1,0:T(8,128)(2,1)S(1)} %shard_map.78.a_ref), channel_id=1, source_target_pairs={{0,28},{1,5},{2,30},{3,7},{4,0},{5,9},{6,2},{7,11},{8,4},{9,13},{1... | collective-permute-start | bytes 786440 | tf_op jit(solution)/shard_map/ppermute | solution.py:255
  40.4 6.6 %shard_map.79 = (bf16[8192,512]{1,0:T(8,128)(2,1)S(1)}, bf16[16,512,256]{2,1,0:T(8,128)(2,1)S(1)}, bf16[16,512,256]{2,1,0:T(8,128)(2,1)S(1)}) custom-call(s32[2,80]{1,0:T(2,128)} %bitcast.10, s32[2,32]{1,0:T(2,128)} %bitcast.9, bf16[80,128,128]{2,1,0:T(8,128)(2,1)} %bitcast.7), custom_call_target="tpu_custom_call" | custom-call | bytes 20971520 | tf_op jit(solution)/shard_map/pallas_call | solution.py:288
  47.0 1.9 %collective-permute-start.13 = (bf16[16,512,256]{2,1,0:T(8,128)(2,1)S(1)}, bf16[16,512,256]{2,1,0:T(8,128)(2,1)S(1)}, u32[]{:S(2)}, u32[]{:S(2)}) collective-permute-start(bf16[16,512,256]{2,1,0:T(8,128)(2,1)S(1)} %get-tuple-element.63), channel_id=1, source_target_pairs={{0,1},{1,0},{2,3},{3,2},{4,5},{5,4},{6,7},{7,6},{8,9},{9,8},{10,11... | collective-permute-start | bytes 12582920 | tf_op jit(solution)/shard_map/ppermute | solution.py:255
  49.0 4.4 %collective-permute-start.5 = (bf16[4,256,256]{2,1,0:T(8,128)(2,1)S(1)}, bf16[4,256,256]{2,1,0:T(8,128)(2,1)S(1)}, u32[]{:S(2)}, u32[]{:S(2)}) collective-permute-start(bf16[4,256,256]{2,1,0:T(8,128)(2,1)S(1)} %shard_map.80.a_ref.refs_0_), channel_id=1, source_target_pairs={{0,30},{1,3},{2,0},{3,5},{4,2},{5,7},{6,4},{7,9},{8,6},{9,11},{10,... | collective-permute-start | bytes 1572872 | tf_op jit(solution)/shard_map/ppermute | solution.py:255
  53.4 3.5 %collective-permute-start.9 = (bf16[4,256,256]{2,1,0:T(8,128)(2,1)S(1)}, bf16[4,256,256]{2,1,0:T(8,128)(2,1)S(1)}, u32[]{:S(2)}, u32[]{:S(2)}) collective-permute-start(bf16[4,256,256]{2,1,0:T(8,128)(2,1)S(1)} %shard_map.81.b_ref.refs_1_), channel_id=1, source_target_pairs={{0,30},{1,3},{2,0},{3,5},{4,2},{5,7},{6,4},{7,9},{8,6},{9,11},{10,... | collective-permute-start | bytes 1572872 | tf_op jit(solution)/shard_map/ppermute | solution.py:255
  56.8 3.4 %collective-permute-done.5.la_ref.refs_2_ = bf16[4,256,256]{2,1,0:T(8,128)(2,1)S(1)} collective-permute-done((bf16[4,256,256]{2,1,0:T(8,128)(2,1)S(1)}, bf16[4,256,256]{2,1,0:T(8,128)(2,1)S(1)}, u32[]{:S(2)}, u32[]{:S(2)}) %collective-permute-start.5) | collective-permute-done | bytes 524320 | tf_op jit(solution)/shard_map/ppermute | solution.py:255
  60.2 2.9 %collective-permute-start.7 = (bf16[4,256,256]{2,1,0:T(8,128)(2,1)S(1)}, bf16[4,256,256]{2,1,0:T(8,128)(2,1)S(1)}, u32[]{:S(2)}, u32[]{:S(2)}) collective-permute-start(bf16[4,256,256]{2,1,0:T(8,128)(2,1)S(1)} %shard_map.80.a_ref.refs_0_), channel_id=1, source_target_pairs={{0,1},{1,0},{2,3},{3,2},{4,5},{5,4},{6,7},{7,6},{8,9},{9,8},{10,11... | collective-permute-start | bytes 1572872 | tf_op jit(solution)/shard_map/ppermute | solution.py:255
  63.2 1.9 %collective-permute-start.8 = (bf16[4,256,256]{2,1,0:T(8,128)(2,1)S(1)}, bf16[4,256,256]{2,1,0:T(8,128)(2,1)S(1)}, u32[]{:S(2)}, u32[]{:S(2)}) collective-permute-start(bf16[4,256,256]{2,1,0:T(8,128)(2,1)S(1)} %shard_map.81.b_ref.refs_1_), channel_id=1, source_target_pairs={{0,1},{1,0},{2,3},{3,2},{4,5},{5,4},{6,7},{7,6},{8,9},{9,8},{10,11... | collective-permute-start | bytes 1572872 | tf_op jit(solution)/shard_map/ppermute | solution.py:255
  65.1 2.4 %collective-permute-start.10 = (bf16[4,256,256]{2,1,0:T(8,128)(2,1)S(1)}, bf16[4,256,256]{2,1,0:T(8,128)(2,1)S(1)}, u32[]{:S(2)}, u32[]{:S(2)}) collective-permute-start(bf16[4,256,256]{2,1,0:T(8,128)(2,1)S(1)} %collective-permute-done.5.la_ref.refs_2_), channel_id=1, source_target_pairs={{0,1},{1,0},{2,3},{3,2},{4,5},{5,4},{6,7},{7,6},{8,9},{9,8},{10,11... | collective-permute-start | bytes 1572872 | tf_op jit(solution)/shard_map/ppermute | solution.py:255
  67.5 1.9 %collective-permute-start.11 = (bf16[4,256,256]{2,1,0:T(8,128)(2,1)S(1)}, bf16[4,256,256]{2,1,0:T(8,128)(2,1)S(1)}, u32[]{:S(2)}, u32[]{:S(2)}) collective-permute-start(bf16[4,256,256]{2,1,0:T(8,128)(2,1)S(1)} %collective-permute-done.9.lb_ref.refs_3_), channel_id=1, source_target_pairs={{0,1},{1,0},{2,3},{3,2},{4,5},{5,4},{6,7},{7,6},{8,9},{9,8},{10,11... | collective-permute-start | bytes 1572872 | tf_op jit(solution)/shard_map/ppermute | solution.py:255
  69.4 0.7 shard_map.82.so_far
  70.2 1.0 shard_map.83.so_far
  71.2 0.7 shard_map.84.so_far
  71.9 0.2 copy-done.1
  72.1 1.3 shard_map.85
  73.4 2.4 %collective-permute-start.12 = (bf16[256,512]{1,0:T(8,128)(2,1)S(1)}, bf16[256,512]{1,0:T(8,128)(2,1)S(1)}, u32[]{:S(2)}, u32[]{:S(2)}) collective-permute-start(bf16[256,512]{1,0:T(8,128)(2,1)S(1)} %get-tuple-element.82.pg_ref), channel_id=1, source_target_pairs={{0,1},{1,0},{2,3},{3,2},{4,5},{5,4},{6,7},{7,6},{8,9},{9,8},{10,11... | collective-permute-start | bytes 786440 | tf_op jit(solution)/shard_map/ppermute | solution.py:255
  75.8 1.1 collective-permute-done.12.pg2_ref
  76.9 0.7 shard_map.86
  77.6 5.2 %collective-permute-start.14 = (bf16[4,256,256]{2,1,0:T(8,128)(2,1)S(1)}, bf16[4,256,256]{2,1,0:T(8,128)(2,1)S(1)}, u32[]{:S(2)}, u32[]{:S(2)}) collective-permute-start(bf16[4,256,256]{2,1,0:T(8,128)(2,1)S(1)} %shard_map.86), channel_id=1, source_target_pairs={{0,2},{1,31},{2,4},{3,1},{4,6},{5,3},{6,8},{7,5},{8,10},{9,7},{10,... | collective-permute-start | bytes 1572872 | tf_op jit(solution)/shard_map/ppermute | solution.py:255
  82.8 1.5 shard_map.87
  84.3 2.5 %collective-permute-start.16 = (bf16[4,256,256]{2,1,0:T(8,128)(2,1)}, bf16[4,256,256]{2,1,0:T(8,128)(2,1)}, u32[]{:S(2)}, u32[]{:S(2)}) collective-permute-start(bf16[4,256,256]{2,1,0:T(8,128)(2,1)} %shard_map.87), channel_id=1, source_target_pairs={{0,2},{1,31},{2,4},{3,1},{4,6},{5,3},{6,8},{7,5},{8,10},{9,7},{10,... | collective-permute-start | bytes 1572872 | tf_op jit(solution)/shard_map/ppermute | solution.py:255
  86.9 0.7 shard_map.89.refs_0_
  87.6 0.7 shard_map.88.refs_0_
  88.3 5.6 %shard_map.95 = bf16[80,128,128]{2,1,0:T(8,128)(2,1)S(1)} custom-call(s32[2,80]{1,0:T(2,128)} %bitcast.11, bf16[256,512]{1,0:T(8,128)(2,1)S(1)} %get-tuple-element.82.pg_ref, bf16[4,256,256]{2,1,0:T(8,128)(2,1)S(1)} %shard_map.80.a_ref.refs_0_, bf16[4,256,256]{2,1,0:T(8,128)(2,1)S(1)} %shard_map.81.b_ref.refs_1_, ...), custom_call_target="tpu_custom_call" | custom-call | flops 2147483648 | bytes 16777216 | tf_op jit(solution)/shard_map/pallas_call | solution.py:334
  94.0 1.5 %copy-done = bf16[80,128,128]{2,1,0:T(8,128)(2,1)} copy-done((bf16[80,128,128]{2,1,0:T(8,128)(2,1)}, bf16[80,128,128]{2,1,0:T(8,128)(2,1)S(1)}, u32[]{:S(2)}) %copy-start) | copy-done | bytes 2621464
  95.5 6.8 %all-to-all-start = ((bf16[80,128,128]{2,1,0:T(8,128)(2,1)}), bf16[80,128,128]{2,1,0:T(8,128)(2,1)}, u32[]{:S(2)}, u32[]{:S(2)}) async-start(bf16[80,128,128]{2,1,0:T(8,128)(2,1)} %copy-done), calls=%async_computation | async-start | bytes 5242880 | tf_op jit(solution)/shard_map/all_to_all | solution.py:342
  102.4 4.5 %collective-permute-start.15 = (bf16[2,256,256]{2,1,0:T(8,128)(2,1)S(1)}, bf16[2,256,256]{2,1,0:T(8,128)(2,1)S(1)}, u32[]{:S(2)}, u32[]{:S(2)}) collective-permute-start(bf16[2,256,256]{2,1,0:T(8,128)(2,1)S(1)} %get-tuple-element.66), channel_id=1, source_target_pairs={{0,4},{1,29},{2,6},{3,31},{4,8},{5,1},{6,10},{7,3},{8,12},{9,5},{1... | collective-permute-start | bytes 786440 | tf_op jit(solution)/shard_map/ppermute | solution.py:255
  106.9 1.1 shard_map.91
  107.9 5.0 %collective-permute-start.19 = (bf16[2,256,256]{2,1,0:T(8,128)(2,1)S(1)}, bf16[2,256,256]{2,1,0:T(8,128)(2,1)S(1)}, u32[]{:S(2)}, u32[]{:S(2)}) collective-permute-start(bf16[2,256,256]{2,1,0:T(8,128)(2,1)S(1)} %get-tuple-element.76), channel_id=1, source_target_pairs={{0,4},{1,29},{2,6},{3,31},{4,8},{5,1},{6,10},{7,3},{8,12},{9,5},{1... | collective-permute-start | bytes 786440 | tf_op jit(solution)/shard_map/ppermute | solution.py:255
  113.0 0.1 shard_map.92
  113.1 6.2 %collective-permute-done.19.refs_2_ = bf16[2,256,256]{2,1,0:T(8,128)(2,1)S(1)} collective-permute-done((bf16[2,256,256]{2,1,0:T(8,128)(2,1)S(1)}, bf16[2,256,256]{2,1,0:T(8,128)(2,1)S(1)}, u32[]{:S(2)}, u32[]{:S(2)}) %collective-permute-start.19) | collective-permute-done | bytes 262176 | tf_op jit(solution)/shard_map/ppermute | solution.py:255
  119.3 4.8 %collective-permute-start.17 = (bf16[256,256]{1,0:T(8,128)(2,1)S(1)}, bf16[256,256]{1,0:T(8,128)(2,1)S(1)}, u32[]{:S(2)}, u32[]{:S(2)}) collective-permute-start(bf16[256,256]{1,0:T(8,128)(2,1)S(1)} %get-tuple-element.74.refs_0_), channel_id=1, source_target_pairs={{1,31},{3,1},{5,3},{7,5},{9,7},{11,9},{13,11},{15,13},{17,15},{19,... | collective-permute-start | bytes 393224 | tf_op jit(solution)/shard_map/ppermute | solution.py:255
  124.1 7.0 %collective-permute-start.18 = (bf16[256,256]{1,0:T(8,128)(2,1)S(1)}, bf16[256,256]{1,0:T(8,128)(2,1)S(1)}, u32[]{:S(2)}, u32[]{:S(2)}) collective-permute-start(bf16[256,256]{1,0:T(8,128)(2,1)S(1)} %get-tuple-element.75), channel_id=1, source_target_pairs={{0,8},{1,23},{2,10},{3,25},{4,12},{5,27},{6,14},{7,29},{8,16},{9,3... | collective-permute-start | bytes 393224 | tf_op jit(solution)/shard_map/ppermute | solution.py:255
  131.1 1.1 shard_map.93
  132.3 1.9 %collective-permute-start.21 = (bf16[256,256]{1,0:T(8,128)(2,1)S(1)}, bf16[256,256]{1,0:T(8,128)(2,1)S(1)}, u32[]{:S(2)}, u32[]{:S(2)}) collective-permute-start(bf16[256,256]{1,0:T(8,128)(2,1)S(1)} %get-tuple-element.83.base_ref), channel_id=1, source_target_pairs={{1,31},{3,1},{5,3},{7,5},{9,7},{11,9},{13,11},{15,13},{17,15},{19,... | collective-permute-start | bytes 393224 | tf_op jit(solution)/shard_map/ppermute | solution.py:255
  134.2 3.7 %collective-permute-start.22 = (bf16[256,256]{1,0:T(8,128)(2,1)S(1)}, bf16[256,256]{1,0:T(8,128)(2,1)S(1)}, u32[]{:S(2)}, u32[]{:S(2)}) collective-permute-start(bf16[256,256]{1,0:T(8,128)(2,1)S(1)} %get-tuple-element.84), channel_id=1, source_target_pairs={{0,8},{1,23},{2,10},{3,25},{4,12},{5,27},{6,14},{7,29},{8,16},{9,3... | collective-permute-start | bytes 393224 | tf_op jit(solution)/shard_map/ppermute | solution.py:255
  138.0 1.9 %collective-permute-start.20 = (bf16[256,256]{1,0:T(8,128)(2,1)S(1)}, bf16[256,256]{1,0:T(8,128)(2,1)S(1)}, u32[]{:S(2)}, u32[]{:S(2)}) collective-permute-start(bf16[256,256]{1,0:T(8,128)(2,1)S(1)} %get-tuple-element.81), channel_id=1, source_target_pairs={{0,1},{1,0},{2,3},{3,2},{4,5},{5,4},{6,7},{7,6},{8,9},{9,8},{10,11... | collective-permute-start | bytes 393224 | tf_op jit(solution)/shard_map/ppermute | solution.py:255
  140.0 8.8 %collective-permute-done.22.r3_ref = bf16[256,256]{1,0:T(8,128)(2,1)S(1)} collective-permute-done((bf16[256,256]{1,0:T(8,128)(2,1)S(1)}, bf16[256,256]{1,0:T(8,128)(2,1)S(1)}, u32[]{:S(2)}, u32[]{:S(2)}) %collective-permute-start.22) | collective-permute-done | bytes 131104 | tf_op jit(solution)/shard_map/ppermute | solution.py:255
  148.8 2.9 %shard_map.96 = f32[5,128,128]{2,1,0:T(8,128)} custom-call(bf16[16,5,128,128]{3,2,1,0:T(8,128)(2,1)} %bitcast.4.in_ref), custom_call_target="tpu_custom_call" | custom-call | tf_op jit(solution)/shard_map/pallas_call | solution.py:369
  151.7 0.7 shard_map.98
  (30 shorter events, 0.3 us)
Async XLA Ops:
  0.6 10.0 %collective-permute-start = (bf16[256,256]{1,0:T(8,128)(2,1)}, bf16[256,256]{1,0:T(8,128)(2,1)S(1)}, u32[]{:S(2)}, u32[]{:S(2)}) collective-permute-start(bf16[256,256]{1,0:T(8,128)(2,1)} %a_ref.1), channel_id=1, source_target_pairs={{0,1},{1,0},{2,3},{3,2},{4,5},{5,4},{6,7},{7,6},{8,9},{9,8},{10,11... | collective-permute-start | bytes 393224 | tf_op jit(solution)/shard_map/ppermute | solution.py:255
  10.6 0.9 copy-start.2
  11.5 15.9 %collective-permute-start.2 = (bf16[2,256,256]{2,1,0:T(8,128)(2,1)S(1)}, bf16[2,256,256]{2,1,0:T(8,128)(2,1)S(1)}, u32[]{:S(2)}, u32[]{:S(2)}) collective-permute-start(bf16[2,256,256]{2,1,0:T(8,128)(2,1)S(1)} %shard_map.76.pair_ref), channel_id=1, source_target_pairs={{1,3},{3,5},{5,7},{7,9},{9,11},{11,13},{13,15},{15,17},{17,19},{19... | collective-permute-start | bytes 786440 | tf_op jit(solution)/shard_map/ppermute | solution.py:255
  13.5 13.9 %collective-permute-start.3 = (bf16[256,256]{1,0:T(8,128)(2,1)}, bf16[256,256]{1,0:T(8,128)(2,1)S(1)}, u32[]{:S(2)}, u32[]{:S(2)}) collective-permute-start(bf16[256,256]{1,0:T(8,128)(2,1)} %a_ref.1), channel_id=1, source_target_pairs={{0,24},{1,11},{2,26},{3,13},{4,28},{5,15},{6,30},{7,17},{8,0},{9,1... | collective-permute-start | bytes 393224 | tf_op jit(solution)/shard_map/ppermute | solution.py:255
  19.9 14.5 %collective-permute-start.1 = (bf16[256,256]{1,0:T(8,128)(2,1)S(1)}, bf16[256,256]{1,0:T(8,128)(2,1)S(1)}, u32[]{:S(2)}, u32[]{:S(2)}) collective-permute-start(bf16[256,256]{1,0:T(8,128)(2,1)S(1)} %collective-permute-done.b_ref), channel_id=1, source_target_pairs={{0,24},{1,11},{2,26},{3,13},{4,28},{5,15},{6,30},{7,17},{8,0},{9,1... | collective-permute-start | bytes 393224 | tf_op jit(solution)/shard_map/ppermute | solution.py:255
  27.4 21.5 %collective-permute-start.4 = (bf16[2,256,256]{2,1,0:T(8,128)(2,1)S(1)}, bf16[2,256,256]{2,1,0:T(8,128)(2,1)S(1)}, u32[]{:S(2)}, u32[]{:S(2)}) collective-permute-start(bf16[2,256,256]{2,1,0:T(8,128)(2,1)S(1)} %shard_map.77.a_ref), channel_id=1, source_target_pairs={{0,28},{1,5},{2,30},{3,7},{4,0},{5,9},{6,2},{7,11},{8,4},{9,13},{1... | collective-permute-start | bytes 786440 | tf_op jit(solution)/shard_map/ppermute | solution.py:255
  34.4 18.9 %collective-permute-start.6 = (bf16[2,256,256]{2,1,0:T(8,128)(2,1)S(1)}, bf16[2,256,256]{2,1,0:T(8,128)(2,1)S(1)}, u32[]{:S(2)}, u32[]{:S(2)}) collective-permute-start(bf16[2,256,256]{2,1,0:T(8,128)(2,1)S(1)} %shard_map.78.a_ref), channel_id=1, source_target_pairs={{0,28},{1,5},{2,30},{3,7},{4,0},{5,9},{6,2},{7,11},{8,4},{9,13},{1... | collective-permute-start | bytes 786440 | tf_op jit(solution)/shard_map/ppermute | solution.py:255
  47.0 29.9 %collective-permute-start.13 = (bf16[16,512,256]{2,1,0:T(8,128)(2,1)S(1)}, bf16[16,512,256]{2,1,0:T(8,128)(2,1)S(1)}, u32[]{:S(2)}, u32[]{:S(2)}) collective-permute-start(bf16[16,512,256]{2,1,0:T(8,128)(2,1)S(1)} %get-tuple-element.63), channel_id=1, source_target_pairs={{0,1},{1,0},{2,3},{3,2},{4,5},{5,4},{6,7},{7,6},{8,9},{9,8},{10,11... | collective-permute-start | bytes 12582920 | tf_op jit(solution)/shard_map/ppermute | solution.py:255
  49.0 11.3 %collective-permute-start.5 = (bf16[4,256,256]{2,1,0:T(8,128)(2,1)S(1)}, bf16[4,256,256]{2,1,0:T(8,128)(2,1)S(1)}, u32[]{:S(2)}, u32[]{:S(2)}) collective-permute-start(bf16[4,256,256]{2,1,0:T(8,128)(2,1)S(1)} %shard_map.80.a_ref.refs_0_), channel_id=1, source_target_pairs={{0,30},{1,3},{2,0},{3,5},{4,2},{5,7},{6,4},{7,9},{8,6},{9,11},{10,... | collective-permute-start | bytes 1572872 | tf_op jit(solution)/shard_map/ppermute | solution.py:255
  53.4 14.1 %collective-permute-start.9 = (bf16[4,256,256]{2,1,0:T(8,128)(2,1)S(1)}, bf16[4,256,256]{2,1,0:T(8,128)(2,1)S(1)}, u32[]{:S(2)}, u32[]{:S(2)}) collective-permute-start(bf16[4,256,256]{2,1,0:T(8,128)(2,1)S(1)} %shard_map.81.b_ref.refs_1_), channel_id=1, source_target_pairs={{0,30},{1,3},{2,0},{3,5},{4,2},{5,7},{6,4},{7,9},{8,6},{9,11},{10,... | collective-permute-start | bytes 1572872 | tf_op jit(solution)/shard_map/ppermute | solution.py:255
  60.2 9.9 %collective-permute-start.7 = (bf16[4,256,256]{2,1,0:T(8,128)(2,1)S(1)}, bf16[4,256,256]{2,1,0:T(8,128)(2,1)S(1)}, u32[]{:S(2)}, u32[]{:S(2)}) collective-permute-start(bf16[4,256,256]{2,1,0:T(8,128)(2,1)S(1)} %shard_map.80.a_ref.refs_0_), channel_id=1, source_target_pairs={{0,1},{1,0},{2,3},{3,2},{4,5},{5,4},{6,7},{7,6},{8,9},{9,8},{10,11... | collective-permute-start | bytes 1572872 | tf_op jit(solution)/shard_map/ppermute | solution.py:255
  63.2 7.0 %collective-permute-start.8 = (bf16[4,256,256]{2,1,0:T(8,128)(2,1)S(1)}, bf16[4,256,256]{2,1,0:T(8,128)(2,1)S(1)}, u32[]{:S(2)}, u32[]{:S(2)}) collective-permute-start(bf16[4,256,256]{2,1,0:T(8,128)(2,1)S(1)} %shard_map.81.b_ref.refs_1_), channel_id=1, source_target_pairs={{0,1},{1,0},{2,3},{3,2},{4,5},{5,4},{6,7},{7,6},{8,9},{9,8},{10,11... | collective-permute-start | bytes 1572872 | tf_op jit(solution)/shard_map/ppermute | solution.py:255
  65.1 6.1 %collective-permute-start.10 = (bf16[4,256,256]{2,1,0:T(8,128)(2,1)S(1)}, bf16[4,256,256]{2,1,0:T(8,128)(2,1)S(1)}, u32[]{:S(2)}, u32[]{:S(2)}) collective-permute-start(bf16[4,256,256]{2,1,0:T(8,128)(2,1)S(1)} %collective-permute-done.5.la_ref.refs_2_), channel_id=1, source_target_pairs={{0,1},{1,0},{2,3},{3,2},{4,5},{5,4},{6,7},{7,6},{8,9},{9,8},{10,11... | collective-permute-start | bytes 1572872 | tf_op jit(solution)/shard_map/ppermute | solution.py:255
  67.5 4.4 %collective-permute-start.11 = (bf16[4,256,256]{2,1,0:T(8,128)(2,1)S(1)}, bf16[4,256,256]{2,1,0:T(8,128)(2,1)S(1)}, u32[]{:S(2)}, u32[]{:S(2)}) collective-permute-start(bf16[4,256,256]{2,1,0:T(8,128)(2,1)S(1)} %collective-permute-done.9.lb_ref.refs_3_), channel_id=1, source_target_pairs={{0,1},{1,0},{2,3},{3,2},{4,5},{5,4},{6,7},{7,6},{8,9},{9,8},{10,11... | collective-permute-start | bytes 1572872 | tf_op jit(solution)/shard_map/ppermute | solution.py:255
  71.1 1.0 copy-start.1
  73.4 3.5 %collective-permute-start.12 = (bf16[256,512]{1,0:T(8,128)(2,1)S(1)}, bf16[256,512]{1,0:T(8,128)(2,1)S(1)}, u32[]{:S(2)}, u32[]{:S(2)}) collective-permute-start(bf16[256,512]{1,0:T(8,128)(2,1)S(1)} %get-tuple-element.82.pg_ref), channel_id=1, source_target_pairs={{0,1},{1,0},{2,3},{3,2},{4,5},{5,4},{6,7},{7,6},{8,9},{9,8},{10,11... | collective-permute-start | bytes 786440 | tf_op jit(solution)/shard_map/ppermute | solution.py:255
  77.6 24.7 %collective-permute-start.14 = (bf16[4,256,256]{2,1,0:T(8,128)(2,1)S(1)}, bf16[4,256,256]{2,1,0:T(8,128)(2,1)S(1)}, u32[]{:S(2)}, u32[]{:S(2)}) collective-permute-start(bf16[4,256,256]{2,1,0:T(8,128)(2,1)S(1)} %shard_map.86), channel_id=1, source_target_pairs={{0,2},{1,31},{2,4},{3,1},{4,6},{5,3},{6,8},{7,5},{8,10},{9,7},{10,... | collective-permute-start | bytes 1572872 | tf_op jit(solution)/shard_map/ppermute | solution.py:255
  84.3 22.5 %collective-permute-start.16 = (bf16[4,256,256]{2,1,0:T(8,128)(2,1)}, bf16[4,256,256]{2,1,0:T(8,128)(2,1)}, u32[]{:S(2)}, u32[]{:S(2)}) collective-permute-start(bf16[4,256,256]{2,1,0:T(8,128)(2,1)} %shard_map.87), channel_id=1, source_target_pairs={{0,2},{1,31},{2,4},{3,1},{4,6},{5,3},{6,8},{7,5},{8,10},{9,7},{10,... | collective-permute-start | bytes 1572872 | tf_op jit(solution)/shard_map/ppermute | solution.py:255
  93.9 1.6 %copy-start = (bf16[80,128,128]{2,1,0:T(8,128)(2,1)}, bf16[80,128,128]{2,1,0:T(8,128)(2,1)S(1)}, u32[]{:S(2)}) copy-start(bf16[80,128,128]{2,1,0:T(8,128)(2,1)S(1)} %shard_map.95) | copy-start | bytes 7864324
  95.5 53.3 %all-to-all-start = ((bf16[80,128,128]{2,1,0:T(8,128)(2,1)}), bf16[80,128,128]{2,1,0:T(8,128)(2,1)}, u32[]{:S(2)}, u32[]{:S(2)}) async-start(bf16[80,128,128]{2,1,0:T(8,128)(2,1)} %copy-done), calls=%async_computation | async-start | bytes 5242880 | tf_op jit(solution)/shard_map/all_to_all | solution.py:342
  102.4 10.6 %collective-permute-start.15 = (bf16[2,256,256]{2,1,0:T(8,128)(2,1)S(1)}, bf16[2,256,256]{2,1,0:T(8,128)(2,1)S(1)}, u32[]{:S(2)}, u32[]{:S(2)}) collective-permute-start(bf16[2,256,256]{2,1,0:T(8,128)(2,1)S(1)} %get-tuple-element.66), channel_id=1, source_target_pairs={{0,4},{1,29},{2,6},{3,31},{4,8},{5,1},{6,10},{7,3},{8,12},{9,5},{1... | collective-permute-start | bytes 786440 | tf_op jit(solution)/shard_map/ppermute | solution.py:255
  107.9 11.3 %collective-permute-start.19 = (bf16[2,256,256]{2,1,0:T(8,128)(2,1)S(1)}, bf16[2,256,256]{2,1,0:T(8,128)(2,1)S(1)}, u32[]{:S(2)}, u32[]{:S(2)}) collective-permute-start(bf16[2,256,256]{2,1,0:T(8,128)(2,1)S(1)} %get-tuple-element.76), channel_id=1, source_target_pairs={{0,4},{1,29},{2,6},{3,31},{4,8},{5,1},{6,10},{7,3},{8,12},{9,5},{1... | collective-permute-start | bytes 786440 | tf_op jit(solution)/shard_map/ppermute | solution.py:255
  119.3 18.7 %collective-permute-start.17 = (bf16[256,256]{1,0:T(8,128)(2,1)S(1)}, bf16[256,256]{1,0:T(8,128)(2,1)S(1)}, u32[]{:S(2)}, u32[]{:S(2)}) collective-permute-start(bf16[256,256]{1,0:T(8,128)(2,1)S(1)} %get-tuple-element.74.refs_0_), channel_id=1, source_target_pairs={{1,31},{3,1},{5,3},{7,5},{9,7},{11,9},{13,11},{15,13},{17,15},{19,... | collective-permute-start | bytes 393224 | tf_op jit(solution)/shard_map/ppermute | solution.py:255
  124.1 13.9 %collective-permute-start.18 = (bf16[256,256]{1,0:T(8,128)(2,1)S(1)}, bf16[256,256]{1,0:T(8,128)(2,1)S(1)}, u32[]{:S(2)}, u32[]{:S(2)}) collective-permute-start(bf16[256,256]{1,0:T(8,128)(2,1)S(1)} %get-tuple-element.75), channel_id=1, source_target_pairs={{0,8},{1,23},{2,10},{3,25},{4,12},{5,27},{6,14},{7,29},{8,16},{9,3... | collective-permute-start | bytes 393224 | tf_op jit(solution)/shard_map/ppermute | solution.py:255
  132.3 7.7 %collective-permute-start.21 = (bf16[256,256]{1,0:T(8,128)(2,1)S(1)}, bf16[256,256]{1,0:T(8,128)(2,1)S(1)}, u32[]{:S(2)}, u32[]{:S(2)}) collective-permute-start(bf16[256,256]{1,0:T(8,128)(2,1)S(1)} %get-tuple-element.83.base_ref), channel_id=1, source_target_pairs={{1,31},{3,1},{5,3},{7,5},{9,7},{11,9},{13,11},{15,13},{17,15},{19,... | collective-permute-start | bytes 393224 | tf_op jit(solution)/shard_map/ppermute | solution.py:255
  134.2 14.5 %collective-permute-start.22 = (bf16[256,256]{1,0:T(8,128)(2,1)S(1)}, bf16[256,256]{1,0:T(8,128)(2,1)S(1)}, u32[]{:S(2)}, u32[]{:S(2)}) collective-permute-start(bf16[256,256]{1,0:T(8,128)(2,1)S(1)} %get-tuple-element.84), channel_id=1, source_target_pairs={{0,8},{1,23},{2,10},{3,25},{4,12},{5,27},{6,14},{7,29},{8,16},{9,3... | collective-permute-start | bytes 393224 | tf_op jit(solution)/shard_map/ppermute | solution.py:255
  138.0 13.6 %collective-permute-start.20 = (bf16[256,256]{1,0:T(8,128)(2,1)S(1)}, bf16[256,256]{1,0:T(8,128)(2,1)S(1)}, u32[]{:S(2)}, u32[]{:S(2)}) collective-permute-start(bf16[256,256]{1,0:T(8,128)(2,1)S(1)} %get-tuple-element.81), channel_id=1, source_target_pairs={{0,1},{1,0},{2,3},{3,2},{4,5},{5,4},{6,7},{7,6},{8,9},{9,8},{10,11... | collective-permute-start | bytes 393224 | tf_op jit(solution)/shard_map/ppermute | solution.py:255

commit v6 on v5

--- a/solution.py
+++ b/solution.py
@@ -13,10 +13,8 @@
 MIB = 1 << 20
 BF16, F32 = jnp.bfloat16, jnp.float32
 NZ = 16
-JOIN = 80 * 10**9
+LONG = 80 * 10**9
 FIRST = 200 * 10**9
-SECOND = 0
-TURN = 10 * 10**9
 
 
 def params(mib):
@@ -41,8 +39,8 @@
     step = lax.rem(dev // 2 - z + NZ, NZ)
     chosen = (step >= NZ // 2).astype(jnp.int32)
     i = jnp.where(step < NZ // 2, step, NZ - 1 - step)
-    stream = (lax.rem(dev, 2) != chosen).astype(jnp.int32)
-    return chosen == core, 8 * lax.rem(i, 2) + 4 * stream + i // 4 + 2 * lax.rem(i // 2, 2)
+    second = (lax.rem(dev, 2) != chosen).astype(jnp.int32)
+    return chosen == core, 8 * lax.rem(i, 2) + 2 * (i // 4) + 4 * lax.rem(i // 2, 2) + second
 
 
 def in_hbm(v):
@@ -119,12 +117,12 @@
         use(core_1_ref)
 
 
-def join_base(stream, pair_ref, hop_ref, g4_ref, out_ref):
+def join_base(pair_ref, hop_ref, g4_ref, out_ref):
     def put(ref):
-        out_ref[0] = ref[stream]
+        out_ref[:2] = ref[...]
 
     chosen_base(pair_ref, hop_ref, put)
-    out_ref[1] = g4_ref[...]
+    out_ref[2:] = g4_ref[...]
 
 
 def join(a_ref, b_ref, out_ref):
@@ -142,20 +140,16 @@
     return jnp.dot(x, up_ref[first * feats : (first + len(parts)) * feats], preferred_element_type=F32)
 
 
-def forward_early(a_ref, b_ref, up_ref, out_ref):
-    out_ref[...] = times(up_ref, 0, a_ref, b_ref)
-
-
-def forward_next(so_far, la_ref, a_ref, b_ref, up_ref, out_ref):
-    out_ref[...] = so_far[...] + times(up_ref, 8, la_ref) + times(up_ref, 16, a_ref, b_ref)
-
-
-def forward_late(so_far, lb_ref, la_ref, up_ref, out_ref):
-    out_ref[...] = so_far[...] + times(up_ref, 12, lb_ref) + times(up_ref, 24, la_ref)
-
-
-def forward_last(so_far, lb_ref, up_ref, og_ref, act_ref, pg_ref):
-    hidden = so_far[...] + times(up_ref, 28, lb_ref)
+def forward_first(x_ref, up_ref, out_ref):
+    out_ref[...] = times(up_ref, 0, x_ref)
+
+
+def forward_more(place, so_far, x_ref, up_ref, out_ref):
+    out_ref[...] = so_far[...] + times(up_ref, place, x_ref)
+
+
+def forward_last(so_far, x_ref, up_ref, og_ref, act_ref, pg_ref):
+    hidden = so_far[...] + times(up_ref, 24, x_ref)
     sig = jax.nn.sigmoid(hidden)
     act_ref[...] = (hidden * sig).astype(BF16)
     pg_ref[...] = (og_ref[...].astype(F32) * sig * (1.0 + hidden * (1.0 - sig))).astype(BF16)
@@ -174,18 +168,20 @@
 
 
 def add_first(d_ref, r1_ref, out_ref):
+    for n in range(4):
+        out_ref[n] = (d_ref[4 + n] + f32(r1_ref[4 + n])).astype(BF16)
+
+
+def add_second(d_ref, r1_ref, r2_ref, next_ref, base_ref):
     for n in range(2):
-        out_ref[n] = (d_ref[2 + n] + f32(r1_ref[2 + n])).astype(BF16)
-
-
-def add_second(d_ref, r1_ref, r2_ref, next_ref, base_ref):
-    for n, out_ref in enumerate((base_ref, next_ref)):
-        out_ref[...] = (d_ref[n] + f32(r1_ref[n]) + f32(r2_ref[n])).astype(BF16)
-
-
-def add_cross(base_ref, hop_ref, r3_ref, out_ref):
+        base_ref[n] = (d_ref[n] + f32(r1_ref[n]) + f32(r2_ref[n])).astype(BF16)
+        next_ref[n] = (d_ref[2 + n] + f32(r1_ref[2 + n]) + f32(r2_ref[2 + n])).astype(BF16)
+
+
+def add_third(base_ref, hop_ref, r3_ref, cross_ref, own_ref):
     def put(ref):
-        out_ref[...] = (f32(ref[...]) + f32(r3_ref[...])).astype(out_ref.dtype)
+        cross_ref[...] = (f32(ref[1]) + f32(r3_ref[1])).astype(BF16)
+        own_ref[...] = f32(ref[0]) + f32(r3_ref[0])
 
     chosen_base(base_ref, hop_ref, put)
 
@@ -270,21 +266,11 @@
     def shards(n, dtype=BF16):
         return shape(n, tok_rows, feats, dtype=dtype)
 
-    g4a = steps(tokens, -4, -5)
     theirs = other_core(tokens)
-    g4b = steps(theirs, -4, -5)
-    pair = kernel(pair_up, shards(2), n_in=2)(tokens, theirs)
+    pair = kernel(pair_up, shards(2), n_in=2, size=0)(tokens, theirs)
+    g4 = steps(pair, -4, -5)
     base = hop(pair, 1)
-
-    def based(n, g):
-        return kernel(functools.partial(join_base, n), shards(2), n_in=3, flops=n * JOIN, size=0)(pair, base, g)
-
-    g04a = based(0, g4a)
-    g26a = steps(g04a, -2)
-    g4b, g04a = together((g4b, g04a))
-    g04b = based(1, g4b)
-    g26b = steps(g04b, -2)
-    g04b, listed = together((g04b, listed))
+    pair, listed = together((pair, listed))
     up_w, down_w, down_other = kernel(
         lay_weights,
         (shape(2 * NZ * feats, width),) + (shape(NZ, width, feats),) * 2,
@@ -294,84 +280,61 @@
             pltpu.VMEM((slots, blk, blk), BF16), pltpu.SemaphoreType.DMA((3,)),
         ],
     )(in_hbm(listed), in_hbm(cut), in_hbm(up_blocks[0]))
-    g26a, g04b, up_w = together((g26a, g04b, up_w))
+    g4, up_w = together((g4, up_w))
+    g04 = kernel(join_base, shards(4), n_in=3, size=0)(pair, base, g4)
+    g26 = steps(g04, -2)
+    early = kernel(join, shards(8), n_in=2, size=0)(g04, g26)
+    late = steps(early, -1)
+    early, down_other = together((early, down_other))
+    early_other = other_core(early)
     down_sibling = other_core(down_other)
-    ea = kernel(join, shards(4), n_in=2, size=0)(g04a, g26a)
-    la = steps(ea, -1)
-    g26b, ea = together((g26b, ea))
-    eb = kernel(join, shards(4), n_in=2, flops=JOIN, size=0)(g04b, g26b)
-    lb = steps(eb, -1)
-    la, ea, eb = together((la, ea, eb))
-    ea2, eb2 = other_core(ea), other_core(eb)
 
     hidden_shape = shape(tok_rows, width, dtype=F32)
 
-    def more(body, *operands):
-        return kernel(body, hidden_shape, n_in=len(operands), size=0)(*operands)
-
-    hidden = more(forward_early, ea, eb, up_w)
-    la2 = other_core(la)
-    hidden = more(forward_next, hidden, la, ea2, eb2, up_w)
-    lb2 = other_core(lb)
-    hidden = more(forward_late, hidden, lb, la2, up_w)
+    def more(body, *operands, flops=0):
+        return kernel(body, hidden_shape, n_in=len(operands), flops=flops, size=0)(*operands)
+
+    hidden = more(forward_first, early, up_w)
+    late, hidden = together((late, hidden))
+    late_other = other_core(late)
+    hidden = more(functools.partial(forward_more, 8), hidden, late, up_w, flops=LONG)
+    hidden = more(functools.partial(forward_more, 16), hidden, early_other, up_w)
     act, pg = kernel(forward_last, (shape(tok_rows, width),) * 2, n_in=4, flops=flops_of(4), size=4 * MIB)(
-        hidden, lb2, up_w, out_grad
+        hidden, late_other, up_w, out_grad
     )
     pg2 = other_core(pg)
 
     def back_of(first, dtype):
-        return kernel(functools.partial(back, first), shards(4, dtype), n_in=4, flops=flops_of(8), size=4 * MIB)(
+        return kernel(functools.partial(back, first), shards(8, dtype), n_in=4, flops=flops_of(8), size=4 * MIB)(
             pg, pg2, down_w, down_sibling
         )
 
-    d1b = back_of(12, BF16)
-    r1b = steps(d1b, 1)
-    pg, d1b = together((pg, d1b))
-    d1a = back_of(8, BF16)
-    r1a = steps(d1a, 1)
-    d2b, d2a = back_of(4, F32), back_of(0, F32)
-    pg, d1a, d2b, d2a = together((pg, d1a, d2b, d2a))
+    d1 = back_of(8, BF16)
+    r1 = steps(d1, 1)
+    pg, d1 = together((pg, d1))
+    d2 = back_of(0, F32)
+    pg, d2 = together((pg, d2))
     terms = kernel(
-        weight_terms, shape(slots, blk, blk), ins=[HBM], n_in=9, mib=14,
+        weight_terms, shape(slots, blk, blk), ins=[HBM], n_in=5, mib=14,
         flops=flops_of(32), size=16 * MIB,
         scratch=[
             pltpu.SMEM(listed.shape, jnp.int32), pltpu.VMEM((width, tok_rows), BF16),
             pltpu.VMEM((2 * NZ, width, feats), BF16), pltpu.SemaphoreType.DMA,
         ],
-    )(in_hbm(listed), pg, ea, eb, la, lb, ea2, eb2, la2, lb2)
+    )(in_hbm(listed), pg, early, late, early_other, late_other)
     got = lax.all_to_all(terms, "dp", 0, 0, tiled=True)
-    def in_turn(body, out, turn, *operands, flops=0):
-        n = len(operands)
-
-        def ordered(*refs):
-            body(*refs[:n], *refs[n + 1 : -1])
-            refs[-1][...] = refs[n][...]
-
-        return kernel(ordered, out + (shape(8, blk, dtype=F32),), n_in=n + 1, flops=flops, size=0)(*operands, turn)
-
-    one = shape(tok_rows, feats)
-    turn = jnp.zeros((8, blk), F32)
-    q, turn = in_turn(add_first, (shards(2),), turn, d2b, r1b, flops=FIRST)
-    r2b = steps(q, 2)
-    r1a, turn = together((r1a, turn))
-    q, turn = in_turn(add_first, (shards(2),), turn, d2a, r1a, flops=SECOND)
-    r2a = steps(q, 2)
-    r2b, turn = together((r2b, turn))
-    q, sum_b, turn = in_turn(add_second, (one, one), turn, d2b, r1b, r2b)
-    r3b = steps(q, 4, 5)
-    moved_b = hop(sum_b, -1)
-    r2a, turn = together((r2a, turn))
-    q, sum_a, turn = in_turn(add_second, (one, one), turn, d2a, r1a, r2a, flops=SECOND)
-    r3a = steps(q, 4, 5)
-    moved_a = hop(sum_a, -1)
-    q, turn = in_turn(add_cross, (one,), turn, sum_b, moved_b, r3b)
-    cross = other_core(q)
+
+    r2 = steps(kernel(add_first, shards(4), n_in=2, flops=FIRST, size=0)(d2, r1), 2)
+    q, sums = kernel(add_second, (shards(2),) * 2, n_in=3, size=0)(d2, r1, r2)
+    r3 = steps(q, 4, 5)
+    moved = hop(sums, -1)
     own_grads = kernel(
         functools.partial(add_terms, 1.0 / (tok_rows * n_dp) ** 0.5), shape(per, blk, blk, dtype=F32), size=0
     )(got.reshape(n_dp, per, blk, blk))
-    total = kernel(add_cross, shape(tok_rows, feats, dtype=F32), n_in=3, flops=TURN, size=0)(sum_a, moved_a, r3a)
-    cross, own_grads, total, turn = together((cross, own_grads, total, turn))
-    in_grad, _ = in_turn(add_last, (one,), turn, total, cross)
+    r3, moved, own_grads = together((r3, moved, own_grads))
+    one = shape(tok_rows, feats)
+    cross, total = kernel(add_third, (one, shape(tok_rows, feats, dtype=F32)), n_in=3, size=0)(sums, moved, r3)
+    in_grad = kernel(add_last, one, n_in=2, size=0)(total, other_core(cross))
     return act, in_grad, own_grads[None]
 
 

time: 153 us -> 145 us (0.948)
  starting transfers between devices: 101 us -> 57.4 us
  waiting for transfers between devices: 22.1 us -> 58.4 us
    ppermute x23 -> x14, starting transfers between devices: 94 us -> 50.7 us  [send(): return lax.ppermute(v, 'blk', pairs)]
    ppermute x23 -> x14, waiting for transfers between devices: 22.1 us -> 50.8 us  [send(): return lax.ppermute(v, 'blk', pairs)]
    all_to_all x1, waiting for transfers between devices: 0.01 us -> 7.58 us  [on_device(): got = lax.all_to_all(terms, 'dp', 0, 0, tiled=True)]
    pallas_call x20 -> x13, Pallas kernels: 14.9 us -> 13 us  [the longest x1 5.69 us: on_device(): kernel(weight_terms, shape(slots, blk, blk), ins=[HBM], n_in=5, mib=14, f...]
    pallas_call x1, Pallas kernels: 6.61 us -> 8.26 us  [on_device(): kernel(lay_weights, (shape(2 * NZ * feats, width),) + (shape(NZ, width, f...]
  transfers between devices with their start and end apart: 24 -> 15, of which waited for: 6 -> 11; matrix products, arithmetic and copies ran while one was open for 0% -> 0% of each run, Pallas kernels for 16% -> 16%
where the time goes in v6:
time: 145 us
  waiting for transfers between devices  58.4 us (40%)
  starting transfers between devices  57.4 us (40%)
  Pallas kernels  25.7 us (18%)
  local copies, waits for them, and re-layouts  2.44 us (2%)
    ppermute x14, waiting for transfers between devices, send(): return lax.ppermute(v, 'blk', pairs)  50.8 us
    ppermute x14, starting transfers between devices, send(): return lax.ppermute(v, 'blk', pairs)  50.7 us
    pallas_call x1, Pallas kernels, on_device(): kernel(lay_weights, (shape(2 * NZ * feats, width),) + (shape(NZ, width, f...  8.26 us
    all_to_all x1, waiting for transfers between devices, on_device(): got = lax.all_to_all(terms, 'dp', 0, 0, tiled=True)  7.58 us
    all_to_all x1, starting transfers between devices, on_device(): got = lax.all_to_all(terms, 'dp', 0, 0, tiled=True)  6.7 us
    pallas_call x1, Pallas kernels, on_device(): kernel(weight_terms, shape(slots, blk, blk), ins=[HBM], n_in=5, mib=14, f...  5.69 us
    pallas_call x2, Pallas kernels, back_of(): kernel(functools.partial(back, first), shards(8, dtype), n_in=4, flops=fl...  3.5 us
  transfers between devices with their start and end apart: 15, of which 11 were waited for; matrix products, arithmetic and copies ran while one was open for 0% of the time, Pallas kernels for 16%

profile of v6, /device:TPU:1, one launch (start us, length us, event | category | flops | bytes accessed | tf_op | source)
XLA Modules:
  0.0 144.8 jit_solution(16739228504720240379)
XLA Ops:
  0.6 8.8 %collective-permute-start = (bf16[256,256]{1,0:T(8,128)(2,1)}, bf16[256,256]{1,0:T(8,128)(2,1)S(1)}, u32[]{:S(2)}, u32[]{:S(2)}) collective-permute-start(bf16[256,256]{1,0:T(8,128)(2,1)} %a_ref.1), channel_id=1, source_target_pairs={{0,1},{1,0},{2,3},{3,2},{4,5},{5,4},{6,7},{7,6},{8,9},{9,8},{10,11... | collective-permute-start | bytes 393224 | tf_op jit(solution)/shard_map/ppermute | solution.py:251
  9.4 1.2 collective-permute-done.b_ref
  10.6 0.9 copy-done.2
  11.5 4.8 %collective-permute-start.2 = (bf16[2,256,256]{2,1,0:T(8,128)(2,1)S(1)}, bf16[2,256,256]{2,1,0:T(8,128)(2,1)S(1)}, u32[]{:S(2)}, u32[]{:S(2)}) collective-permute-start(bf16[2,256,256]{2,1,0:T(8,128)(2,1)S(1)} %shard_map.76.pair_ref), channel_id=1, source_target_pairs={{0,24},{1,11},{2,26},{3,13},{4,28},{5,15},{6,30},{7,17},{8,0},{9,1... | collective-permute-start | bytes 786440 | tf_op jit(solution)/shard_map/ppermute | solution.py:251
  16.3 3.5 %collective-permute-start.1 = (bf16[2,256,256]{2,1,0:T(8,128)(2,1)S(1)}, bf16[2,256,256]{2,1,0:T(8,128)(2,1)S(1)}, u32[]{:S(2)}, u32[]{:S(2)}) collective-permute-start(bf16[2,256,256]{2,1,0:T(8,128)(2,1)S(1)} %shard_map.76.pair_ref), channel_id=1, source_target_pairs={{1,3},{3,5},{5,7},{7,9},{9,11},{11,13},{13,15},{15,17},{17,19},{19... | collective-permute-start | bytes 786440 | tf_op jit(solution)/shard_map/ppermute | solution.py:251
  19.9 8.3 %shard_map.77 = (bf16[8192,512]{1,0:T(8,128)(2,1)S(1)}, bf16[16,512,256]{2,1,0:T(8,128)(2,1)S(1)}, bf16[16,512,256]{2,1,0:T(8,128)(2,1)S(1)}) custom-call(s32[2,80]{1,0:T(2,128)} %bitcast.10, s32[2,32]{1,0:T(2,128)} %bitcast.9, bf16[80,128,128]{2,1,0:T(8,128)(2,1)} %bitcast.7), custom_call_target="tpu_custom_call" | custom-call | bytes 20971520 | tf_op jit(solution)/shard_map/pallas_call | solution.py:274
  28.2 0.2 collective-permute-done.2.g4_ref
  28.3 6.9 %collective-permute-done.1.hop_ref = bf16[2,256,256]{2,1,0:T(8,128)(2,1)S(1)} collective-permute-done((bf16[2,256,256]{2,1,0:T(8,128)(2,1)S(1)}, bf16[2,256,256]{2,1,0:T(8,128)(2,1)S(1)}, u32[]{:S(2)}, u32[]{:S(2)}) %collective-permute-start.1) | collective-permute-done | bytes 262176 | tf_op jit(solution)/shard_map/ppermute | solution.py:251
  35.3 3.2 %collective-permute-start.3 = (bf16[4,256,256]{2,1,0:T(8,128)(2,1)S(1)}, bf16[4,256,256]{2,1,0:T(8,128)(2,1)S(1)}, u32[]{:S(2)}, u32[]{:S(2)}) collective-permute-start(bf16[4,256,256]{2,1,0:T(8,128)(2,1)S(1)} %shard_map.78.a_ref), channel_id=1, source_target_pairs={{0,28},{1,5},{2,30},{3,7},{4,0},{5,9},{6,2},{7,11},{8,4},{9,13},{1... | collective-permute-start | bytes 1572872 | tf_op jit(solution)/shard_map/ppermute | solution.py:251
  38.5 13.7 %collective-permute-done.3.b_ref = bf16[4,256,256]{2,1,0:T(8,128)(2,1)S(1)} collective-permute-done((bf16[4,256,256]{2,1,0:T(8,128)(2,1)S(1)}, bf16[4,256,256]{2,1,0:T(8,128)(2,1)S(1)}, u32[]{:S(2)}, u32[]{:S(2)}) %collective-permute-start.3) | collective-permute-done | bytes 524320 | tf_op jit(solution)/shard_map/ppermute | solution.py:251
  52.2 0.1 shard_map.79.x_ref.refs_0_
  52.3 1.9 %collective-permute-start.4 = (bf16[8,256,256]{2,1,0:T(8,128)(2,1)S(1)}, bf16[8,256,256]{2,1,0:T(8,128)(2,1)S(1)}, u32[]{:S(2)}, u32[]{:S(2)}) collective-permute-start(bf16[8,256,256]{2,1,0:T(8,128)(2,1)S(1)} %shard_map.79.x_ref.refs_0_), channel_id=1, source_target_pairs={{0,30},{1,3},{2,0},{3,5},{4,2},{5,7},{6,4},{7,9},{8,6},{9,11},{10,... | collective-permute-start | bytes 3145736 | tf_op jit(solution)/shard_map/ppermute | solution.py:251
  54.2 2.0 %collective-permute-start.5 = (bf16[8,256,256]{2,1,0:T(8,128)(2,1)S(1)}, bf16[8,256,256]{2,1,0:T(8,128)(2,1)S(1)}, u32[]{:S(2)}, u32[]{:S(2)}) collective-permute-start(bf16[8,256,256]{2,1,0:T(8,128)(2,1)S(1)} %shard_map.79.x_ref.refs_0_), channel_id=1, source_target_pairs={{0,1},{1,0},{2,3},{3,2},{4,5},{5,4},{6,7},{7,6},{8,9},{9,8},{10,11... | collective-permute-start | bytes 3145736 | tf_op jit(solution)/shard_map/ppermute | solution.py:251
  56.2 0.7 shard_map.80.so_far
  56.9 2.3 %collective-permute-start.8 = (bf16[16,512,256]{2,1,0:T(8,128)(2,1)S(1)}, bf16[16,512,256]{2,1,0:T(8,128)(2,1)S(1)}, u32[]{:S(2)}, u32[]{:S(2)}) collective-permute-start(bf16[16,512,256]{2,1,0:T(8,128)(2,1)S(1)} %get-tuple-element.38), channel_id=1, source_target_pairs={{0,1},{1,0},{2,3},{3,2},{4,5},{5,4},{6,7},{7,6},{8,9},{9,8},{10,11... | collective-permute-start | bytes 12582920 | tf_op jit(solution)/shard_map/ppermute | solution.py:251
  59.3 9.8 %collective-permute-done.4.x_ref.refs_1_ = bf16[8,256,256]{2,1,0:T(8,128)(2,1)S(1)} collective-permute-done((bf16[8,256,256]{2,1,0:T(8,128)(2,1)S(1)}, bf16[8,256,256]{2,1,0:T(8,128)(2,1)S(1)}, u32[]{:S(2)}, u32[]{:S(2)}) %collective-permute-start.4) | collective-permute-done | bytes 1048608 | tf_op jit(solution)/shard_map/ppermute | solution.py:251
  69.0 1.9 %collective-permute-start.6 = (bf16[8,256,256]{2,1,0:T(8,128)(2,1)S(1)}, bf16[8,256,256]{2,1,0:T(8,128)(2,1)S(1)}, u32[]{:S(2)}, u32[]{:S(2)}) collective-permute-start(bf16[8,256,256]{2,1,0:T(8,128)(2,1)S(1)} %collective-permute-done.4.x_ref.refs_1_), channel_id=1, source_target_pairs={{0,1},{1,0},{2,3},{3,2},{4,5},{5,4},{6,7},{7,6},{8,9},{9,8},{10,11... | collective-permute-start | bytes 3145736 | tf_op jit(solution)/shard_map/ppermute | solution.py:251
  71.0 0.7 shard_map.81.so_far
  71.7 0.0 copy-start.1
  71.7 0.0 collective-permute-done.5.x_ref.refs_2_
  71.7 0.7 shard_map.82.so_far
  72.4 1.2 collective-permute-done.6.x_ref.refs_3_
  73.6 0.0 copy-done.1
  73.6 1.5 %shard_map.83 = (bf16[256,512]{1,0:T(8,128)(2,1)}, bf16[256,512]{1,0:T(8,128)(2,1)S(1)}) custom-call(f32[256,512]{1,0:T(8,128)S(1)} %shard_map.82.so_far, bf16[8,256,256]{2,1,0:T(8,128)(2,1)S(1)} %collective-permute-done.6.x_ref.refs_3_, bf16[8192,512]{1,0:T(8,128)(2,1)S(1)} %get-tuple-element.32.up_ref, bf16[256,512]{1,0:T(8,128)(2,1)S(1)} %copy-done.1), custom_call_target="tpu_custom_call" | custom-call | flops 268435456 | bytes 4194304 | tf_op jit(solution)/shard_map/pallas_call | solution.py:302
  75.1 2.0 %collective-permute-start.7 = (bf16[256,512]{1,0:T(8,128)(2,1)S(1)}, bf16[256,512]{1,0:T(8,128)(2,1)S(1)}, u32[]{:S(2)}, u32[]{:S(2)}) collective-permute-start(bf16[256,512]{1,0:T(8,128)(2,1)S(1)} %get-tuple-element.43.pg_ref), channel_id=1, source_target_pairs={{0,1},{1,0},{2,3},{3,2},{4,5},{5,4},{6,7},{7,6},{8,9},{9,8},{10,11... | collective-permute-start | bytes 786440 | tf_op jit(solution)/shard_map/ppermute | solution.py:251
  77.2 1.4 collective-permute-done.7.pg2_ref
  78.5 0.0 collective-permute-done.8.sibling_ref
  78.5 2.2 %shard_map.84 = bf16[8,256,256]{2,1,0:T(8,128)(2,1)} custom-call(bf16[256,512]{1,0:T(8,128)(2,1)S(1)} %get-tuple-element.43.pg_ref, bf16[256,512]{1,0:T(8,128)(2,1)S(1)} %collective-permute-done.7.pg2_ref, bf16[16,512,256]{2,1,0:T(8,128)(2,1)S(1)} %get-tuple-element.37.own_ref, bf16[16,512,256]{2,1,0:T(8,128)(2,1)S(1)} %collective-permute-done.8.sibling_ref), custom_call_target="tpu_custom_call" | custom-call | flops 536870912 | bytes 4194304 | tf_op jit(solution)/shard_map/pallas_call | solution.py:308
  80.8 2.7 %collective-permute-start.9 = (bf16[8,256,256]{2,1,0:T(8,128)(2,1)}, bf16[8,256,256]{2,1,0:T(8,128)(2,1)S(1)}, u32[]{:S(2)}, u32[]{:S(2)}) collective-permute-start(bf16[8,256,256]{2,1,0:T(8,128)(2,1)} %shard_map.84), channel_id=1, source_target_pairs={{0,2},{1,31},{2,4},{3,1},{4,6},{5,3},{6,8},{7,5},{8,10},{9,7},{10,... | collective-permute-start | bytes 3145736 | tf_op jit(solution)/shard_map/ppermute | solution.py:251
  83.5 1.2 shard_map.85.d_ref
  84.8 5.7 %shard_map.88 = bf16[80,128,128]{2,1,0:T(8,128)(2,1)S(1)} custom-call(s32[2,80]{1,0:T(2,128)} %bitcast.11, bf16[256,512]{1,0:T(8,128)(2,1)S(1)} %get-tuple-element.43.pg_ref, bf16[8,256,256]{2,1,0:T(8,128)(2,1)S(1)} %shard_map.79.x_ref.refs_0_, bf16[8,256,256]{2,1,0:T(8,128)(2,1)S(1)} %collective-permute-done.4.x_ref.refs_1_, ...), custom_call_target="tpu_custom_call" | custom-call | flops 2147483648 | bytes 16777216 | tf_op jit(solution)/shard_map/pallas_call | solution.py:317
  90.5 1.5 %copy-done = bf16[80,128,128]{2,1,0:T(8,128)(2,1)} copy-done((bf16[80,128,128]{2,1,0:T(8,128)(2,1)}, bf16[80,128,128]{2,1,0:T(8,128)(2,1)S(1)}, u32[]{:S(2)}) %copy-start) | copy-done | bytes 2621464
  92.0 6.7 %all-to-all-start = ((bf16[80,128,128]{2,1,0:T(8,128)(2,1)}), bf16[80,128,128]{2,1,0:T(8,128)(2,1)}, u32[]{:S(2)}, u32[]{:S(2)}) async-start(bf16[80,128,128]{2,1,0:T(8,128)(2,1)} %copy-done), calls=%async_computation | async-start | bytes 5242880 | tf_op jit(solution)/shard_map/all_to_all | solution.py:325
  98.7 0.0 collective-permute-done.9.r1_ref
  98.7 0.1 shard_map.86
  98.8 3.6 %collective-permute-start.10 = (bf16[4,256,256]{2,1,0:T(8,128)(2,1)S(1)}, bf16[4,256,256]{2,1,0:T(8,128)(2,1)S(1)}, u32[]{:S(2)}, u32[]{:S(2)}) collective-permute-start(bf16[4,256,256]{2,1,0:T(8,128)(2,1)S(1)} %shard_map.86), channel_id=1, source_target_pairs={{0,4},{1,29},{2,6},{3,31},{4,8},{5,1},{6,10},{7,3},{8,12},{9,5},{1... | collective-permute-start | bytes 1572872 | tf_op jit(solution)/shard_map/ppermute | solution.py:251
  102.5 12.6 %collective-permute-done.10.r2_ref = bf16[4,256,256]{2,1,0:T(8,128)(2,1)S(1)} collective-permute-done((bf16[4,256,256]{2,1,0:T(8,128)(2,1)S(1)}, bf16[4,256,256]{2,1,0:T(8,128)(2,1)S(1)}, u32[]{:S(2)}, u32[]{:S(2)}) %collective-permute-start.10) | collective-permute-done | bytes 524320 | tf_op jit(solution)/shard_map/ppermute | solution.py:251
  115.1 0.8 shard_map.87
  115.9 8.6 %collective-permute-start.11 = (bf16[2,256,256]{2,1,0:T(8,128)(2,1)}, bf16[2,256,256]{2,1,0:T(8,128)(2,1)S(1)}, u32[]{:S(2)}, u32[]{:S(2)}) collective-permute-start(bf16[2,256,256]{2,1,0:T(8,128)(2,1)} %get-tuple-element.42), channel_id=1, source_target_pairs={{0,8},{1,23},{2,10},{3,25},{4,12},{5,27},{6,14},{7,29},{8,16},{9,3... | collective-permute-start | bytes 786440 | tf_op jit(solution)/shard_map/ppermute | solution.py:251
  124.4 3.3 %collective-permute-start.12 = (bf16[2,256,256]{2,1,0:T(8,128)(2,1)S(1)}, bf16[2,256,256]{2,1,0:T(8,128)(2,1)S(1)}, u32[]{:S(2)}, u32[]{:S(2)}) collective-permute-start(bf16[2,256,256]{2,1,0:T(8,128)(2,1)S(1)} %get-tuple-element.41.base_ref), channel_id=1, source_target_pairs={{1,31},{3,1},{5,3},{7,5},{9,7},{11,9},{13,11},{15,13},{17,15},{19,... | collective-permute-start | bytes 786440 | tf_op jit(solution)/shard_map/ppermute | solution.py:251
  127.8 7.6 %all-to-all-done = bf16[80,128,128]{2,1,0:T(8,128)(2,1)} async-done(((bf16[80,128,128]{2,1,0:T(8,128)(2,1)}), bf16[80,128,128]{2,1,0:T(8,128)(2,1)}, u32[]{:S(2)}, u32[]{:S(2)}) %all-to-all-start) | async-done | bytes 2621472 | tf_op jit(solution)/shard_map/all_to_all | solution.py:325
  135.3 2.9 %shard_map.89 = f32[5,128,128]{2,1,0:T(8,128)} custom-call(bf16[16,5,128,128]{3,2,1,0:T(8,128)(2,1)} %bitcast.4.in_ref), custom_call_target="tpu_custom_call" | custom-call | tf_op jit(solution)/shard_map/pallas_call | solution.py:331
  138.2 0.0 collective-permute-done.11.r3_ref
  138.2 2.6 %collective-permute-done.12.hop_ref = bf16[2,256,256]{2,1,0:T(8,128)(2,1)S(1)} collective-permute-done((bf16[2,256,256]{2,1,0:T(8,128)(2,1)S(1)}, bf16[2,256,256]{2,1,0:T(8,128)(2,1)S(1)}, u32[]{:S(2)}, u32[]{:S(2)}) %collective-permute-start.12) | collective-permute-done | bytes 262176 | tf_op jit(solution)/shard_map/ppermute | solution.py:251
  140.8 0.1 shard_map.90
  140.8 1.9 %collective-permute-start.13 = (bf16[256,256]{1,0:T(8,128)(2,1)S(1)}, bf16[256,256]{1,0:T(8,128)(2,1)S(1)}, u32[]{:S(2)}, u32[]{:S(2)}) collective-permute-start(bf16[256,256]{1,0:T(8,128)(2,1)S(1)} %get-tuple-element.47), channel_id=1, source_target_pairs={{0,1},{1,0},{2,3},{3,2},{4,5},{5,4},{6,7},{7,6},{8,9},{9,8},{10,11... | collective-permute-start | bytes 393224 | tf_op jit(solution)/shard_map/ppermute | solution.py:251
  142.8 1.3 collective-permute-done.13.cross_ref
  144.1 0.7 shard_map.91
  (4 shorter events, 0.1 us)
Async XLA Ops:
  0.6 10.0 %collective-permute-start = (bf16[256,256]{1,0:T(8,128)(2,1)}, bf16[256,256]{1,0:T(8,128)(2,1)S(1)}, u32[]{:S(2)}, u32[]{:S(2)}) collective-permute-start(bf16[256,256]{1,0:T(8,128)(2,1)} %a_ref.1), channel_id=1, source_target_pairs={{0,1},{1,0},{2,3},{3,2},{4,5},{5,4},{6,7},{7,6},{8,9},{9,8},{10,11... | collective-permute-start | bytes 393224 | tf_op jit(solution)/shard_map/ppermute | solution.py:251
  10.6 0.9 copy-start.2
  11.5 16.8 %collective-permute-start.2 = (bf16[2,256,256]{2,1,0:T(8,128)(2,1)S(1)}, bf16[2,256,256]{2,1,0:T(8,128)(2,1)S(1)}, u32[]{:S(2)}, u32[]{:S(2)}) collective-permute-start(bf16[2,256,256]{2,1,0:T(8,128)(2,1)S(1)} %shard_map.76.pair_ref), channel_id=1, source_target_pairs={{0,24},{1,11},{2,26},{3,13},{4,28},{5,15},{6,30},{7,17},{8,0},{9,1... | collective-permute-start | bytes 786440 | tf_op jit(solution)/shard_map/ppermute | solution.py:251
  16.3 18.9 %collective-permute-start.1 = (bf16[2,256,256]{2,1,0:T(8,128)(2,1)S(1)}, bf16[2,256,256]{2,1,0:T(8,128)(2,1)S(1)}, u32[]{:S(2)}, u32[]{:S(2)}) collective-permute-start(bf16[2,256,256]{2,1,0:T(8,128)(2,1)S(1)} %shard_map.76.pair_ref), channel_id=1, source_target_pairs={{1,3},{3,5},{5,7},{7,9},{9,11},{11,13},{13,15},{15,17},{17,19},{19... | collective-permute-start | bytes 786440 | tf_op jit(solution)/shard_map/ppermute | solution.py:251
  35.3 16.9 %collective-permute-start.3 = (bf16[4,256,256]{2,1,0:T(8,128)(2,1)S(1)}, bf16[4,256,256]{2,1,0:T(8,128)(2,1)S(1)}, u32[]{:S(2)}, u32[]{:S(2)}) collective-permute-start(bf16[4,256,256]{2,1,0:T(8,128)(2,1)S(1)} %shard_map.78.a_ref), channel_id=1, source_target_pairs={{0,28},{1,5},{2,30},{3,7},{4,0},{5,9},{6,2},{7,11},{8,4},{9,13},{1... | collective-permute-start | bytes 1572872 | tf_op jit(solution)/shard_map/ppermute | solution.py:251
  52.3 16.8 %collective-permute-start.4 = (bf16[8,256,256]{2,1,0:T(8,128)(2,1)S(1)}, bf16[8,256,256]{2,1,0:T(8,128)(2,1)S(1)}, u32[]{:S(2)}, u32[]{:S(2)}) collective-permute-start(bf16[8,256,256]{2,1,0:T(8,128)(2,1)S(1)} %shard_map.79.x_ref.refs_0_), channel_id=1, source_target_pairs={{0,30},{1,3},{2,0},{3,5},{4,2},{5,7},{6,4},{7,9},{8,6},{9,11},{10,... | collective-permute-start | bytes 3145736 | tf_op jit(solution)/shard_map/ppermute | solution.py:251
  54.2 17.5 %collective-permute-start.5 = (bf16[8,256,256]{2,1,0:T(8,128)(2,1)S(1)}, bf16[8,256,256]{2,1,0:T(8,128)(2,1)S(1)}, u32[]{:S(2)}, u32[]{:S(2)}) collective-permute-start(bf16[8,256,256]{2,1,0:T(8,128)(2,1)S(1)} %shard_map.79.x_ref.refs_0_), channel_id=1, source_target_pairs={{0,1},{1,0},{2,3},{3,2},{4,5},{5,4},{6,7},{7,6},{8,9},{9,8},{10,11... | collective-permute-start | bytes 3145736 | tf_op jit(solution)/shard_map/ppermute | solution.py:251
  56.9 21.6 %collective-permute-start.8 = (bf16[16,512,256]{2,1,0:T(8,128)(2,1)S(1)}, bf16[16,512,256]{2,1,0:T(8,128)(2,1)S(1)}, u32[]{:S(2)}, u32[]{:S(2)}) collective-permute-start(bf16[16,512,256]{2,1,0:T(8,128)(2,1)S(1)} %get-tuple-element.38), channel_id=1, source_target_pairs={{0,1},{1,0},{2,3},{3,2},{4,5},{5,4},{6,7},{7,6},{8,9},{9,8},{10,11... | collective-permute-start | bytes 12582920 | tf_op jit(solution)/shard_map/ppermute | solution.py:251
  69.0 4.5 %collective-permute-start.6 = (bf16[8,256,256]{2,1,0:T(8,128)(2,1)S(1)}, bf16[8,256,256]{2,1,0:T(8,128)(2,1)S(1)}, u32[]{:S(2)}, u32[]{:S(2)}) collective-permute-start(bf16[8,256,256]{2,1,0:T(8,128)(2,1)S(1)} %collective-permute-done.4.x_ref.refs_1_), channel_id=1, source_target_pairs={{0,1},{1,0},{2,3},{3,2},{4,5},{5,4},{6,7},{7,6},{8,9},{9,8},{10,11... | collective-permute-start | bytes 3145736 | tf_op jit(solution)/shard_map/ppermute | solution.py:251
  71.7 1.9 %copy-start.1 = (bf16[256,512]{1,0:T(8,128)(2,1)S(1)}, bf16[256,512]{1,0:T(8,128)(2,1)}, u32[]{:S(2)}) copy-start(bf16[256,512]{1,0:T(8,128)(2,1)} %og_ref.1) | copy-start | bytes 786436
  75.1 3.4 %collective-permute-start.7 = (bf16[256,512]{1,0:T(8,128)(2,1)S(1)}, bf16[256,512]{1,0:T(8,128)(2,1)S(1)}, u32[]{:S(2)}, u32[]{:S(2)}) collective-permute-start(bf16[256,512]{1,0:T(8,128)(2,1)S(1)} %get-tuple-element.43.pg_ref), channel_id=1, source_target_pairs={{0,1},{1,0},{2,3},{3,2},{4,5},{5,4},{6,7},{7,6},{8,9},{9,8},{10,11... | collective-permute-start | bytes 786440 | tf_op jit(solution)/shard_map/ppermute | solution.py:251
  80.8 17.9 %collective-permute-start.9 = (bf16[8,256,256]{2,1,0:T(8,128)(2,1)}, bf16[8,256,256]{2,1,0:T(8,128)(2,1)S(1)}, u32[]{:S(2)}, u32[]{:S(2)}) collective-permute-start(bf16[8,256,256]{2,1,0:T(8,128)(2,1)} %shard_map.84), channel_id=1, source_target_pairs={{0,2},{1,31},{2,4},{3,1},{4,6},{5,3},{6,8},{7,5},{8,10},{9,7},{10,... | collective-permute-start | bytes 3145736 | tf_op jit(solution)/shard_map/ppermute | solution.py:251
  90.5 1.5 %copy-start = (bf16[80,128,128]{2,1,0:T(8,128)(2,1)}, bf16[80,128,128]{2,1,0:T(8,128)(2,1)S(1)}, u32[]{:S(2)}) copy-start(bf16[80,128,128]{2,1,0:T(8,128)(2,1)S(1)} %shard_map.88) | copy-start | bytes 7864324
  92.0 43.3 %all-to-all-start = ((bf16[80,128,128]{2,1,0:T(8,128)(2,1)}), bf16[80,128,128]{2,1,0:T(8,128)(2,1)}, u32[]{:S(2)}, u32[]{:S(2)}) async-start(bf16[80,128,128]{2,1,0:T(8,128)(2,1)} %copy-done), calls=%async_computation | async-start | bytes 5242880 | tf_op jit(solution)/shard_map/all_to_all | solution.py:325
  98.8 16.2 %collective-permute-start.10 = (bf16[4,256,256]{2,1,0:T(8,128)(2,1)S(1)}, bf16[4,256,256]{2,1,0:T(8,128)(2,1)S(1)}, u32[]{:S(2)}, u32[]{:S(2)}) collective-permute-start(bf16[4,256,256]{2,1,0:T(8,128)(2,1)S(1)} %shard_map.86), channel_id=1, source_target_pairs={{0,4},{1,29},{2,6},{3,31},{4,8},{5,1},{6,10},{7,3},{8,12},{9,5},{1... | collective-permute-start | bytes 1572872 | tf_op jit(solution)/shard_map/ppermute | solution.py:251
  115.9 22.4 %collective-permute-start.11 = (bf16[2,256,256]{2,1,0:T(8,128)(2,1)}, bf16[2,256,256]{2,1,0:T(8,128)(2,1)S(1)}, u32[]{:S(2)}, u32[]{:S(2)}) collective-permute-start(bf16[2,256,256]{2,1,0:T(8,128)(2,1)} %get-tuple-element.42), channel_id=1, source_target_pairs={{0,8},{1,23},{2,10},{3,25},{4,12},{5,27},{6,14},{7,29},{8,16},{9,3... | collective-permute-start | bytes 786440 | tf_op jit(solution)/shard_map/ppermute | solution.py:251
  124.4 16.3 %collective-permute-start.12 = (bf16[2,256,256]{2,1,0:T(8,128)(2,1)S(1)}, bf16[2,256,256]{2,1,0:T(8,128)(2,1)S(1)}, u32[]{:S(2)}, u32[]{:S(2)}) collective-permute-start(bf16[2,256,256]{2,1,0:T(8,128)(2,1)S(1)} %get-tuple-element.41.base_ref), channel_id=1, source_target_pairs={{1,31},{3,1},{5,3},{7,5},{9,7},{11,9},{13,11},{15,13},{17,15},{19,... | collective-permute-start | bytes 786440 | tf_op jit(solution)/shard_map/ppermute | solution.py:251
  140.8 3.2 %collective-permute-start.13 = (bf16[256,256]{1,0:T(8,128)(2,1)S(1)}, bf16[256,256]{1,0:T(8,128)(2,1)S(1)}, u32[]{:S(2)}, u32[]{:S(2)}) collective-permute-start(bf16[256,256]{1,0:T(8,128)(2,1)S(1)} %get-tuple-element.47), channel_id=1, source_target_pairs={{0,1},{1,0},{2,3},{3,2},{4,5},{5,4},{6,7},{7,6},{8,9},{9,8},{10,11... | collective-permute-start | bytes 393224 | tf_op jit(solution)/shard_map/ppermute | solution.py:251

commit v7 on v6

--- a/solution.py
+++ b/solution.py
@@ -315,7 +315,7 @@
     d2 = back_of(0, F32)
     pg, d2 = together((pg, d2))
     terms = kernel(
-        weight_terms, shape(slots, blk, blk), ins=[HBM], n_in=5, mib=14,
+        weight_terms, shape(slots, blk, blk), ins=[HBM], n_in=5, mib=12,
         flops=flops_of(32), size=16 * MIB,
         scratch=[
             pltpu.SMEM(listed.shape, jnp.int32), pltpu.VMEM((width, tok_rows), BF16),
@@ -331,10 +331,10 @@
     own_grads = kernel(
         functools.partial(add_terms, 1.0 / (tok_rows * n_dp) ** 0.5), shape(per, blk, blk, dtype=F32), size=0
     )(got.reshape(n_dp, per, blk, blk))
-    r3, moved, own_grads = together((r3, moved, own_grads))
     one = shape(tok_rows, feats)
     cross, total = kernel(add_third, (one, shape(tok_rows, feats, dtype=F32)), n_in=3, size=0)(sums, moved, r3)
-    in_grad = kernel(add_last, one, n_in=2, size=0)(total, other_core(cross))
+    cross, own_grads = together((other_core(cross), own_grads))
+    in_grad = kernel(add_last, one, n_in=2, size=0)(total, cross)
     return act, in_grad, own_grads[None]
 
 

time: 145 us -> 146 us (level)
  waiting for transfers between devices: 58.4 us -> 61.5 us
  Pallas kernels: 25.7 us -> 23.3 us
    ppermute x14, waiting for transfers between devices: 50.8 us -> 61.5 us  [send(): return lax.ppermute(v, 'blk', pairs)]
    all_to_all x1, waiting for transfers between devices: 7.58 us -> 0.01 us  [on_device(): got = lax.all_to_all(terms, 'dp', 0, 0, tiled=True)]
    pallas_call x1, Pallas kernels: 8.26 us -> 6.49 us  [on_device(): kernel(lay_weights, (shape(2 * NZ * feats, width),) + (shape(NZ, width, f...]
  transfers between devices with their start and end apart: 15 -> 15, of which waited for: 11 -> 10; matrix products, arithmetic and copies ran while one was open for 0% -> 0% of each run, Pallas kernels for 16% -> 14%
where the time goes in v7:
time: 146 us
  waiting for transfers between devices  61.5 us (42%)
  starting transfers between devices  57.4 us (39%)
  Pallas kernels  23.3 us (16%)
  local copies, waits for them, and re-layouts  2.44 us (2%)
    ppermute x14, waiting for transfers between devices, send(): return lax.ppermute(v, 'blk', pairs)  61.5 us
    ppermute x14, starting transfers between devices, send(): return lax.ppermute(v, 'blk', pairs)  50.7 us
    all_to_all x1, starting transfers between devices, on_device(): got = lax.all_to_all(terms, 'dp', 0, 0, tiled=True)  6.7 us
    pallas_call x1, Pallas kernels, on_device(): kernel(lay_weights, (shape(2 * NZ * feats, width),) + (shape(NZ, width, f...  6.49 us
    pallas_call x1, Pallas kernels, on_device(): kernel(weight_terms, shape(slots, blk, blk), ins=[HBM], n_in=5, mib=12, f...  5.69 us
    pallas_call x2, Pallas kernels, back_of(): kernel(functools.partial(back, first), shards(8, dtype), n_in=4, flops=fl...  3.5 us
  transfers between devices with their start and end apart: 15, of which 10 were waited for; matrix products, arithmetic and copies ran while one was open for 0% of the time, Pallas kernels for 14%

profile of v7, /device:TPU:1, one launch (start us, length us, event | category | flops | bytes accessed | tf_op | source)
XLA Modules:
  0.0 145.5 jit_solution(6780293249013946537)
XLA Ops:
  0.6 8.8 %collective-permute-start = (bf16[256,256]{1,0:T(8,128)(2,1)}, bf16[256,256]{1,0:T(8,128)(2,1)S(1)}, u32[]{:S(2)}, u32[]{:S(2)}) collective-permute-start(bf16[256,256]{1,0:T(8,128)(2,1)} %a_ref.1), channel_id=1, source_target_pairs={{0,1},{1,0},{2,3},{3,2},{4,5},{5,4},{6,7},{7,6},{8,9},{9,8},{10,11... | collective-permute-start | bytes 393224 | tf_op jit(solution)/shard_map/ppermute | solution.py:251
  9.4 1.2 collective-permute-done.b_ref
  10.6 0.9 copy-done.2
  11.5 4.8 %collective-permute-start.2 = (bf16[2,256,256]{2,1,0:T(8,128)(2,1)S(1)}, bf16[2,256,256]{2,1,0:T(8,128)(2,1)S(1)}, u32[]{:S(2)}, u32[]{:S(2)}) collective-permute-start(bf16[2,256,256]{2,1,0:T(8,128)(2,1)S(1)} %shard_map.76.pair_ref), channel_id=1, source_target_pairs={{0,24},{1,11},{2,26},{3,13},{4,28},{5,15},{6,30},{7,17},{8,0},{9,1... | collective-permute-start | bytes 786440 | tf_op jit(solution)/shard_map/ppermute | solution.py:251
  16.3 3.5 %collective-permute-start.1 = (bf16[2,256,256]{2,1,0:T(8,128)(2,1)S(1)}, bf16[2,256,256]{2,1,0:T(8,128)(2,1)S(1)}, u32[]{:S(2)}, u32[]{:S(2)}) collective-permute-start(bf16[2,256,256]{2,1,0:T(8,128)(2,1)S(1)} %shard_map.76.pair_ref), channel_id=1, source_target_pairs={{1,3},{3,5},{5,7},{7,9},{9,11},{11,13},{13,15},{15,17},{17,19},{19... | collective-permute-start | bytes 786440 | tf_op jit(solution)/shard_map/ppermute | solution.py:251
  19.9 6.5 %shard_map.77 = (bf16[8192,512]{1,0:T(8,128)(2,1)S(1)}, bf16[16,512,256]{2,1,0:T(8,128)(2,1)S(1)}, bf16[16,512,256]{2,1,0:T(8,128)(2,1)S(1)}) custom-call(s32[2,80]{1,0:T(2,128)} %bitcast.10, s32[2,32]{1,0:T(2,128)} %bitcast.9, bf16[80,128,128]{2,1,0:T(8,128)(2,1)} %bitcast.7), custom_call_target="tpu_custom_call" | custom-call | bytes 20971520 | tf_op jit(solution)/shard_map/pallas_call | solution.py:274
  26.4 1.9 %collective-permute-done.2.g4_ref = bf16[2,256,256]{2,1,0:T(8,128)(2,1)S(1)} collective-permute-done((bf16[2,256,256]{2,1,0:T(8,128)(2,1)S(1)}, bf16[2,256,256]{2,1,0:T(8,128)(2,1)S(1)}, u32[]{:S(2)}, u32[]{:S(2)}) %collective-permute-start.2) | collective-permute-done | bytes 262176 | tf_op jit(solution)/shard_map/ppermute | solution.py:251
  28.3 6.9 %collective-permute-done.1.hop_ref = bf16[2,256,256]{2,1,0:T(8,128)(2,1)S(1)} collective-permute-done((bf16[2,256,256]{2,1,0:T(8,128)(2,1)S(1)}, bf16[2,256,256]{2,1,0:T(8,128)(2,1)S(1)}, u32[]{:S(2)}, u32[]{:S(2)}) %collective-permute-start.1) | collective-permute-done | bytes 262176 | tf_op jit(solution)/shard_map/ppermute | solution.py:251
  35.3 3.2 %collective-permute-start.3 = (bf16[4,256,256]{2,1,0:T(8,128)(2,1)S(1)}, bf16[4,256,256]{2,1,0:T(8,128)(2,1)S(1)}, u32[]{:S(2)}, u32[]{:S(2)}) collective-permute-start(bf16[4,256,256]{2,1,0:T(8,128)(2,1)S(1)} %shard_map.78.a_ref), channel_id=1, source_target_pairs={{0,28},{1,5},{2,30},{3,7},{4,0},{5,9},{6,2},{7,11},{8,4},{9,13},{1... | collective-permute-start | bytes 1572872 | tf_op jit(solution)/shard_map/ppermute | solution.py:251
  38.5 13.7 %collective-permute-done.3.b_ref = bf16[4,256,256]{2,1,0:T(8,128)(2,1)S(1)} collective-permute-done((bf16[4,256,256]{2,1,0:T(8,128)(2,1)S(1)}, bf16[4,256,256]{2,1,0:T(8,128)(2,1)S(1)}, u32[]{:S(2)}, u32[]{:S(2)}) %collective-permute-start.3) | collective-permute-done | bytes 524320 | tf_op jit(solution)/shard_map/ppermute | solution.py:251
  52.2 0.1 shard_map.79.x_ref.refs_0_
  52.3 1.9 %collective-permute-start.4 = (bf16[8,256,256]{2,1,0:T(8,128)(2,1)S(1)}, bf16[8,256,256]{2,1,0:T(8,128)(2,1)S(1)}, u32[]{:S(2)}, u32[]{:S(2)}) collective-permute-start(bf16[8,256,256]{2,1,0:T(8,128)(2,1)S(1)} %shard_map.79.x_ref.refs_0_), channel_id=1, source_target_pairs={{0,30},{1,3},{2,0},{3,5},{4,2},{5,7},{6,4},{7,9},{8,6},{9,11},{10,... | collective-permute-start | bytes 3145736 | tf_op jit(solution)/shard_map/ppermute | solution.py:251
  54.2 2.0 %collective-permute-start.5 = (bf16[8,256,256]{2,1,0:T(8,128)(2,1)S(1)}, bf16[8,256,256]{2,1,0:T(8,128)(2,1)S(1)}, u32[]{:S(2)}, u32[]{:S(2)}) collective-permute-start(bf16[8,256,256]{2,1,0:T(8,128)(2,1)S(1)} %shard_map.79.x_ref.refs_0_), channel_id=1, source_target_pairs={{0,1},{1,0},{2,3},{3,2},{4,5},{5,4},{6,7},{7,6},{8,9},{9,8},{10,11... | collective-permute-start | bytes 3145736 | tf_op jit(solution)/shard_map/ppermute | solution.py:251
  56.2 0.7 shard_map.80.so_far
  56.9 2.3 %collective-permute-start.8 = (bf16[16,512,256]{2,1,0:T(8,128)(2,1)S(1)}, bf16[16,512,256]{2,1,0:T(8,128)(2,1)S(1)}, u32[]{:S(2)}, u32[]{:S(2)}) collective-permute-start(bf16[16,512,256]{2,1,0:T(8,128)(2,1)S(1)} %get-tuple-element.37), channel_id=1, source_target_pairs={{0,1},{1,0},{2,3},{3,2},{4,5},{5,4},{6,7},{7,6},{8,9},{9,8},{10,11... | collective-permute-start | bytes 12582920 | tf_op jit(solution)/shard_map/ppermute | solution.py:251
  59.3 9.8 %collective-permute-done.4.x_ref.refs_1_ = bf16[8,256,256]{2,1,0:T(8,128)(2,1)S(1)} collective-permute-done((bf16[8,256,256]{2,1,0:T(8,128)(2,1)S(1)}, bf16[8,256,256]{2,1,0:T(8,128)(2,1)S(1)}, u32[]{:S(2)}, u32[]{:S(2)}) %collective-permute-start.4) | collective-permute-done | bytes 1048608 | tf_op jit(solution)/shard_map/ppermute | solution.py:251
  69.0 1.9 %collective-permute-start.6 = (bf16[8,256,256]{2,1,0:T(8,128)(2,1)S(1)}, bf16[8,256,256]{2,1,0:T(8,128)(2,1)S(1)}, u32[]{:S(2)}, u32[]{:S(2)}) collective-permute-start(bf16[8,256,256]{2,1,0:T(8,128)(2,1)S(1)} %collective-permute-done.4.x_ref.refs_1_), channel_id=1, source_target_pairs={{0,1},{1,0},{2,3},{3,2},{4,5},{5,4},{6,7},{7,6},{8,9},{9,8},{10,11... | collective-permute-start | bytes 3145736 | tf_op jit(solution)/shard_map/ppermute | solution.py:251
  71.0 0.7 shard_map.81.so_far
  71.7 0.0 copy-start.1
  71.7 0.0 collective-permute-done.5.x_ref.refs_2_
  71.7 0.7 shard_map.82.so_far
  72.4 1.2 collective-permute-done.6.x_ref.refs_3_
  73.6 0.0 copy-done.1
  73.6 1.5 %shard_map.83 = (bf16[256,512]{1,0:T(8,128)(2,1)}, bf16[256,512]{1,0:T(8,128)(2,1)S(1)}) custom-call(f32[256,512]{1,0:T(8,128)S(1)} %shard_map.82.so_far, bf16[8,256,256]{2,1,0:T(8,128)(2,1)S(1)} %collective-permute-done.6.x_ref.refs_3_, bf16[8192,512]{1,0:T(8,128)(2,1)S(1)} %get-tuple-element.31.up_ref, bf16[256,512]{1,0:T(8,128)(2,1)S(1)} %copy-done.1), custom_call_target="tpu_custom_call" | custom-call | flops 268435456 | bytes 4194304 | tf_op jit(solution)/shard_map/pallas_call | solution.py:302
  75.1 2.0 %collective-permute-start.7 = (bf16[256,512]{1,0:T(8,128)(2,1)S(1)}, bf16[256,512]{1,0:T(8,128)(2,1)S(1)}, u32[]{:S(2)}, u32[]{:S(2)}) collective-permute-start(bf16[256,512]{1,0:T(8,128)(2,1)S(1)} %get-tuple-element.44.pg_ref), channel_id=1, source_target_pairs={{0,1},{1,0},{2,3},{3,2},{4,5},{5,4},{6,7},{7,6},{8,9},{9,8},{10,11... | collective-permute-start | bytes 786440 | tf_op jit(solution)/shard_map/ppermute | solution.py:251
  77.2 1.4 collective-permute-done.7.pg2_ref
  78.5 0.0 collective-permute-done.8.sibling_ref
  78.5 2.2 %shard_map.84 = bf16[8,256,256]{2,1,0:T(8,128)(2,1)} custom-call(bf16[256,512]{1,0:T(8,128)(2,1)S(1)} %get-tuple-element.44.pg_ref, bf16[256,512]{1,0:T(8,128)(2,1)S(1)} %collective-permute-done.7.pg2_ref, bf16[16,512,256]{2,1,0:T(8,128)(2,1)S(1)} %get-tuple-element.36.own_ref, bf16[16,512,256]{2,1,0:T(8,128)(2,1)S(1)} %collective-permute-done.8.sibling_ref), custom_call_target="tpu_custom_call" | custom-call | flops 536870912 | bytes 4194304 | tf_op jit(solution)/shard_map/pallas_call | solution.py:308
  80.8 2.7 %collective-permute-start.9 = (bf16[8,256,256]{2,1,0:T(8,128)(2,1)}, bf16[8,256,256]{2,1,0:T(8,128)(2,1)S(1)}, u32[]{:S(2)}, u32[]{:S(2)}) collective-permute-start(bf16[8,256,256]{2,1,0:T(8,128)(2,1)} %shard_map.84), channel_id=1, source_target_pairs={{0,2},{1,31},{2,4},{3,1},{4,6},{5,3},{6,8},{7,5},{8,10},{9,7},{10,... | collective-permute-start | bytes 3145736 | tf_op jit(solution)/shard_map/ppermute | solution.py:251
  83.5 1.2 shard_map.85.d_ref
  84.8 5.7 %shard_map.89 = bf16[80,128,128]{2,1,0:T(8,128)(2,1)S(1)} custom-call(s32[2,80]{1,0:T(2,128)} %bitcast.11, bf16[256,512]{1,0:T(8,128)(2,1)S(1)} %get-tuple-element.44.pg_ref, bf16[8,256,256]{2,1,0:T(8,128)(2,1)S(1)} %shard_map.79.x_ref.refs_0_, bf16[8,256,256]{2,1,0:T(8,128)(2,1)S(1)} %collective-permute-done.4.x_ref.refs_1_, ...), custom_call_target="tpu_custom_call" | custom-call | flops 2147483648 | bytes 16777216 | tf_op jit(solution)/shard_map/pallas_call | solution.py:317
  90.5 1.5 %copy-done = bf16[80,128,128]{2,1,0:T(8,128)(2,1)} copy-done((bf16[80,128,128]{2,1,0:T(8,128)(2,1)}, bf16[80,128,128]{2,1,0:T(8,128)(2,1)S(1)}, u32[]{:S(2)}) %copy-start) | copy-done | bytes 2621464
  92.0 6.7 %all-to-all-start = ((bf16[80,128,128]{2,1,0:T(8,128)(2,1)}), bf16[80,128,128]{2,1,0:T(8,128)(2,1)}, u32[]{:S(2)}, u32[]{:S(2)}) async-start(bf16[80,128,128]{2,1,0:T(8,128)(2,1)} %copy-done), calls=%async_computation | async-start | bytes 5242880 | tf_op jit(solution)/shard_map/all_to_all | solution.py:325
  98.7 0.0 collective-permute-done.9.r1_ref
  98.7 0.1 shard_map.86
  98.8 3.6 %collective-permute-start.10 = (bf16[4,256,256]{2,1,0:T(8,128)(2,1)S(1)}, bf16[4,256,256]{2,1,0:T(8,128)(2,1)S(1)}, u32[]{:S(2)}, u32[]{:S(2)}) collective-permute-start(bf16[4,256,256]{2,1,0:T(8,128)(2,1)S(1)} %shard_map.86), channel_id=1, source_target_pairs={{0,4},{1,29},{2,6},{3,31},{4,8},{5,1},{6,10},{7,3},{8,12},{9,5},{1... | collective-permute-start | bytes 1572872 | tf_op jit(solution)/shard_map/ppermute | solution.py:251
  102.5 12.6 %collective-permute-done.10.r2_ref = bf16[4,256,256]{2,1,0:T(8,128)(2,1)S(1)} collective-permute-done((bf16[4,256,256]{2,1,0:T(8,128)(2,1)S(1)}, bf16[4,256,256]{2,1,0:T(8,128)(2,1)S(1)}, u32[]{:S(2)}, u32[]{:S(2)}) %collective-permute-start.10) | collective-permute-done | bytes 524320 | tf_op jit(solution)/shard_map/ppermute | solution.py:251
  115.1 0.2 shard_map.87
  115.2 8.6 %collective-permute-start.12 = (bf16[2,256,256]{2,1,0:T(8,128)(2,1)S(1)}, bf16[2,256,256]{2,1,0:T(8,128)(2,1)S(1)}, u32[]{:S(2)}, u32[]{:S(2)}) collective-permute-start(bf16[2,256,256]{2,1,0:T(8,128)(2,1)S(1)} %get-tuple-element.41), channel_id=1, source_target_pairs={{0,8},{1,23},{2,10},{3,25},{4,12},{5,27},{6,14},{7,29},{8,16},{9,3... | collective-permute-start | bytes 786440 | tf_op jit(solution)/shard_map/ppermute | solution.py:251
  123.8 3.3 %collective-permute-start.11 = (bf16[2,256,256]{2,1,0:T(8,128)(2,1)S(1)}, bf16[2,256,256]{2,1,0:T(8,128)(2,1)S(1)}, u32[]{:S(2)}, u32[]{:S(2)}) collective-permute-start(bf16[2,256,256]{2,1,0:T(8,128)(2,1)S(1)} %get-tuple-element.40.base_ref), channel_id=1, source_target_pairs={{1,31},{3,1},{5,3},{7,5},{9,7},{11,9},{13,11},{15,13},{17,15},{19,... | collective-permute-start | bytes 786440 | tf_op jit(solution)/shard_map/ppermute | solution.py:251
  127.1 9.1 %collective-permute-done.12.r3_ref = bf16[2,256,256]{2,1,0:T(8,128)(2,1)S(1)} collective-permute-done((bf16[2,256,256]{2,1,0:T(8,128)(2,1)S(1)}, bf16[2,256,256]{2,1,0:T(8,128)(2,1)S(1)}, u32[]{:S(2)}, u32[]{:S(2)}) %collective-permute-start.12) | collective-permute-done | bytes 262176 | tf_op jit(solution)/shard_map/ppermute | solution.py:251
  136.2 3.7 %collective-permute-done.11.hop_ref = bf16[2,256,256]{2,1,0:T(8,128)(2,1)S(1)} collective-permute-done((bf16[2,256,256]{2,1,0:T(8,128)(2,1)S(1)}, bf16[2,256,256]{2,1,0:T(8,128)(2,1)S(1)}, u32[]{:S(2)}, u32[]{:S(2)}) %collective-permute-start.11) | collective-permute-done | bytes 262176 | tf_op jit(solution)/shard_map/ppermute | solution.py:251
  139.9 0.1 shard_map.88
  140.0 1.9 %collective-permute-start.13 = (bf16[256,256]{1,0:T(8,128)(2,1)S(1)}, bf16[256,256]{1,0:T(8,128)(2,1)S(1)}, u32[]{:S(2)}, u32[]{:S(2)}) collective-permute-start(bf16[256,256]{1,0:T(8,128)(2,1)S(1)} %get-tuple-element.43), channel_id=1, source_target_pairs={{0,1},{1,0},{2,3},{3,2},{4,5},{5,4},{6,7},{7,6},{8,9},{9,8},{10,11... | collective-permute-start | bytes 393224 | tf_op jit(solution)/shard_map/ppermute | solution.py:251
  141.9 0.0 all-to-all-done
  141.9 2.9 %shard_map.90 = f32[5,128,128]{2,1,0:T(8,128)} custom-call(bf16[16,5,128,128]{3,2,1,0:T(8,128)(2,1)} %bitcast.4.in_ref), custom_call_target="tpu_custom_call" | custom-call | tf_op jit(solution)/shard_map/pallas_call | solution.py:331
  144.8 0.0 collective-permute-done.13.cross_ref
  144.8 0.7 shard_map.91
  (4 shorter events, 0.1 us)
Async XLA Ops:
  0.6 10.0 %collective-permute-start = (bf16[256,256]{1,0:T(8,128)(2,1)}, bf16[256,256]{1,0:T(8,128)(2,1)S(1)}, u32[]{:S(2)}, u32[]{:S(2)}) collective-permute-start(bf16[256,256]{1,0:T(8,128)(2,1)} %a_ref.1), channel_id=1, source_target_pairs={{0,1},{1,0},{2,3},{3,2},{4,5},{5,4},{6,7},{7,6},{8,9},{9,8},{10,11... | collective-permute-start | bytes 393224 | tf_op jit(solution)/shard_map/ppermute | solution.py:251
  10.6 0.9 copy-start.2
  11.5 16.8 %collective-permute-start.2 = (bf16[2,256,256]{2,1,0:T(8,128)(2,1)S(1)}, bf16[2,256,256]{2,1,0:T(8,128)(2,1)S(1)}, u32[]{:S(2)}, u32[]{:S(2)}) collective-permute-start(bf16[2,256,256]{2,1,0:T(8,128)(2,1)S(1)} %shard_map.76.pair_ref), channel_id=1, source_target_pairs={{0,24},{1,11},{2,26},{3,13},{4,28},{5,15},{6,30},{7,17},{8,0},{9,1... | collective-permute-start | bytes 786440 | tf_op jit(solution)/shard_map/ppermute | solution.py:251
  16.3 18.9 %collective-permute-start.1 = (bf16[2,256,256]{2,1,0:T(8,128)(2,1)S(1)}, bf16[2,256,256]{2,1,0:T(8,128)(2,1)S(1)}, u32[]{:S(2)}, u32[]{:S(2)}) collective-permute-start(bf16[2,256,256]{2,1,0:T(8,128)(2,1)S(1)} %shard_map.76.pair_ref), channel_id=1, source_target_pairs={{1,3},{3,5},{5,7},{7,9},{9,11},{11,13},{13,15},{15,17},{17,19},{19... | collective-permute-start | bytes 786440 | tf_op jit(solution)/shard_map/ppermute | solution.py:251
  35.3 16.9 %collective-permute-start.3 = (bf16[4,256,256]{2,1,0:T(8,128)(2,1)S(1)}, bf16[4,256,256]{2,1,0:T(8,128)(2,1)S(1)}, u32[]{:S(2)}, u32[]{:S(2)}) collective-permute-start(bf16[4,256,256]{2,1,0:T(8,128)(2,1)S(1)} %shard_map.78.a_ref), channel_id=1, source_target_pairs={{0,28},{1,5},{2,30},{3,7},{4,0},{5,9},{6,2},{7,11},{8,4},{9,13},{1... | collective-permute-start | bytes 1572872 | tf_op jit(solution)/shard_map/ppermute | solution.py:251
  52.3 16.8 %collective-permute-start.4 = (bf16[8,256,256]{2,1,0:T(8,128)(2,1)S(1)}, bf16[8,256,256]{2,1,0:T(8,128)(2,1)S(1)}, u32[]{:S(2)}, u32[]{:S(2)}) collective-permute-start(bf16[8,256,256]{2,1,0:T(8,128)(2,1)S(1)} %shard_map.79.x_ref.refs_0_), channel_id=1, source_target_pairs={{0,30},{1,3},{2,0},{3,5},{4,2},{5,7},{6,4},{7,9},{8,6},{9,11},{10,... | collective-permute-start | bytes 3145736 | tf_op jit(solution)/shard_map/ppermute | solution.py:251
  54.2 17.5 %collective-permute-start.5 = (bf16[8,256,256]{2,1,0:T(8,128)(2,1)S(1)}, bf16[8,256,256]{2,1,0:T(8,128)(2,1)S(1)}, u32[]{:S(2)}, u32[]{:S(2)}) collective-permute-start(bf16[8,256,256]{2,1,0:T(8,128)(2,1)S(1)} %shard_map.79.x_ref.refs_0_), channel_id=1, source_target_pairs={{0,1},{1,0},{2,3},{3,2},{4,5},{5,4},{6,7},{7,6},{8,9},{9,8},{10,11... | collective-permute-start | bytes 3145736 | tf_op jit(solution)/shard_map/ppermute | solution.py:251
  56.9 21.6 %collective-permute-start.8 = (bf16[16,512,256]{2,1,0:T(8,128)(2,1)S(1)}, bf16[16,512,256]{2,1,0:T(8,128)(2,1)S(1)}, u32[]{:S(2)}, u32[]{:S(2)}) collective-permute-start(bf16[16,512,256]{2,1,0:T(8,128)(2,1)S(1)} %get-tuple-element.37), channel_id=1, source_target_pairs={{0,1},{1,0},{2,3},{3,2},{4,5},{5,4},{6,7},{7,6},{8,9},{9,8},{10,11... | collective-permute-start | bytes 12582920 | tf_op jit(solution)/shard_map/ppermute | solution.py:251
  69.0 4.5 %collective-permute-start.6 = (bf16[8,256,256]{2,1,0:T(8,128)(2,1)S(1)}, bf16[8,256,256]{2,1,0:T(8,128)(2,1)S(1)}, u32[]{:S(2)}, u32[]{:S(2)}) collective-permute-start(bf16[8,256,256]{2,1,0:T(8,128)(2,1)S(1)} %collective-permute-done.4.x_ref.refs_1_), channel_id=1, source_target_pairs={{0,1},{1,0},{2,3},{3,2},{4,5},{5,4},{6,7},{7,6},{8,9},{9,8},{10,11... | collective-permute-start | bytes 3145736 | tf_op jit(solution)/shard_map/ppermute | solution.py:251
  71.7 1.9 %copy-start.1 = (bf16[256,512]{1,0:T(8,128)(2,1)S(1)}, bf16[256,512]{1,0:T(8,128)(2,1)}, u32[]{:S(2)}) copy-start(bf16[256,512]{1,0:T(8,128)(2,1)} %og_ref.1) | copy-start | bytes 786436
  75.1 3.4 %collective-permute-start.7 = (bf16[256,512]{1,0:T(8,128)(2,1)S(1)}, bf16[256,512]{1,0:T(8,128)(2,1)S(1)}, u32[]{:S(2)}, u32[]{:S(2)}) collective-permute-start(bf16[256,512]{1,0:T(8,128)(2,1)S(1)} %get-tuple-element.44.pg_ref), channel_id=1, source_target_pairs={{0,1},{1,0},{2,3},{3,2},{4,5},{5,4},{6,7},{7,6},{8,9},{9,8},{10,11... | collective-permute-start | bytes 786440 | tf_op jit(solution)/shard_map/ppermute | solution.py:251
  80.8 17.9 %collective-permute-start.9 = (bf16[8,256,256]{2,1,0:T(8,128)(2,1)}, bf16[8,256,256]{2,1,0:T(8,128)(2,1)S(1)}, u32[]{:S(2)}, u32[]{:S(2)}) collective-permute-start(bf16[8,256,256]{2,1,0:T(8,128)(2,1)} %shard_map.84), channel_id=1, source_target_pairs={{0,2},{1,31},{2,4},{3,1},{4,6},{5,3},{6,8},{7,5},{8,10},{9,7},{10,... | collective-permute-start | bytes 3145736 | tf_op jit(solution)/shard_map/ppermute | solution.py:251
  90.5 1.5 %copy-start = (bf16[80,128,128]{2,1,0:T(8,128)(2,1)}, bf16[80,128,128]{2,1,0:T(8,128)(2,1)S(1)}, u32[]{:S(2)}) copy-start(bf16[80,128,128]{2,1,0:T(8,128)(2,1)S(1)} %shard_map.89) | copy-start | bytes 7864324
  92.0 49.9 %all-to-all-start = ((bf16[80,128,128]{2,1,0:T(8,128)(2,1)}), bf16[80,128,128]{2,1,0:T(8,128)(2,1)}, u32[]{:S(2)}, u32[]{:S(2)}) async-start(bf16[80,128,128]{2,1,0:T(8,128)(2,1)} %copy-done), calls=%async_computation | async-start | bytes 5242880 | tf_op jit(solution)/shard_map/all_to_all | solution.py:325
  98.8 16.2 %collective-permute-start.10 = (bf16[4,256,256]{2,1,0:T(8,128)(2,1)S(1)}, bf16[4,256,256]{2,1,0:T(8,128)(2,1)S(1)}, u32[]{:S(2)}, u32[]{:S(2)}) collective-permute-start(bf16[4,256,256]{2,1,0:T(8,128)(2,1)S(1)} %shard_map.86), channel_id=1, source_target_pairs={{0,4},{1,29},{2,6},{3,31},{4,8},{5,1},{6,10},{7,3},{8,12},{9,5},{1... | collective-permute-start | bytes 1572872 | tf_op jit(solution)/shard_map/ppermute | solution.py:251
  115.2 21.0 %collective-permute-start.12 = (bf16[2,256,256]{2,1,0:T(8,128)(2,1)S(1)}, bf16[2,256,256]{2,1,0:T(8,128)(2,1)S(1)}, u32[]{:S(2)}, u32[]{:S(2)}) collective-permute-start(bf16[2,256,256]{2,1,0:T(8,128)(2,1)S(1)} %get-tuple-element.41), channel_id=1, source_target_pairs={{0,8},{1,23},{2,10},{3,25},{4,12},{5,27},{6,14},{7,29},{8,16},{9,3... | collective-permute-start | bytes 786440 | tf_op jit(solution)/shard_map/ppermute | solution.py:251
  123.8 16.1 %collective-permute-start.11 = (bf16[2,256,256]{2,1,0:T(8,128)(2,1)S(1)}, bf16[2,256,256]{2,1,0:T(8,128)(2,1)S(1)}, u32[]{:S(2)}, u32[]{:S(2)}) collective-permute-start(bf16[2,256,256]{2,1,0:T(8,128)(2,1)S(1)} %get-tuple-element.40.base_ref), channel_id=1, source_target_pairs={{1,31},{3,1},{5,3},{7,5},{9,7},{11,9},{13,11},{15,13},{17,15},{19,... | collective-permute-start | bytes 786440 | tf_op jit(solution)/shard_map/ppermute | solution.py:251
  140.0 4.8 %collective-permute-start.13 = (bf16[256,256]{1,0:T(8,128)(2,1)S(1)}, bf16[256,256]{1,0:T(8,128)(2,1)S(1)}, u32[]{:S(2)}, u32[]{:S(2)}) collective-permute-start(bf16[256,256]{1,0:T(8,128)(2,1)S(1)} %get-tuple-element.43), channel_id=1, source_target_pairs={{0,1},{1,0},{2,3},{3,2},{4,5},{5,4},{6,7},{7,6},{8,9},{9,8},{10,11... | collective-permute-start | bytes 393224 | tf_op jit(solution)/shard_map/ppermute | solution.py:251

commit v8 on v7

--- a/solution.py
+++ b/solution.py
@@ -13,6 +13,7 @@
 MIB = 1 << 20
 BF16, F32 = jnp.bfloat16, jnp.float32
 NZ = 16
+SET = 17
 LONG = 80 * 10**9
 FIRST = 200 * 10**9
 
@@ -37,10 +38,25 @@
 def place_of(dev, me):
     z, core = me
     step = lax.rem(dev // 2 - z + NZ, NZ)
-    chosen = (step >= NZ // 2).astype(jnp.int32)
-    i = jnp.where(step < NZ // 2, step, NZ - 1 - step)
+    same = lax.rem(dev, 2) == core
+    chosen = jnp.where(step == 0, core, (step > NZ // 2).astype(jnp.int32))
+    i = jnp.where(step <= NZ // 2, step, NZ - step)
     second = (lax.rem(dev, 2) != chosen).astype(jnp.int32)
-    return chosen == core, 8 * lax.rem(i, 2) + 2 * (i // 4) + 4 * lax.rem(i // 2, 2) + second
+    place = 8 * lax.rem(i, 2) + 2 * (i // 4) + 4 * lax.rem(i // 2, 2) + second
+    return step, same, chosen == core, jnp.where(step == NZ // 2, 16, place)
+
+
+def up_place(dev, me):
+    step, same, mine, n = place_of(dev, me)
+    mine = jnp.where(step == NZ // 2, same.astype(jnp.int32), mine.astype(jnp.int32))
+    return n + SET * (1 - mine)
+
+
+def down_place(dev, me):
+    step, same, mine, n = place_of(dev, me)
+    by_parity = lax.rem(step, NZ // 2) == 0
+    mine = jnp.where(by_parity, same.astype(jnp.int32), mine.astype(jnp.int32))
+    return mine == 1, jnp.where(step == 0, 0, n)
 
 
 def in_hbm(v):
@@ -79,11 +95,10 @@
         @pl.when(row >= 0)
         def _():
             block = w_ref[s]
-            mine, n = place_of(row // rows_per_dev, me)
-            n = jnp.where(mine, n, n + NZ)
+            n = up_place(row // rows_per_dev, me)
             up_ref[at(n * rows_per_dev + lax.rem(row, rows_per_dev), blk), at(col, blk)] = block
             to = place[row]
-            mine, n = place_of(to // rows_per_dev, me)
+            mine, n = down_place(to // rows_per_dev, me)
             a = lax.rem(to, rows_per_dev)
             flipped = block.T
 
@@ -103,32 +118,22 @@
 def pair_up(a_ref, b_ref, out_ref):
     out_ref[0] = a_ref[...]
     out_ref[1] = b_ref[...]
-
-
-def chosen_base(core_0_ref, core_1_ref, use):
-    core = my_place()[1]
-
-    @pl.when(core == 0)
-    def _():
-        use(core_0_ref)
-
-    @pl.when(core != 0)
-    def _():
-        use(core_1_ref)
-
-
-def join_base(pair_ref, hop_ref, g4_ref, out_ref):
-    def put(ref):
-        out_ref[:2] = ref[...]
-
-    chosen_base(pair_ref, hop_ref, put)
-    out_ref[2:] = g4_ref[...]
 
 
 def join(a_ref, b_ref, out_ref):
     n = a_ref.shape[0]
     out_ref[:n] = a_ref[...]
     out_ref[n:] = b_ref[...]
+
+
+def join_early(a_ref, b_ref, out_ref, sixth_ref):
+    join(a_ref, b_ref, out_ref)
+    sixth_ref[...] = b_ref[2]
+
+
+def join_across(a_ref, b_ref, out_ref):
+    out_ref[:8] = a_ref[...]
+    out_ref[8] = b_ref[...]
 
 
 def times(up_ref, first, *x_refs):
@@ -149,7 +154,7 @@
 
 
 def forward_last(so_far, x_ref, up_ref, og_ref, act_ref, pg_ref):
-    hidden = so_far[...] + times(up_ref, 24, x_ref)
+    hidden = so_far[...] + times(up_ref, 25, x_ref)
     sig = jax.nn.sigmoid(hidden)
     act_ref[...] = (hidden * sig).astype(BF16)
     pg_ref[...] = (og_ref[...].astype(F32) * sig * (1.0 + hidden * (1.0 - sig))).astype(BF16)
@@ -163,13 +168,22 @@
         ).astype(out_ref.dtype)
 
 
+def back_late(pg_ref, pg2_ref, own_ref, sibling_ref, out_ref, across_ref):
+    back(8, pg_ref, pg2_ref, own_ref, sibling_ref, out_ref)
+    across_ref[...] = (
+        jnp.dot(pg_ref[...], own_ref[16], preferred_element_type=F32)
+        + jnp.dot(pg2_ref[...], sibling_ref[16], preferred_element_type=F32)
+    ).astype(BF16)
+
+
 def f32(v):
     return v.astype(F32)
 
 
-def add_first(d_ref, r1_ref, out_ref):
+def add_first(d_ref, r1_ref, r8_ref, out_ref):
     for n in range(4):
-        out_ref[n] = (d_ref[4 + n] + f32(r1_ref[4 + n])).astype(BF16)
+        total = d_ref[4 + n] + f32(r1_ref[4 + n])
+        out_ref[n] = (total + f32(r8_ref[...]) if n == 2 else total).astype(BF16)
 
 
 def add_second(d_ref, r1_ref, r2_ref, next_ref, base_ref):
@@ -178,12 +192,9 @@
         next_ref[n] = (d_ref[2 + n] + f32(r1_ref[2 + n]) + f32(r2_ref[2 + n])).astype(BF16)
 
 
-def add_third(base_ref, hop_ref, r3_ref, cross_ref, own_ref):
-    def put(ref):
-        cross_ref[...] = (f32(ref[1]) + f32(r3_ref[1])).astype(BF16)
-        own_ref[...] = f32(ref[0]) + f32(r3_ref[0])
-
-    chosen_base(base_ref, hop_ref, put)
+def add_third(base_ref, r3_ref, cross_ref, own_ref):
+    cross_ref[...] = (f32(base_ref[1]) + f32(r3_ref[1])).astype(BF16)
+    own_ref[...] = f32(base_ref[0]) + f32(r3_ref[0])
 
 
 def add_last(own_ref, cross_ref, out_ref):
@@ -207,8 +218,7 @@
         row, col = listed[0, s], listed[1, s]
         used = row >= 0
         row, col = jnp.maximum(row, 0), jnp.maximum(col, 0)
-        mine, n = place_of(row // rows_per_dev, me)
-        n = jnp.where(mine, n, n + NZ)
+        n = up_place(row // rows_per_dev, me)
         block = dense[n, at(col, blk), at(lax.rem(row, rows_per_dev), blk)]
         out_ref[s] = jnp.where(used, block, jnp.zeros_like(block))
         return carry
@@ -253,12 +263,8 @@
     def other_core(v):
         return send(v, [(n, n ^ 1) for n in range(2 * NZ)])
 
-    def steps(v, d, d1=None):
-        by = (d, -(d if d1 is None else d1))
-        return send(v, [(2 * z + c, 2 * ((z + by[c]) % NZ) + c) for z in around for c in range(2)])
-
-    def hop(v, d):
-        return send(v, [(2 * z + 1, 2 * ((z + d) % NZ) + 1) for z in around])
+    def steps(v, d):
+        return send(v, [(2 * z + c, 2 * ((z + (d, -d)[c]) % NZ) + c) for z in around for c in range(2)])
 
     def flops_of(shards):
         return 2 * shards * tok_rows * feats * width
@@ -268,12 +274,11 @@
 
     theirs = other_core(tokens)
     pair = kernel(pair_up, shards(2), n_in=2, size=0)(tokens, theirs)
-    g4 = steps(pair, -4, -5)
-    base = hop(pair, 1)
+    g4 = steps(pair, -4)
     pair, listed = together((pair, listed))
     up_w, down_w, down_other = kernel(
         lay_weights,
-        (shape(2 * NZ * feats, width),) + (shape(NZ, width, feats),) * 2,
+        (shape(2 * SET * feats, width),) + (shape(SET, width, feats),) * 2,
         ins=[HBM] * 3, n_in=0, mib=24, size=20 * MIB,
         scratch=[
             pltpu.SMEM(listed.shape, jnp.int32), pltpu.SMEM(cut.shape, jnp.int32), pltpu.SMEM((cut.size,), jnp.int32),
@@ -281,10 +286,12 @@
         ],
     )(in_hbm(listed), in_hbm(cut), in_hbm(up_blocks[0]))
     g4, up_w = together((g4, up_w))
-    g04 = kernel(join_base, shards(4), n_in=3, size=0)(pair, base, g4)
+    g04 = kernel(join, shards(4), n_in=2, size=0)(pair, g4)
     g26 = steps(g04, -2)
-    early = kernel(join, shards(8), n_in=2, size=0)(g04, g26)
+    one = shape(tok_rows, feats)
+    early, g6 = kernel(join_early, (shards(8), one), n_in=2, size=0)(g04, g26)
     late = steps(early, -1)
+    g8 = steps(g6, -2)
     early, down_other = together((early, down_other))
     early_other = other_core(early)
     down_sibling = other_core(down_other)
@@ -295,10 +302,11 @@
         return kernel(body, hidden_shape, n_in=len(operands), flops=flops, size=0)(*operands)
 
     hidden = more(forward_first, early, up_w)
-    late, hidden = together((late, hidden))
+    late, g8, hidden = together((late, g8, hidden))
+    late = kernel(join_across, shards(9), n_in=2, size=0)(late, g8)
     late_other = other_core(late)
     hidden = more(functools.partial(forward_more, 8), hidden, late, up_w, flops=LONG)
-    hidden = more(functools.partial(forward_more, 16), hidden, early_other, up_w)
+    hidden = more(functools.partial(forward_more, 17), hidden, early_other, up_w)
     act, pg = kernel(forward_last, (shape(tok_rows, width),) * 2, n_in=4, flops=flops_of(4), size=4 * MIB)(
         hidden, late_other, up_w, out_grad
     )
@@ -309,8 +317,9 @@
             pg, pg2, down_w, down_sibling
         )
 
-    d1 = back_of(8, BF16)
+    d1, d8 = kernel(back_late, (shards(8), one), n_in=4, flops=flops_of(9), size=4 * MIB)(pg, pg2, down_w, down_sibling)
     r1 = steps(d1, 1)
+    r8 = steps(d8, 2)
     pg, d1 = together((pg, d1))
     d2 = back_of(0, F32)
     pg, d2 = together((pg, d2))
@@ -319,20 +328,18 @@
         flops=flops_of(32), size=16 * MIB,
         scratch=[
             pltpu.SMEM(listed.shape, jnp.int32), pltpu.VMEM((width, tok_rows), BF16),
-            pltpu.VMEM((2 * NZ, width, feats), BF16), pltpu.SemaphoreType.DMA,
+            pltpu.VMEM((2 * SET, width, feats), BF16), pltpu.SemaphoreType.DMA,
         ],
     )(in_hbm(listed), pg, early, late, early_other, late_other)
     got = lax.all_to_all(terms, "dp", 0, 0, tiled=True)
 
-    r2 = steps(kernel(add_first, shards(4), n_in=2, flops=FIRST, size=0)(d2, r1), 2)
+    r2 = steps(kernel(add_first, shards(4), n_in=3, flops=FIRST, size=0)(d2, r1, r8), 2)
     q, sums = kernel(add_second, (shards(2),) * 2, n_in=3, size=0)(d2, r1, r2)
-    r3 = steps(q, 4, 5)
-    moved = hop(sums, -1)
+    r3 = steps(q, 4)
     own_grads = kernel(
         functools.partial(add_terms, 1.0 / (tok_rows * n_dp) ** 0.5), shape(per, blk, blk, dtype=F32), size=0
     )(got.reshape(n_dp, per, blk, blk))
-    one = shape(tok_rows, feats)
-    cross, total = kernel(add_third, (one, shape(tok_rows, feats, dtype=F32)), n_in=3, size=0)(sums, moved, r3)
+    cross, total = kernel(add_third, (one, shape(tok_rows, feats, dtype=F32)), n_in=2, size=0)(sums, r3)
     cross, own_grads = together((other_core(cross), own_grads))
     in_grad = kernel(add_last, one, n_in=2, size=0)(total, cross)
     return act, in_grad, own_grads[None]

time: 146 us -> 148 us (1.014)
  the two profiles are of different devices: /device:TPU:1 before, /device:TPU:65 now
where the time goes in v8:
time: 148 us; the launch traced here: 147 us
  starting transfers between devices  66.5 us (45%)
  waiting for transfers between devices  52.4 us (35%)
  Pallas kernels  25.2 us (17%)
  local copies, waits for them, and re-layouts  2.47 us (2%)
    ppermute x14, starting transfers between devices, send(): return lax.ppermute(v, 'blk', pairs)  60.6 us
    ppermute x14, waiting for transfers between devices, send(): return lax.ppermute(v, 'blk', pairs)  52.3 us
    pallas_call x1, Pallas kernels, on_device(): kernel(lay_weights, (shape(2 * SET * feats, width),) + (shape(SET, width,...  7.66 us
    pallas_call x1, Pallas kernels, on_device(): kernel(weight_terms, shape(slots, blk, blk), ins=[HBM], n_in=5, mib=12, f...  6.03 us
    all_to_all x1, starting transfers between devices, on_device(): got = lax.all_to_all(terms, 'dp', 0, 0, tiled=True)  5.84 us
  transfers between devices with their start and end apart: 15, of which 8 were waited for; matrix products, arithmetic and copies ran while one was open for 0% of the time, Pallas kernels for 15%

profile of v8, /device:TPU:65, one launch (start us, length us, event | category | flops | bytes accessed | tf_op | source)
XLA Modules:
  0.0 147.4 jit_solution(9884388403663851119)
XLA Ops:
  0.6 2.6 %collective-permute-start = (bf16[256,256]{1,0:T(8,128)(2,1)}, bf16[256,256]{1,0:T(8,128)(2,1)S(1)}, u32[]{:S(2)}, u32[]{:S(2)}) collective-permute-start(bf16[256,256]{1,0:T(8,128)(2,1)} %a_ref.1), channel_id=1, source_target_pairs={{0,1},{1,0},{2,3},{3,2},{4,5},{5,4},{6,7},{7,6},{8,9},{9,8},{10,11... | collective-permute-start | bytes 393224 | tf_op jit(solution)/shard_map/ppermute | solution.py:261
  3.2 1.2 collective-permute-done.b_ref
  4.4 0.9 copy-done.2
  5.3 8.8 %collective-permute-start.1 = (bf16[2,256,256]{2,1,0:T(8,128)(2,1)S(1)}, bf16[2,256,256]{2,1,0:T(8,128)(2,1)S(1)}, u32[]{:S(2)}, u32[]{:S(2)}) collective-permute-start(bf16[2,256,256]{2,1,0:T(8,128)(2,1)S(1)} %shard_map.76.a_ref), channel_id=1, source_target_pairs={{0,24},{1,9},{2,26},{3,11},{4,28},{5,13},{6,30},{7,15},{8,0},{9,17... | collective-permute-start | bytes 786440 | tf_op jit(solution)/shard_map/ppermute | solution.py:261
  14.1 7.7 %shard_map.77 = (bf16[8704,512]{1,0:T(8,128)(2,1)S(1)}, bf16[17,512,256]{2,1,0:T(8,128)(2,1)S(1)}, bf16[17,512,256]{2,1,0:T(8,128)(2,1)S(1)}) custom-call(s32[2,80]{1,0:T(2,128)} %bitcast.10, s32[2,32]{1,0:T(2,128)} %bitcast.9, bf16[80,128,128]{2,1,0:T(8,128)(2,1)} %bitcast.7), custom_call_target="tpu_custom_call" | custom-call | bytes 20971520 | tf_op jit(solution)/shard_map/pallas_call | solution.py:279
  21.8 4.6 %collective-permute-done.1.b_ref = bf16[2,256,256]{2,1,0:T(8,128)(2,1)S(1)} collective-permute-done((bf16[2,256,256]{2,1,0:T(8,128)(2,1)S(1)}, bf16[2,256,256]{2,1,0:T(8,128)(2,1)S(1)}, u32[]{:S(2)}, u32[]{:S(2)}) %collective-permute-start.1) | collective-permute-done | bytes 262176 | tf_op jit(solution)/shard_map/ppermute | solution.py:261
  26.5 5.3 %collective-permute-start.2 = (bf16[4,256,256]{2,1,0:T(8,128)(2,1)S(1)}, bf16[4,256,256]{2,1,0:T(8,128)(2,1)S(1)}, u32[]{:S(2)}, u32[]{:S(2)}) collective-permute-start(bf16[4,256,256]{2,1,0:T(8,128)(2,1)S(1)} %shard_map.78.a_ref), channel_id=1, source_target_pairs={{0,28},{1,5},{2,30},{3,7},{4,0},{5,9},{6,2},{7,11},{8,4},{9,13},{1... | collective-permute-start | bytes 1572872 | tf_op jit(solution)/shard_map/ppermute | solution.py:261
  31.8 11.7 %collective-permute-done.2.b_ref = bf16[4,256,256]{2,1,0:T(8,128)(2,1)S(1)} collective-permute-done((bf16[4,256,256]{2,1,0:T(8,128)(2,1)S(1)}, bf16[4,256,256]{2,1,0:T(8,128)(2,1)S(1)}, u32[]{:S(2)}, u32[]{:S(2)}) %collective-permute-start.2) | collective-permute-done | bytes 524320 | tf_op jit(solution)/shard_map/ppermute | solution.py:261
  43.5 0.1 shard_map.79
  43.6 2.6 %collective-permute-start.3 = (bf16[8,256,256]{2,1,0:T(8,128)(2,1)S(1)}, bf16[8,256,256]{2,1,0:T(8,128)(2,1)S(1)}, u32[]{:S(2)}, u32[]{:S(2)}) collective-permute-start(bf16[8,256,256]{2,1,0:T(8,128)(2,1)S(1)} %get-tuple-element.37.x_ref.refs_0_), channel_id=1, source_target_pairs={{0,30},{1,3},{2,0},{3,5},{4,2},{5,7},{6,4},{7,9},{8,6},{9,11},{10,... | collective-permute-start | bytes 3145736 | tf_op jit(solution)/shard_map/ppermute | solution.py:261
  46.2 5.2 %collective-permute-start.4 = (bf16[256,256]{1,0:T(8,128)(2,1)S(1)}, bf16[256,256]{1,0:T(8,128)(2,1)S(1)}, u32[]{:S(2)}, u32[]{:S(2)}) collective-permute-start(bf16[256,256]{1,0:T(8,128)(2,1)S(1)} %get-tuple-element.35), channel_id=1, source_target_pairs={{0,28},{1,5},{2,30},{3,7},{4,0},{5,9},{6,2},{7,11},{8,4},{9,13},{1... | collective-permute-start | bytes 393224 | tf_op jit(solution)/shard_map/ppermute | solution.py:261
  51.5 5.5 %collective-permute-start.5 = (bf16[8,256,256]{2,1,0:T(8,128)(2,1)S(1)}, bf16[8,256,256]{2,1,0:T(8,128)(2,1)S(1)}, u32[]{:S(2)}, u32[]{:S(2)}) collective-permute-start(bf16[8,256,256]{2,1,0:T(8,128)(2,1)S(1)} %get-tuple-element.37.x_ref.refs_0_), channel_id=1, source_target_pairs={{0,1},{1,0},{2,3},{3,2},{4,5},{5,4},{6,7},{7,6},{8,9},{9,8},{10,11... | collective-permute-start | bytes 3145736 | tf_op jit(solution)/shard_map/ppermute | solution.py:261
  57.0 0.7 shard_map.80.so_far
  57.7 1.9 %collective-permute-start.8 = (bf16[17,512,256]{2,1,0:T(8,128)(2,1)S(1)}, bf16[17,512,256]{2,1,0:T(8,128)(2,1)S(1)}, u32[]{:S(2)}, u32[]{:S(2)}) collective-permute-start(bf16[17,512,256]{2,1,0:T(8,128)(2,1)S(1)} %get-tuple-element.45), channel_id=1, source_target_pairs={{0,1},{1,0},{2,3},{3,2},{4,5},{5,4},{6,7},{7,6},{8,9},{9,8},{10,11... | collective-permute-start | bytes 13369352 | tf_op jit(solution)/shard_map/ppermute | solution.py:261
  59.6 5.1 %collective-permute-done.4.b_ref = bf16[256,256]{1,0:T(8,128)(2,1)S(1)} collective-permute-done((bf16[256,256]{1,0:T(8,128)(2,1)S(1)}, bf16[256,256]{1,0:T(8,128)(2,1)S(1)}, u32[]{:S(2)}, u32[]{:S(2)}) %collective-permute-start.4) | collective-permute-done | bytes 131104 | tf_op jit(solution)/shard_map/ppermute | solution.py:261
  64.8 0.0 collective-permute-done.3.a_ref
  64.8 0.1 shard_map.81.x_ref.refs_1_
  64.8 3.0 %collective-permute-start.6 = (bf16[9,256,256]{2,1,0:T(8,128)(2,1)S(1)}, bf16[9,256,256]{2,1,0:T(8,128)(2,1)S(1)}, u32[]{:S(2)}, u32[]{:S(2)}) collective-permute-start(bf16[9,256,256]{2,1,0:T(8,128)(2,1)S(1)} %shard_map.81.x_ref.refs_1_), channel_id=1, source_target_pairs={{0,1},{1,0},{2,3},{3,2},{4,5},{5,4},{6,7},{7,6},{8,9},{9,8},{10,11... | collective-permute-start | bytes 3538952 | tf_op jit(solution)/shard_map/ppermute | solution.py:261
  67.9 0.8 shard_map.82.so_far
  68.7 0.0 copy-start.1
  68.7 0.0 collective-permute-done.5.x_ref.refs_2_
  68.7 0.7 shard_map.83.so_far
  69.4 0.9 collective-permute-done.6.x_ref.refs_3_
  70.3 1.6 %shard_map.84 = (bf16[256,512]{1,0:T(8,128)(2,1)}, bf16[256,512]{1,0:T(8,128)(2,1)S(1)}) custom-call(f32[256,512]{1,0:T(8,128)S(1)} %shard_map.83.so_far, bf16[9,256,256]{2,1,0:T(8,128)(2,1)S(1)} %collective-permute-done.6.x_ref.refs_3_, bf16[8704,512]{1,0:T(8,128)(2,1)S(1)} %get-tuple-element.38.up_ref, bf16[256,512]{1,0:T(8,128)(2,1)S(1)} %copy-done.1), custom_call_target="tpu_custom_call" | custom-call | flops 268435456 | bytes 4194304 | tf_op jit(solution)/shard_map/pallas_call | solution.py:310
  71.9 2.3 %collective-permute-start.7 = (bf16[256,512]{1,0:T(8,128)(2,1)S(1)}, bf16[256,512]{1,0:T(8,128)(2,1)S(1)}, u32[]{:S(2)}, u32[]{:S(2)}) collective-permute-start(bf16[256,512]{1,0:T(8,128)(2,1)S(1)} %get-tuple-element.54.pg_ref), channel_id=1, source_target_pairs={{0,1},{1,0},{2,3},{3,2},{4,5},{5,4},{6,7},{7,6},{8,9},{9,8},{10,11... | collective-permute-start | bytes 786440 | tf_op jit(solution)/shard_map/ppermute | solution.py:261
  74.2 1.1 collective-permute-done.7.pg2_ref
  75.4 0.0 collective-permute-done.8.sibling_ref
  75.4 2.4 %shard_map.85 = (bf16[8,256,256]{2,1,0:T(8,128)(2,1)}, bf16[256,256]{1,0:T(8,128)(2,1)S(1)}) custom-call(bf16[256,512]{1,0:T(8,128)(2,1)S(1)} %get-tuple-element.54.pg_ref, bf16[256,512]{1,0:T(8,128)(2,1)S(1)} %collective-permute-done.7.pg2_ref, bf16[17,512,256]{2,1,0:T(8,128)(2,1)S(1)} %get-tuple-element.44.own_ref, ...), custom_call_target="tpu_custom_call" | custom-call | flops 603979776 | bytes 4194304 | tf_op jit(solution)/shard_map/pallas_call | solution.py:320
  77.7 1.9 %collective-permute-start.9 = (bf16[8,256,256]{2,1,0:T(8,128)(2,1)}, bf16[8,256,256]{2,1,0:T(8,128)(2,1)S(1)}, u32[]{:S(2)}, u32[]{:S(2)}) collective-permute-start(bf16[8,256,256]{2,1,0:T(8,128)(2,1)} %get-tuple-element.46), channel_id=1, source_target_pairs={{0,2},{1,31},{2,4},{3,1},{4,6},{5,3},{6,8},{7,5},{8,10},{9,7},{10,... | collective-permute-start | bytes 3145736 | tf_op jit(solution)/shard_map/ppermute | solution.py:261
  79.7 1.2 shard_map.86.d_ref
  80.9 6.0 %collective-permute-start.10 = (bf16[256,256]{1,0:T(8,128)(2,1)S(1)}, bf16[256,256]{1,0:T(8,128)(2,1)S(1)}, u32[]{:S(2)}, u32[]{:S(2)}) collective-permute-start(bf16[256,256]{1,0:T(8,128)(2,1)S(1)} %get-tuple-element.49), channel_id=1, source_target_pairs={{0,4},{1,29},{2,6},{3,31},{4,8},{5,1},{6,10},{7,3},{8,12},{9,5},{1... | collective-permute-start | bytes 393224 | tf_op jit(solution)/shard_map/ppermute | solution.py:261
  86.9 6.0 %shard_map.90 = bf16[80,128,128]{2,1,0:T(8,128)(2,1)S(1)} custom-call(s32[2,80]{1,0:T(2,128)} %bitcast.11, bf16[256,512]{1,0:T(8,128)(2,1)S(1)} %get-tuple-element.54.pg_ref, bf16[8,256,256]{2,1,0:T(8,128)(2,1)S(1)} %get-tuple-element.37.x_ref.refs_0_, bf16[9,256,256]{2,1,0:T(8,128)(2,1)S(1)} %shard_map.81.x_ref.refs_1_, ...), custom_call_target="tpu_custom_call" | custom-call | flops 2147483648 | bytes 16777216 | tf_op jit(solution)/shard_map/pallas_call | solution.py:326
  93.0 1.6 %copy-done = bf16[80,128,128]{2,1,0:T(8,128)(2,1)} copy-done((bf16[80,128,128]{2,1,0:T(8,128)(2,1)}, bf16[80,128,128]{2,1,0:T(8,128)(2,1)S(1)}, u32[]{:S(2)}) %copy-start) | copy-done | bytes 2621464
  94.5 5.8 %all-to-all-start = ((bf16[80,128,128]{2,1,0:T(8,128)(2,1)}), bf16[80,128,128]{2,1,0:T(8,128)(2,1)}, u32[]{:S(2)}, u32[]{:S(2)}) async-start(bf16[80,128,128]{2,1,0:T(8,128)(2,1)} %copy-done), calls=%async_computation | async-start | bytes 5242880 | tf_op jit(solution)/shard_map/all_to_all | solution.py:334
  100.4 0.0 collective-permute-done.10.r8_ref
  100.4 0.0 collective-permute-done.9.r1_ref
  100.4 0.1 shard_map.87
  100.5 4.2 %collective-permute-start.11 = (bf16[4,256,256]{2,1,0:T(8,128)(2,1)S(1)}, bf16[4,256,256]{2,1,0:T(8,128)(2,1)S(1)}, u32[]{:S(2)}, u32[]{:S(2)}) collective-permute-start(bf16[4,256,256]{2,1,0:T(8,128)(2,1)S(1)} %shard_map.87), channel_id=1, source_target_pairs={{0,4},{1,29},{2,6},{3,31},{4,8},{5,1},{6,10},{7,3},{8,12},{9,5},{1... | collective-permute-start | bytes 1572872 | tf_op jit(solution)/shard_map/ppermute | solution.py:261
  104.7 13.2 %collective-permute-done.11.r2_ref = bf16[4,256,256]{2,1,0:T(8,128)(2,1)S(1)} collective-permute-done((bf16[4,256,256]{2,1,0:T(8,128)(2,1)S(1)}, bf16[4,256,256]{2,1,0:T(8,128)(2,1)S(1)}, u32[]{:S(2)}, u32[]{:S(2)}) %collective-permute-start.11) | collective-permute-done | bytes 524320 | tf_op jit(solution)/shard_map/ppermute | solution.py:261
  118.0 0.2 shard_map.88
  118.1 3.6 %collective-permute-start.12 = (bf16[2,256,256]{2,1,0:T(8,128)(2,1)S(1)}, bf16[2,256,256]{2,1,0:T(8,128)(2,1)S(1)}, u32[]{:S(2)}, u32[]{:S(2)}) collective-permute-start(bf16[2,256,256]{2,1,0:T(8,128)(2,1)S(1)} %get-tuple-element.51), channel_id=1, source_target_pairs={{0,8},{1,25},{2,10},{3,27},{4,12},{5,29},{6,14},{7,31},{8,16},{9,1... | collective-permute-start | bytes 786440 | tf_op jit(solution)/shard_map/ppermute | solution.py:261
  121.8 14.4 %collective-permute-done.12.r3_ref = bf16[2,256,256]{2,1,0:T(8,128)(2,1)S(1)} collective-permute-done((bf16[2,256,256]{2,1,0:T(8,128)(2,1)S(1)}, bf16[2,256,256]{2,1,0:T(8,128)(2,1)S(1)}, u32[]{:S(2)}, u32[]{:S(2)}) %collective-permute-start.12) | collective-permute-done | bytes 262176 | tf_op jit(solution)/shard_map/ppermute | solution.py:261
  136.2 0.1 shard_map.89
  136.2 7.6 %collective-permute-start.13 = (bf16[256,256]{1,0:T(8,128)(2,1)S(1)}, bf16[256,256]{1,0:T(8,128)(2,1)S(1)}, u32[]{:S(2)}, u32[]{:S(2)}) collective-permute-start(bf16[256,256]{1,0:T(8,128)(2,1)S(1)} %get-tuple-element.53), channel_id=1, source_target_pairs={{0,1},{1,0},{2,3},{3,2},{4,5},{5,4},{6,7},{7,6},{8,9},{9,8},{10,11... | collective-permute-start | bytes 393224 | tf_op jit(solution)/shard_map/ppermute | solution.py:261
  143.8 0.0 all-to-all-done
  143.8 2.9 %shard_map.91 = f32[5,128,128]{2,1,0:T(8,128)} custom-call(bf16[16,5,128,128]{3,2,1,0:T(8,128)(2,1)} %bitcast.4.in_ref), custom_call_target="tpu_custom_call" | custom-call | tf_op jit(solution)/shard_map/pallas_call | solution.py:339
  146.7 0.0 collective-permute-done.13.cross_ref
  146.7 0.7 shard_map.92
  (5 shorter events, 0.1 us)
Async XLA Ops:
  0.6 3.8 %collective-permute-start = (bf16[256,256]{1,0:T(8,128)(2,1)}, bf16[256,256]{1,0:T(8,128)(2,1)S(1)}, u32[]{:S(2)}, u32[]{:S(2)}) collective-permute-start(bf16[256,256]{1,0:T(8,128)(2,1)} %a_ref.1), channel_id=1, source_target_pairs={{0,1},{1,0},{2,3},{3,2},{4,5},{5,4},{6,7},{7,6},{8,9},{9,8},{10,11... | collective-permute-start | bytes 393224 | tf_op jit(solution)/shard_map/ppermute | solution.py:261
  4.4 0.9 copy-start.2
  5.3 21.1 %collective-permute-start.1 = (bf16[2,256,256]{2,1,0:T(8,128)(2,1)S(1)}, bf16[2,256,256]{2,1,0:T(8,128)(2,1)S(1)}, u32[]{:S(2)}, u32[]{:S(2)}) collective-permute-start(bf16[2,256,256]{2,1,0:T(8,128)(2,1)S(1)} %shard_map.76.a_ref), channel_id=1, source_target_pairs={{0,24},{1,9},{2,26},{3,11},{4,28},{5,13},{6,30},{7,15},{8,0},{9,17... | collective-permute-start | bytes 786440 | tf_op jit(solution)/shard_map/ppermute | solution.py:261
  26.5 17.1 %collective-permute-start.2 = (bf16[4,256,256]{2,1,0:T(8,128)(2,1)S(1)}, bf16[4,256,256]{2,1,0:T(8,128)(2,1)S(1)}, u32[]{:S(2)}, u32[]{:S(2)}) collective-permute-start(bf16[4,256,256]{2,1,0:T(8,128)(2,1)S(1)} %shard_map.78.a_ref), channel_id=1, source_target_pairs={{0,28},{1,5},{2,30},{3,7},{4,0},{5,9},{6,2},{7,11},{8,4},{9,13},{1... | collective-permute-start | bytes 1572872 | tf_op jit(solution)/shard_map/ppermute | solution.py:261
  43.6 21.2 %collective-permute-start.3 = (bf16[8,256,256]{2,1,0:T(8,128)(2,1)S(1)}, bf16[8,256,256]{2,1,0:T(8,128)(2,1)S(1)}, u32[]{:S(2)}, u32[]{:S(2)}) collective-permute-start(bf16[8,256,256]{2,1,0:T(8,128)(2,1)S(1)} %get-tuple-element.37.x_ref.refs_0_), channel_id=1, source_target_pairs={{0,30},{1,3},{2,0},{3,5},{4,2},{5,7},{6,4},{7,9},{8,6},{9,11},{10,... | collective-permute-start | bytes 3145736 | tf_op jit(solution)/shard_map/ppermute | solution.py:261
  46.2 18.5 %collective-permute-start.4 = (bf16[256,256]{1,0:T(8,128)(2,1)S(1)}, bf16[256,256]{1,0:T(8,128)(2,1)S(1)}, u32[]{:S(2)}, u32[]{:S(2)}) collective-permute-start(bf16[256,256]{1,0:T(8,128)(2,1)S(1)} %get-tuple-element.35), channel_id=1, source_target_pairs={{0,28},{1,5},{2,30},{3,7},{4,0},{5,9},{6,2},{7,11},{8,4},{9,13},{1... | collective-permute-start | bytes 393224 | tf_op jit(solution)/shard_map/ppermute | solution.py:261
  51.5 17.2 %collective-permute-start.5 = (bf16[8,256,256]{2,1,0:T(8,128)(2,1)S(1)}, bf16[8,256,256]{2,1,0:T(8,128)(2,1)S(1)}, u32[]{:S(2)}, u32[]{:S(2)}) collective-permute-start(bf16[8,256,256]{2,1,0:T(8,128)(2,1)S(1)} %get-tuple-element.37.x_ref.refs_0_), channel_id=1, source_target_pairs={{0,1},{1,0},{2,3},{3,2},{4,5},{5,4},{6,7},{7,6},{8,9},{9,8},{10,11... | collective-permute-start | bytes 3145736 | tf_op jit(solution)/shard_map/ppermute | solution.py:261
  57.7 17.7 %collective-permute-start.8 = (bf16[17,512,256]{2,1,0:T(8,128)(2,1)S(1)}, bf16[17,512,256]{2,1,0:T(8,128)(2,1)S(1)}, u32[]{:S(2)}, u32[]{:S(2)}) collective-permute-start(bf16[17,512,256]{2,1,0:T(8,128)(2,1)S(1)} %get-tuple-element.45), channel_id=1, source_target_pairs={{0,1},{1,0},{2,3},{3,2},{4,5},{5,4},{6,7},{7,6},{8,9},{9,8},{10,11... | collective-permute-start | bytes 13369352 | tf_op jit(solution)/shard_map/ppermute | solution.py:261
  64.8 5.5 %collective-permute-start.6 = (bf16[9,256,256]{2,1,0:T(8,128)(2,1)S(1)}, bf16[9,256,256]{2,1,0:T(8,128)(2,1)S(1)}, u32[]{:S(2)}, u32[]{:S(2)}) collective-permute-start(bf16[9,256,256]{2,1,0:T(8,128)(2,1)S(1)} %shard_map.81.x_ref.refs_1_), channel_id=1, source_target_pairs={{0,1},{1,0},{2,3},{3,2},{4,5},{5,4},{6,7},{7,6},{8,9},{9,8},{10,11... | collective-permute-start | bytes 3538952 | tf_op jit(solution)/shard_map/ppermute | solution.py:261
  68.7 1.7 %copy-start.1 = (bf16[256,512]{1,0:T(8,128)(2,1)S(1)}, bf16[256,512]{1,0:T(8,128)(2,1)}, u32[]{:S(2)}) copy-start(bf16[256,512]{1,0:T(8,128)(2,1)} %og_ref.1) | copy-start | bytes 786436
  71.9 3.4 %collective-permute-start.7 = (bf16[256,512]{1,0:T(8,128)(2,1)S(1)}, bf16[256,512]{1,0:T(8,128)(2,1)S(1)}, u32[]{:S(2)}, u32[]{:S(2)}) collective-permute-start(bf16[256,512]{1,0:T(8,128)(2,1)S(1)} %get-tuple-element.54.pg_ref), channel_id=1, source_target_pairs={{0,1},{1,0},{2,3},{3,2},{4,5},{5,4},{6,7},{7,6},{8,9},{9,8},{10,11... | collective-permute-start | bytes 786440 | tf_op jit(solution)/shard_map/ppermute | solution.py:261
  77.7 22.6 %collective-permute-start.9 = (bf16[8,256,256]{2,1,0:T(8,128)(2,1)}, bf16[8,256,256]{2,1,0:T(8,128)(2,1)S(1)}, u32[]{:S(2)}, u32[]{:S(2)}) collective-permute-start(bf16[8,256,256]{2,1,0:T(8,128)(2,1)} %get-tuple-element.46), channel_id=1, source_target_pairs={{0,2},{1,31},{2,4},{3,1},{4,6},{5,3},{6,8},{7,5},{8,10},{9,7},{10,... | collective-permute-start | bytes 3145736 | tf_op jit(solution)/shard_map/ppermute | solution.py:261
  80.9 19.4 %collective-permute-start.10 = (bf16[256,256]{1,0:T(8,128)(2,1)S(1)}, bf16[256,256]{1,0:T(8,128)(2,1)S(1)}, u32[]{:S(2)}, u32[]{:S(2)}) collective-permute-start(bf16[256,256]{1,0:T(8,128)(2,1)S(1)} %get-tuple-element.49), channel_id=1, source_target_pairs={{0,4},{1,29},{2,6},{3,31},{4,8},{5,1},{6,10},{7,3},{8,12},{9,5},{1... | collective-permute-start | bytes 393224 | tf_op jit(solution)/shard_map/ppermute | solution.py:261
  92.9 1.6 %copy-start = (bf16[80,128,128]{2,1,0:T(8,128)(2,1)}, bf16[80,128,128]{2,1,0:T(8,128)(2,1)S(1)}, u32[]{:S(2)}) copy-start(bf16[80,128,128]{2,1,0:T(8,128)(2,1)S(1)} %shard_map.90) | copy-start | bytes 7864324
  94.5 49.3 %all-to-all-start = ((bf16[80,128,128]{2,1,0:T(8,128)(2,1)}), bf16[80,128,128]{2,1,0:T(8,128)(2,1)}, u32[]{:S(2)}, u32[]{:S(2)}) async-start(bf16[80,128,128]{2,1,0:T(8,128)(2,1)} %copy-done), calls=%async_computation | async-start | bytes 5242880 | tf_op jit(solution)/shard_map/all_to_all | solution.py:334
  100.5 17.5 %collective-permute-start.11 = (bf16[4,256,256]{2,1,0:T(8,128)(2,1)S(1)}, bf16[4,256,256]{2,1,0:T(8,128)(2,1)S(1)}, u32[]{:S(2)}, u32[]{:S(2)}) collective-permute-start(bf16[4,256,256]{2,1,0:T(8,128)(2,1)S(1)} %shard_map.87), channel_id=1, source_target_pairs={{0,4},{1,29},{2,6},{3,31},{4,8},{5,1},{6,10},{7,3},{8,12},{9,5},{1... | collective-permute-start | bytes 1572872 | tf_op jit(solution)/shard_map/ppermute | solution.py:261
  118.1 18.0 %collective-permute-start.12 = (bf16[2,256,256]{2,1,0:T(8,128)(2,1)S(1)}, bf16[2,256,256]{2,1,0:T(8,128)(2,1)S(1)}, u32[]{:S(2)}, u32[]{:S(2)}) collective-permute-start(bf16[2,256,256]{2,1,0:T(8,128)(2,1)S(1)} %get-tuple-element.51), channel_id=1, source_target_pairs={{0,8},{1,25},{2,10},{3,27},{4,12},{5,29},{6,14},{7,31},{8,16},{9,1... | collective-permute-start | bytes 786440 | tf_op jit(solution)/shard_map/ppermute | solution.py:261
  136.2 10.5 %collective-permute-start.13 = (bf16[256,256]{1,0:T(8,128)(2,1)S(1)}, bf16[256,256]{1,0:T(8,128)(2,1)S(1)}, u32[]{:S(2)}, u32[]{:S(2)}) collective-permute-start(bf16[256,256]{1,0:T(8,128)(2,1)S(1)} %get-tuple-element.53), channel_id=1, source_target_pairs={{0,1},{1,0},{2,3},{3,2},{4,5},{5,4},{6,7},{7,6},{8,9},{9,8},{10,11... | collective-permute-start | bytes 393224 | tf_op jit(solution)/shard_map/ppermute | solution.py:261

commit v9 on v6

--- a/solution.py
+++ b/solution.py
@@ -169,13 +169,13 @@
 
 def add_first(d_ref, r1_ref, out_ref):
     for n in range(4):
-        out_ref[n] = (d_ref[4 + n] + f32(r1_ref[4 + n])).astype(BF16)
+        out_ref[n] = (f32(d_ref[4 + n]) + f32(r1_ref[4 + n])).astype(BF16)
 
 
 def add_second(d_ref, r1_ref, r2_ref, next_ref, base_ref):
     for n in range(2):
-        base_ref[n] = (d_ref[n] + f32(r1_ref[n]) + f32(r2_ref[n])).astype(BF16)
-        next_ref[n] = (d_ref[2 + n] + f32(r1_ref[2 + n]) + f32(r2_ref[2 + n])).astype(BF16)
+        base_ref[n] = (f32(d_ref[n]) + f32(r1_ref[n]) + f32(r2_ref[n])).astype(BF16)
+        next_ref[n] = (f32(d_ref[2 + n]) + f32(r1_ref[2 + n]) + f32(r2_ref[2 + n])).astype(BF16)
 
 
 def add_third(base_ref, hop_ref, r3_ref, cross_ref, own_ref):
@@ -312,7 +312,7 @@
     d1 = back_of(8, BF16)
     r1 = steps(d1, 1)
     pg, d1 = together((pg, d1))
-    d2 = back_of(0, F32)
+    d2 = back_of(0, BF16)
     pg, d2 = together((pg, d2))
     terms = kernel(
         weight_terms, shape(slots, blk, blk), ins=[HBM], n_in=5, mib=14,

time: 145 us -> 144 us (level)
  Pallas kernels: 25.7 us -> 23.2 us
  transfers between devices with their start and end apart: 15 -> 15, of which waited for: 11 -> 11; matrix products, arithmetic and copies ran while one was open for 0% -> 0% of each run, Pallas kernels for 16% -> 15%
where the time goes in v9:
time: 144 us; the launch traced here: 143 us
  waiting for transfers between devices  59.1 us (41%)
  starting transfers between devices  57.4 us (40%)
  Pallas kernels  23.2 us (16%)
  local copies, waits for them, and re-layouts  2.44 us (2%)
    ppermute x14, waiting for transfers between devices, send(): return lax.ppermute(v, 'blk', pairs)  51 us
    ppermute x14, starting transfers between devices, send(): return lax.ppermute(v, 'blk', pairs)  50.7 us
    all_to_all x1, waiting for transfers between devices, on_device(): got = lax.all_to_all(terms, 'dp', 0, 0, tiled=True)  8.16 us
    pallas_call x1, Pallas kernels, on_device(): kernel(lay_weights, (shape(2 * NZ * feats, width),) + (shape(NZ, width, f...  7.33 us
    all_to_all x1, starting transfers between devices, on_device(): got = lax.all_to_all(terms, 'dp', 0, 0, tiled=True)  6.7 us
    pallas_call x1, Pallas kernels, on_device(): kernel(weight_terms, shape(slots, blk, blk), ins=[HBM], n_in=5, mib=14, f...  5.69 us
    pallas_call x1, Pallas kernels, on_device(): kernel(functools.partial(add_terms, 1.0 / (tok_rows * n_dp) ** 0.5), shap...  2.88 us
  transfers between devices with their start and end apart: 15, of which 11 were waited for; matrix products, arithmetic and copies ran while one was open for 0% of the time, Pallas kernels for 15%

profile of v9, /device:TPU:1, one launch (start us, length us, event | category | flops | bytes accessed | tf_op | source)
XLA Modules:
  0.0 143.0 jit_solution(2358797716428481606)
XLA Ops:
  0.6 8.8 %collective-permute-start = (bf16[256,256]{1,0:T(8,128)(2,1)}, bf16[256,256]{1,0:T(8,128)(2,1)S(1)}, u32[]{:S(2)}, u32[]{:S(2)}) collective-permute-start(bf16[256,256]{1,0:T(8,128)(2,1)} %a_ref.1), channel_id=1, source_target_pairs={{0,1},{1,0},{2,3},{3,2},{4,5},{5,4},{6,7},{7,6},{8,9},{9,8},{10,11... | collective-permute-start | bytes 393224 | tf_op jit(solution)/shard_map/ppermute | solution.py:251
  9.4 1.2 collective-permute-done.b_ref
  10.6 0.9 copy-done.2
  11.5 4.8 %collective-permute-start.2 = (bf16[2,256,256]{2,1,0:T(8,128)(2,1)S(1)}, bf16[2,256,256]{2,1,0:T(8,128)(2,1)S(1)}, u32[]{:S(2)}, u32[]{:S(2)}) collective-permute-start(bf16[2,256,256]{2,1,0:T(8,128)(2,1)S(1)} %shard_map.76.pair_ref), channel_id=1, source_target_pairs={{0,24},{1,11},{2,26},{3,13},{4,28},{5,15},{6,30},{7,17},{8,0},{9,1... | collective-permute-start | bytes 786440 | tf_op jit(solution)/shard_map/ppermute | solution.py:251
  16.3 3.5 %collective-permute-start.1 = (bf16[2,256,256]{2,1,0:T(8,128)(2,1)S(1)}, bf16[2,256,256]{2,1,0:T(8,128)(2,1)S(1)}, u32[]{:S(2)}, u32[]{:S(2)}) collective-permute-start(bf16[2,256,256]{2,1,0:T(8,128)(2,1)S(1)} %shard_map.76.pair_ref), channel_id=1, source_target_pairs={{1,3},{3,5},{5,7},{7,9},{9,11},{11,13},{13,15},{15,17},{17,19},{19... | collective-permute-start | bytes 786440 | tf_op jit(solution)/shard_map/ppermute | solution.py:251
  19.9 7.3 %shard_map.77 = (bf16[8192,512]{1,0:T(8,128)(2,1)S(1)}, bf16[16,512,256]{2,1,0:T(8,128)(2,1)S(1)}, bf16[16,512,256]{2,1,0:T(8,128)(2,1)S(1)}) custom-call(s32[2,80]{1,0:T(2,128)} %bitcast.10, s32[2,32]{1,0:T(2,128)} %bitcast.9, bf16[80,128,128]{2,1,0:T(8,128)(2,1)} %bitcast.7), custom_call_target="tpu_custom_call" | custom-call | bytes 20971520 | tf_op jit(solution)/shard_map/pallas_call | solution.py:274
  27.2 1.1 collective-permute-done.2.g4_ref
  28.3 6.9 %collective-permute-done.1.hop_ref = bf16[2,256,256]{2,1,0:T(8,128)(2,1)S(1)} collective-permute-done((bf16[2,256,256]{2,1,0:T(8,128)(2,1)S(1)}, bf16[2,256,256]{2,1,0:T(8,128)(2,1)S(1)}, u32[]{:S(2)}, u32[]{:S(2)}) %collective-permute-start.1) | collective-permute-done | bytes 262176 | tf_op jit(solution)/shard_map/ppermute | solution.py:251
  35.3 3.2 %collective-permute-start.3 = (bf16[4,256,256]{2,1,0:T(8,128)(2,1)S(1)}, bf16[4,256,256]{2,1,0:T(8,128)(2,1)S(1)}, u32[]{:S(2)}, u32[]{:S(2)}) collective-permute-start(bf16[4,256,256]{2,1,0:T(8,128)(2,1)S(1)} %shard_map.78.a_ref), channel_id=1, source_target_pairs={{0,28},{1,5},{2,30},{3,7},{4,0},{5,9},{6,2},{7,11},{8,4},{9,13},{1... | collective-permute-start | bytes 1572872 | tf_op jit(solution)/shard_map/ppermute | solution.py:251
  38.5 13.7 %collective-permute-done.3.b_ref = bf16[4,256,256]{2,1,0:T(8,128)(2,1)S(1)} collective-permute-done((bf16[4,256,256]{2,1,0:T(8,128)(2,1)S(1)}, bf16[4,256,256]{2,1,0:T(8,128)(2,1)S(1)}, u32[]{:S(2)}, u32[]{:S(2)}) %collective-permute-start.3) | collective-permute-done | bytes 524320 | tf_op jit(solution)/shard_map/ppermute | solution.py:251
  52.2 0.1 shard_map.79.x_ref.refs_0_
  52.3 1.9 %collective-permute-start.4 = (bf16[8,256,256]{2,1,0:T(8,128)(2,1)S(1)}, bf16[8,256,256]{2,1,0:T(8,128)(2,1)S(1)}, u32[]{:S(2)}, u32[]{:S(2)}) collective-permute-start(bf16[8,256,256]{2,1,0:T(8,128)(2,1)S(1)} %shard_map.79.x_ref.refs_0_), channel_id=1, source_target_pairs={{0,30},{1,3},{2,0},{3,5},{4,2},{5,7},{6,4},{7,9},{8,6},{9,11},{10,... | collective-permute-start | bytes 3145736 | tf_op jit(solution)/shard_map/ppermute | solution.py:251
  54.2 2.0 %collective-permute-start.5 = (bf16[8,256,256]{2,1,0:T(8,128)(2,1)S(1)}, bf16[8,256,256]{2,1,0:T(8,128)(2,1)S(1)}, u32[]{:S(2)}, u32[]{:S(2)}) collective-permute-start(bf16[8,256,256]{2,1,0:T(8,128)(2,1)S(1)} %shard_map.79.x_ref.refs_0_), channel_id=1, source_target_pairs={{0,1},{1,0},{2,3},{3,2},{4,5},{5,4},{6,7},{7,6},{8,9},{9,8},{10,11... | collective-permute-start | bytes 3145736 | tf_op jit(solution)/shard_map/ppermute | solution.py:251
  56.2 0.7 shard_map.80.so_far
  56.9 2.3 %collective-permute-start.8 = (bf16[16,512,256]{2,1,0:T(8,128)(2,1)S(1)}, bf16[16,512,256]{2,1,0:T(8,128)(2,1)S(1)}, u32[]{:S(2)}, u32[]{:S(2)}) collective-permute-start(bf16[16,512,256]{2,1,0:T(8,128)(2,1)S(1)} %get-tuple-element.38), channel_id=1, source_target_pairs={{0,1},{1,0},{2,3},{3,2},{4,5},{5,4},{6,7},{7,6},{8,9},{9,8},{10,11... | collective-permute-start | bytes 12582920 | tf_op jit(solution)/shard_map/ppermute | solution.py:251
  59.3 9.8 %collective-permute-done.4.x_ref.refs_1_ = bf16[8,256,256]{2,1,0:T(8,128)(2,1)S(1)} collective-permute-done((bf16[8,256,256]{2,1,0:T(8,128)(2,1)S(1)}, bf16[8,256,256]{2,1,0:T(8,128)(2,1)S(1)}, u32[]{:S(2)}, u32[]{:S(2)}) %collective-permute-start.4) | collective-permute-done | bytes 1048608 | tf_op jit(solution)/shard_map/ppermute | solution.py:251
  69.0 1.9 %collective-permute-start.6 = (bf16[8,256,256]{2,1,0:T(8,128)(2,1)S(1)}, bf16[8,256,256]{2,1,0:T(8,128)(2,1)S(1)}, u32[]{:S(2)}, u32[]{:S(2)}) collective-permute-start(bf16[8,256,256]{2,1,0:T(8,128)(2,1)S(1)} %collective-permute-done.4.x_ref.refs_1_), channel_id=1, source_target_pairs={{0,1},{1,0},{2,3},{3,2},{4,5},{5,4},{6,7},{7,6},{8,9},{9,8},{10,11... | collective-permute-start | bytes 3145736 | tf_op jit(solution)/shard_map/ppermute | solution.py:251
  71.0 0.7 shard_map.81.so_far
  71.7 0.0 copy-start.1
  71.7 0.0 collective-permute-done.5.x_ref.refs_2_
  71.7 0.7 shard_map.82.so_far
  72.4 1.2 collective-permute-done.6.x_ref.refs_3_
  73.6 0.0 copy-done.1
  73.6 1.5 %shard_map.83 = (bf16[256,512]{1,0:T(8,128)(2,1)}, bf16[256,512]{1,0:T(8,128)(2,1)S(1)}) custom-call(f32[256,512]{1,0:T(8,128)S(1)} %shard_map.82.so_far, bf16[8,256,256]{2,1,0:T(8,128)(2,1)S(1)} %collective-permute-done.6.x_ref.refs_3_, bf16[8192,512]{1,0:T(8,128)(2,1)S(1)} %get-tuple-element.32.up_ref, bf16[256,512]{1,0:T(8,128)(2,1)S(1)} %copy-done.1), custom_call_target="tpu_custom_call" | custom-call | flops 268435456 | bytes 4194304 | tf_op jit(solution)/shard_map/pallas_call | solution.py:302
  75.1 2.0 %collective-permute-start.7 = (bf16[256,512]{1,0:T(8,128)(2,1)S(1)}, bf16[256,512]{1,0:T(8,128)(2,1)S(1)}, u32[]{:S(2)}, u32[]{:S(2)}) collective-permute-start(bf16[256,512]{1,0:T(8,128)(2,1)S(1)} %get-tuple-element.43.pg_ref), channel_id=1, source_target_pairs={{0,1},{1,0},{2,3},{3,2},{4,5},{5,4},{6,7},{7,6},{8,9},{9,8},{10,11... | collective-permute-start | bytes 786440 | tf_op jit(solution)/shard_map/ppermute | solution.py:251
  77.2 1.4 collective-permute-done.7.pg2_ref
  78.5 0.0 collective-permute-done.8.sibling_ref
  78.5 1.2 shard_map.84
  79.8 2.7 %collective-permute-start.9 = (bf16[8,256,256]{2,1,0:T(8,128)(2,1)S(1)}, bf16[8,256,256]{2,1,0:T(8,128)(2,1)S(1)}, u32[]{:S(2)}, u32[]{:S(2)}) collective-permute-start(bf16[8,256,256]{2,1,0:T(8,128)(2,1)S(1)} %shard_map.84), channel_id=1, source_target_pairs={{0,2},{1,31},{2,4},{3,1},{4,6},{5,3},{6,8},{7,5},{8,10},{9,7},{10,... | collective-permute-start | bytes 3145736 | tf_op jit(solution)/shard_map/ppermute | solution.py:251
  82.6 1.3 shard_map.85.d_ref
  83.8 5.7 %shard_map.88 = bf16[80,128,128]{2,1,0:T(8,128)(2,1)S(1)} custom-call(s32[2,80]{1,0:T(2,128)} %bitcast.11, bf16[256,512]{1,0:T(8,128)(2,1)S(1)} %get-tuple-element.43.pg_ref, bf16[8,256,256]{2,1,0:T(8,128)(2,1)S(1)} %shard_map.79.x_ref.refs_0_, bf16[8,256,256]{2,1,0:T(8,128)(2,1)S(1)} %collective-permute-done.4.x_ref.refs_1_, ...), custom_call_target="tpu_custom_call" | custom-call | flops 2147483648 | bytes 16777216 | tf_op jit(solution)/shard_map/pallas_call | solution.py:317
  89.5 1.5 %copy-done = bf16[80,128,128]{2,1,0:T(8,128)(2,1)} copy-done((bf16[80,128,128]{2,1,0:T(8,128)(2,1)}, bf16[80,128,128]{2,1,0:T(8,128)(2,1)S(1)}, u32[]{:S(2)}) %copy-start) | copy-done | bytes 2621464
  91.1 6.7 %all-to-all-start = ((bf16[80,128,128]{2,1,0:T(8,128)(2,1)}), bf16[80,128,128]{2,1,0:T(8,128)(2,1)}, u32[]{:S(2)}, u32[]{:S(2)}) async-start(bf16[80,128,128]{2,1,0:T(8,128)(2,1)} %copy-done), calls=%async_computation | async-start | bytes 5242880 | tf_op jit(solution)/shard_map/all_to_all | solution.py:325
  97.8 0.0 collective-permute-done.9.r1_ref
  97.8 0.1 shard_map.86
  97.9 3.6 %collective-permute-start.10 = (bf16[4,256,256]{2,1,0:T(8,128)(2,1)S(1)}, bf16[4,256,256]{2,1,0:T(8,128)(2,1)S(1)}, u32[]{:S(2)}, u32[]{:S(2)}) collective-permute-start(bf16[4,256,256]{2,1,0:T(8,128)(2,1)S(1)} %shard_map.86), channel_id=1, source_target_pairs={{0,4},{1,29},{2,6},{3,31},{4,8},{5,1},{6,10},{7,3},{8,12},{9,5},{1... | collective-permute-start | bytes 1572872 | tf_op jit(solution)/shard_map/ppermute | solution.py:251
  101.5 12.6 %collective-permute-done.10.r2_ref = bf16[4,256,256]{2,1,0:T(8,128)(2,1)S(1)} collective-permute-done((bf16[4,256,256]{2,1,0:T(8,128)(2,1)S(1)}, bf16[4,256,256]{2,1,0:T(8,128)(2,1)S(1)}, u32[]{:S(2)}, u32[]{:S(2)}) %collective-permute-start.10) | collective-permute-done | bytes 524320 | tf_op jit(solution)/shard_map/ppermute | solution.py:251
  114.1 0.2 shard_map.87
  114.3 8.6 %collective-permute-start.11 = (bf16[2,256,256]{2,1,0:T(8,128)(2,1)S(1)}, bf16[2,256,256]{2,1,0:T(8,128)(2,1)S(1)}, u32[]{:S(2)}, u32[]{:S(2)}) collective-permute-start(bf16[2,256,256]{2,1,0:T(8,128)(2,1)S(1)} %get-tuple-element.42), channel_id=1, source_target_pairs={{0,8},{1,23},{2,10},{3,25},{4,12},{5,27},{6,14},{7,29},{8,16},{9,3... | collective-permute-start | bytes 786440 | tf_op jit(solution)/shard_map/ppermute | solution.py:251
  122.9 3.3 %collective-permute-start.12 = (bf16[2,256,256]{2,1,0:T(8,128)(2,1)S(1)}, bf16[2,256,256]{2,1,0:T(8,128)(2,1)S(1)}, u32[]{:S(2)}, u32[]{:S(2)}) collective-permute-start(bf16[2,256,256]{2,1,0:T(8,128)(2,1)S(1)} %get-tuple-element.41.base_ref), channel_id=1, source_target_pairs={{1,31},{3,1},{5,3},{7,5},{9,7},{11,9},{13,11},{15,13},{17,15},{19,... | collective-permute-start | bytes 786440 | tf_op jit(solution)/shard_map/ppermute | solution.py:251
  126.2 8.2 %all-to-all-done = bf16[80,128,128]{2,1,0:T(8,128)(2,1)} async-done(((bf16[80,128,128]{2,1,0:T(8,128)(2,1)}), bf16[80,128,128]{2,1,0:T(8,128)(2,1)}, u32[]{:S(2)}, u32[]{:S(2)}) %all-to-all-start) | async-done | bytes 2621472 | tf_op jit(solution)/shard_map/all_to_all | solution.py:325
  134.4 2.9 %shard_map.89 = f32[5,128,128]{2,1,0:T(8,128)} custom-call(bf16[16,5,128,128]{3,2,1,0:T(8,128)(2,1)} %bitcast.4.in_ref), custom_call_target="tpu_custom_call" | custom-call | tf_op jit(solution)/shard_map/pallas_call | solution.py:331
  137.3 0.0 collective-permute-done.11.r3_ref
  137.3 1.8 %collective-permute-done.12.hop_ref = bf16[2,256,256]{2,1,0:T(8,128)(2,1)S(1)} collective-permute-done((bf16[2,256,256]{2,1,0:T(8,128)(2,1)S(1)}, bf16[2,256,256]{2,1,0:T(8,128)(2,1)S(1)}, u32[]{:S(2)}, u32[]{:S(2)}) %collective-permute-start.12) | collective-permute-done | bytes 262176 | tf_op jit(solution)/shard_map/ppermute | solution.py:251
  139.0 0.1 shard_map.90
  139.1 1.9 %collective-permute-start.13 = (bf16[256,256]{1,0:T(8,128)(2,1)S(1)}, bf16[256,256]{1,0:T(8,128)(2,1)S(1)}, u32[]{:S(2)}, u32[]{:S(2)}) collective-permute-start(bf16[256,256]{1,0:T(8,128)(2,1)S(1)} %get-tuple-element.47), channel_id=1, source_target_pairs={{0,1},{1,0},{2,3},{3,2},{4,5},{5,4},{6,7},{7,6},{8,9},{9,8},{10,11... | collective-permute-start | bytes 393224 | tf_op jit(solution)/shard_map/ppermute | solution.py:251
  141.0 1.3 collective-permute-done.13.cross_ref
  142.3 0.7 shard_map.91
  (4 shorter events, 0.1 us)
Async XLA Ops:
  0.6 10.0 %collective-permute-start = (bf16[256,256]{1,0:T(8,128)(2,1)}, bf16[256,256]{1,0:T(8,128)(2,1)S(1)}, u32[]{:S(2)}, u32[]{:S(2)}) collective-permute-start(bf16[256,256]{1,0:T(8,128)(2,1)} %a_ref.1), channel_id=1, source_target_pairs={{0,1},{1,0},{2,3},{3,2},{4,5},{5,4},{6,7},{7,6},{8,9},{9,8},{10,11... | collective-permute-start | bytes 393224 | tf_op jit(solution)/shard_map/ppermute | solution.py:251
  10.6 0.9 copy-start.2
  11.5 16.8 %collective-permute-start.2 = (bf16[2,256,256]{2,1,0:T(8,128)(2,1)S(1)}, bf16[2,256,256]{2,1,0:T(8,128)(2,1)S(1)}, u32[]{:S(2)}, u32[]{:S(2)}) collective-permute-start(bf16[2,256,256]{2,1,0:T(8,128)(2,1)S(1)} %shard_map.76.pair_ref), channel_id=1, source_target_pairs={{0,24},{1,11},{2,26},{3,13},{4,28},{5,15},{6,30},{7,17},{8,0},{9,1... | collective-permute-start | bytes 786440 | tf_op jit(solution)/shard_map/ppermute | solution.py:251
  16.3 18.9 %collective-permute-start.1 = (bf16[2,256,256]{2,1,0:T(8,128)(2,1)S(1)}, bf16[2,256,256]{2,1,0:T(8,128)(2,1)S(1)}, u32[]{:S(2)}, u32[]{:S(2)}) collective-permute-start(bf16[2,256,256]{2,1,0:T(8,128)(2,1)S(1)} %shard_map.76.pair_ref), channel_id=1, source_target_pairs={{1,3},{3,5},{5,7},{7,9},{9,11},{11,13},{13,15},{15,17},{17,19},{19... | collective-permute-start | bytes 786440 | tf_op jit(solution)/shard_map/ppermute | solution.py:251
  35.3 16.9 %collective-permute-start.3 = (bf16[4,256,256]{2,1,0:T(8,128)(2,1)S(1)}, bf16[4,256,256]{2,1,0:T(8,128)(2,1)S(1)}, u32[]{:S(2)}, u32[]{:S(2)}) collective-permute-start(bf16[4,256,256]{2,1,0:T(8,128)(2,1)S(1)} %shard_map.78.a_ref), channel_id=1, source_target_pairs={{0,28},{1,5},{2,30},{3,7},{4,0},{5,9},{6,2},{7,11},{8,4},{9,13},{1... | collective-permute-start | bytes 1572872 | tf_op jit(solution)/shard_map/ppermute | solution.py:251
  52.3 16.8 %collective-permute-start.4 = (bf16[8,256,256]{2,1,0:T(8,128)(2,1)S(1)}, bf16[8,256,256]{2,1,0:T(8,128)(2,1)S(1)}, u32[]{:S(2)}, u32[]{:S(2)}) collective-permute-start(bf16[8,256,256]{2,1,0:T(8,128)(2,1)S(1)} %shard_map.79.x_ref.refs_0_), channel_id=1, source_target_pairs={{0,30},{1,3},{2,0},{3,5},{4,2},{5,7},{6,4},{7,9},{8,6},{9,11},{10,... | collective-permute-start | bytes 3145736 | tf_op jit(solution)/shard_map/ppermute | solution.py:251
  54.2 17.5 %collective-permute-start.5 = (bf16[8,256,256]{2,1,0:T(8,128)(2,1)S(1)}, bf16[8,256,256]{2,1,0:T(8,128)(2,1)S(1)}, u32[]{:S(2)}, u32[]{:S(2)}) collective-permute-start(bf16[8,256,256]{2,1,0:T(8,128)(2,1)S(1)} %shard_map.79.x_ref.refs_0_), channel_id=1, source_target_pairs={{0,1},{1,0},{2,3},{3,2},{4,5},{5,4},{6,7},{7,6},{8,9},{9,8},{10,11... | collective-permute-start | bytes 3145736 | tf_op jit(solution)/shard_map/ppermute | solution.py:251
  56.9 21.6 %collective-permute-start.8 = (bf16[16,512,256]{2,1,0:T(8,128)(2,1)S(1)}, bf16[16,512,256]{2,1,0:T(8,128)(2,1)S(1)}, u32[]{:S(2)}, u32[]{:S(2)}) collective-permute-start(bf16[16,512,256]{2,1,0:T(8,128)(2,1)S(1)} %get-tuple-element.38), channel_id=1, source_target_pairs={{0,1},{1,0},{2,3},{3,2},{4,5},{5,4},{6,7},{7,6},{8,9},{9,8},{10,11... | collective-permute-start | bytes 12582920 | tf_op jit(solution)/shard_map/ppermute | solution.py:251
  69.0 4.5 %collective-permute-start.6 = (bf16[8,256,256]{2,1,0:T(8,128)(2,1)S(1)}, bf16[8,256,256]{2,1,0:T(8,128)(2,1)S(1)}, u32[]{:S(2)}, u32[]{:S(2)}) collective-permute-start(bf16[8,256,256]{2,1,0:T(8,128)(2,1)S(1)} %collective-permute-done.4.x_ref.refs_1_), channel_id=1, source_target_pairs={{0,1},{1,0},{2,3},{3,2},{4,5},{5,4},{6,7},{7,6},{8,9},{9,8},{10,11... | collective-permute-start | bytes 3145736 | tf_op jit(solution)/shard_map/ppermute | solution.py:251
  71.7 1.9 %copy-start.1 = (bf16[256,512]{1,0:T(8,128)(2,1)S(1)}, bf16[256,512]{1,0:T(8,128)(2,1)}, u32[]{:S(2)}) copy-start(bf16[256,512]{1,0:T(8,128)(2,1)} %og_ref.1) | copy-start | bytes 786436
  75.1 3.4 %collective-permute-start.7 = (bf16[256,512]{1,0:T(8,128)(2,1)S(1)}, bf16[256,512]{1,0:T(8,128)(2,1)S(1)}, u32[]{:S(2)}, u32[]{:S(2)}) collective-permute-start(bf16[256,512]{1,0:T(8,128)(2,1)S(1)} %get-tuple-element.43.pg_ref), channel_id=1, source_target_pairs={{0,1},{1,0},{2,3},{3,2},{4,5},{5,4},{6,7},{7,6},{8,9},{9,8},{10,11... | collective-permute-start | bytes 786440 | tf_op jit(solution)/shard_map/ppermute | solution.py:251
  79.8 18.0 %collective-permute-start.9 = (bf16[8,256,256]{2,1,0:T(8,128)(2,1)S(1)}, bf16[8,256,256]{2,1,0:T(8,128)(2,1)S(1)}, u32[]{:S(2)}, u32[]{:S(2)}) collective-permute-start(bf16[8,256,256]{2,1,0:T(8,128)(2,1)S(1)} %shard_map.84), channel_id=1, source_target_pairs={{0,2},{1,31},{2,4},{3,1},{4,6},{5,3},{6,8},{7,5},{8,10},{9,7},{10,... | collective-permute-start | bytes 3145736 | tf_op jit(solution)/shard_map/ppermute | solution.py:251
  89.5 1.5 %copy-start = (bf16[80,128,128]{2,1,0:T(8,128)(2,1)}, bf16[80,128,128]{2,1,0:T(8,128)(2,1)S(1)}, u32[]{:S(2)}) copy-start(bf16[80,128,128]{2,1,0:T(8,128)(2,1)S(1)} %shard_map.88) | copy-start | bytes 7864324
  91.1 43.3 %all-to-all-start = ((bf16[80,128,128]{2,1,0:T(8,128)(2,1)}), bf16[80,128,128]{2,1,0:T(8,128)(2,1)}, u32[]{:S(2)}, u32[]{:S(2)}) async-start(bf16[80,128,128]{2,1,0:T(8,128)(2,1)} %copy-done), calls=%async_computation | async-start | bytes 5242880 | tf_op jit(solution)/shard_map/all_to_all | solution.py:325
  97.9 16.2 %collective-permute-start.10 = (bf16[4,256,256]{2,1,0:T(8,128)(2,1)S(1)}, bf16[4,256,256]{2,1,0:T(8,128)(2,1)S(1)}, u32[]{:S(2)}, u32[]{:S(2)}) collective-permute-start(bf16[4,256,256]{2,1,0:T(8,128)(2,1)S(1)} %shard_map.86), channel_id=1, source_target_pairs={{0,4},{1,29},{2,6},{3,31},{4,8},{5,1},{6,10},{7,3},{8,12},{9,5},{1... | collective-permute-start | bytes 1572872 | tf_op jit(solution)/shard_map/ppermute | solution.py:251
  114.3 23.0 %collective-permute-start.11 = (bf16[2,256,256]{2,1,0:T(8,128)(2,1)S(1)}, bf16[2,256,256]{2,1,0:T(8,128)(2,1)S(1)}, u32[]{:S(2)}, u32[]{:S(2)}) collective-permute-start(bf16[2,256,256]{2,1,0:T(8,128)(2,1)S(1)} %get-tuple-element.42), channel_id=1, source_target_pairs={{0,8},{1,23},{2,10},{3,25},{4,12},{5,27},{6,14},{7,29},{8,16},{9,3... | collective-permute-start | bytes 786440 | tf_op jit(solution)/shard_map/ppermute | solution.py:251
  122.9 16.1 %collective-permute-start.12 = (bf16[2,256,256]{2,1,0:T(8,128)(2,1)S(1)}, bf16[2,256,256]{2,1,0:T(8,128)(2,1)S(1)}, u32[]{:S(2)}, u32[]{:S(2)}) collective-permute-start(bf16[2,256,256]{2,1,0:T(8,128)(2,1)S(1)} %get-tuple-element.41.base_ref), channel_id=1, source_target_pairs={{1,31},{3,1},{5,3},{7,5},{9,7},{11,9},{13,11},{15,13},{17,15},{19,... | collective-permute-start | bytes 786440 | tf_op jit(solution)/shard_map/ppermute | solution.py:251
  139.1 3.2 %collective-permute-start.13 = (bf16[256,256]{1,0:T(8,128)(2,1)S(1)}, bf16[256,256]{1,0:T(8,128)(2,1)S(1)}, u32[]{:S(2)}, u32[]{:S(2)}) collective-permute-start(bf16[256,256]{1,0:T(8,128)(2,1)S(1)} %get-tuple-element.47), channel_id=1, source_target_pairs={{0,1},{1,0},{2,3},{3,2},{4,5},{5,4},{6,7},{7,6},{8,9},{9,8},{10,11... | collective-permute-start | bytes 393224 | tf_op jit(solution)/shard_map/ppermute | solution.py:251
